TPU v7x, 32 devices: a whole 2x2x4 slice. The times are simulated.
32 devices in a mesh: groups: 2 (over x), chan: 16 (over z, y, core).
Axes of the slice: x: 2, y: 2, z: 4, core: 2. Of those that a mesh axis runs over, the one named last changes fastest.
Arguments:
- samples: bfloat16 [2048, 2, 143, 256], P(('groups', 'chan')), parts along dimension 0, may hold values from -6 to 6
- flags: int32 [2048], P('groups'), parts along dimension 0, may hold values 0 or 1
- delays: int32 [256, 1024], replicated, may hold values from 0 to 255
- order: int32 [2048], P('groups'), parts along dimension 0, may hold values from 0 to 1023, each once
Outputs:
- visibilities: bfloat16 [512, 36, 2, 128, 128], P(('groups', 'chan')), parts along dimension 0
- beam_voltages: bfloat16 [512, 2, 113, 256], P(('groups', 'chan')), parts along dimension 0
There are 2 independent parts, one for each index of `groups`. A program takes and returns all parts, laid end to end along the dimension named above; an argument that names none is the same for every part. Nothing has to cross between parts.
Inputs may be any that keep to these rules, and one draw needn't show every extreme that they name: `order`: each antenna appears once.
All inputs are finite; a program needn't handle non-finite values.
Results may differ from a plain program's by a relative error of at most 0.008.
Values may be sent and summed in bfloat16 or wider, within the bound.
No kernel may reach another device: no remote copies, remote signals or barrier semaphores. Data moves between devices by JAX's collectives and lax.ppermute only.
A program may use at most 128 MiB of HBM per device.

v0:
```python
import math

import jax
import jax.numpy as jnp
import numpy as np
from jax import lax
from jax.sharding import PartitionSpec as P

ANTENNA_INPUTS = 1024
CHANNEL_COUNT = 256
VOLTAGE_BEAMS = 256
TAPS = 16
TILE_ANTENNAS = 128
WINDOW_SPECTRA = 128
OUTFRAMES = 113


def prototype(tap_count, chan_count):
    length = tap_count * chan_count
    counter = jnp.arange(length, dtype=jnp.float32)
    shifted = (counter - (length - 1) / 2.0) / chan_count
    window = 0.5 - 0.5 * jnp.cos(2.0 * math.pi * (counter + 0.5) / length)
    return (jnp.sinc(shifted) * window).reshape(tap_count, chan_count)


def dft_table(chan_count, direction):
    counter = jnp.arange(chan_count, dtype=jnp.int32)
    phase = counter[:, None] * counter[None, :] % chan_count
    angle = phase.astype(jnp.float32) * (2.0 * math.pi / chan_count)
    cosine = jnp.cos(angle)
    sine = jnp.sin(angle)
    top_rows = jnp.stack([cosine, -direction * sine], axis=1)
    bottom_rows = jnp.stack([direction * sine, cosine], axis=1)
    return jnp.stack([top_rows, bottom_rows], axis=0).astype(jnp.bfloat16)


def tile_pairs(tile_count):
    first_tiles = []
    second_tiles = []
    for row_tile in range(tile_count):
        for col_tile in range(row_tile, tile_count):
            first_tiles.append(row_tile)
            second_tiles.append(col_tile)
    return (np.array(first_tiles, np.int32), np.array(second_tiles, np.int32))


def per_device(samples, flags, delays, order):
    device_list = lax.axis_size("chan")
    local_channels = CHANNEL_COUNT // device_list
    local_antennas = samples.shape[0]
    filt = prototype(TAPS, CHANNEL_COUNT)
    filtered_frames = jnp.zeros((local_antennas, 2, WINDOW_SPECTRA, CHANNEL_COUNT), jnp.float32)
    for tap_step in range(TAPS):
        filtered_frames = (
            filtered_frames
            + filt[tap_step] * samples[:, :, tap_step : tap_step + WINDOW_SPECTRA, :]
        )
    filtered_frames = filtered_frames.astype(jnp.bfloat16)
    forward = dft_table(CHANNEL_COUNT, 1.0)
    channel_spectra = jnp.einsum(
        "arsj,rjuk->kaus", filtered_frames, forward, preferred_element_type=jnp.float32
    )
    channel_spectra = (channel_spectra * (1.0 / math.sqrt(CHANNEL_COUNT))).astype(jnp.bfloat16)
    channel_spectra = channel_spectra.reshape(
        device_list, local_channels, local_antennas, 2 * WINDOW_SPECTRA
    )
    flag_values = flags.astype(jnp.bfloat16)
    permuted_flags = jnp.take(flag_values, order, axis=0)
    tile_count = ANTENNA_INPUTS // TILE_ANTENNAS
    first_tiles, second_tiles = tile_pairs(tile_count)

    def correlate_channel(channel_rows):
        other = jnp.concatenate(
            [channel_rows[:, WINDOW_SPECTRA:], -channel_rows[:, :WINDOW_SPECTRA]], axis=1
        )
        stacked = jnp.stack([channel_rows, other], axis=0).reshape(
            2, tile_count, TILE_ANTENNAS, 2 * WINDOW_SPECTRA
        )
        picked = stacked[:, first_tiles]
        columns = channel_rows.reshape(tile_count, TILE_ANTENNAS, 2 * WINDOW_SPECTRA)[second_tiles]
        product = jnp.einsum("upis,pjs->puij", picked, columns, preferred_element_type=jnp.float32)
        return (product * (1.0 / WINDOW_SPECTRA)).astype(jnp.bfloat16)

    received = lax.all_to_all(channel_spectra, "chan", split_axis=0, concat_axis=2, tiled=True)
    turned_rows = received[0]
    permuted = jnp.take(turned_rows, order, axis=1) * permuted_flags[None, :, None]
    visibilities = lax.map(correlate_channel, permuted)
    masked = turned_rows * flag_values[None, :, None]
    other = jnp.concatenate([masked[:, :, WINDOW_SPECTRA:], -masked[:, :, :WINDOW_SPECTRA]], axis=2)
    stacked = jnp.concatenate([masked, other], axis=1)
    channel_ids = lax.axis_index("chan") * local_channels + jnp.arange(
        local_channels, dtype=jnp.int32
    )
    phase = delays[None, :, :] * channel_ids[:, None, None] % CHANNEL_COUNT
    angle = phase.astype(jnp.float32) * (2.0 * math.pi / CHANNEL_COUNT)
    weights = jnp.concatenate([jnp.cos(angle), jnp.sin(angle)], axis=2).astype(jnp.bfloat16)
    formed_beams = jnp.einsum("cba,cas->cbs", weights, stacked, preferred_element_type=jnp.float32)
    beams = (
        (formed_beams * (1.0 / math.sqrt(ANTENNA_INPUTS)))
        .astype(jnp.bfloat16)
        .reshape(local_channels, VOLTAGE_BEAMS, 2, WINDOW_SPECTRA)
    )
    inverse = dft_table(CHANNEL_COUNT, -1.0)
    arranged = lax.all_to_all(beams, "chan", split_axis=1, concat_axis=0, tiled=True)
    result = jnp.einsum("kbrs,rkuj->busj", arranged, inverse, preferred_element_type=jnp.float32)
    zeta = (result * (1.0 / math.sqrt(CHANNEL_COUNT))).astype(jnp.bfloat16)
    beam_local = zeta.shape[0]
    output = jnp.zeros((beam_local, 2, OUTFRAMES, CHANNEL_COUNT), jnp.float32)
    for tap_step in range(TAPS):
        output = output + filt[TAPS - 1 - tap_step] * zeta[:, :, tap_step : tap_step + OUTFRAMES, :]
    return (visibilities, output.astype(jnp.bfloat16))


def solution(mesh):
    in_specs = (P(("groups", "chan"), None, None, None), P("groups"), P(), P("groups"))
    out_specs = (
        P(("groups", "chan"), None, None, None, None),
        P(("groups", "chan"), None, None, None),
    )
    return jax.shard_map(
        per_device, mesh=mesh, in_specs=in_specs, out_specs=out_specs, check_vma=False
    )
```

profile of v0, /device:TPU:15, one launch (start us, length us, event | category | flops | bytes accessed | tf_op | source)
XLA Modules:
  0.0 671.2 jit_solution(12600181944661369911)
XLA Ops:
  3.7 115.9 %add_convert_fusion = bf16[64,2,128,256]{3,1,2,0:T(2,128)(2,1)S(1)} fusion(bf16[64,2,143,256]{3,1,2,0:T(2,128)(2,1)} %param.10, f32[256]{0:T(256)S(1)} %get-tuple-element.109, f32[256]{0:T(256)S(1)} %get-tuple-element.110, f32[256]{0:T(256)S(1)} %get-tuple-element.111, f32[256]{0:T(256)S(1)} %get-tuple-element.112, f32[256]{0:T(256)S(1)} %get-tuple-element.113, ...), kind=kLoop, calls=%fused_computation.37 | loop fusion | flops 201326592 | bytes 142622720 | tf_op jit(solution)/shard_map/convert_element_type | solution.py:58
  119.6 5.3 fusion.22
  124.9 20.5 %copy.30 = bf16[256,64,2,128]{3,2,1,0:T(2,128)(2,1)} copy(bf16[256,64,2,128]{3,0,1,2:T(8,128)(2,1)S(1)} %fusion.22) | data formatting | bytes 16777216 | tf_op jit(solution)/shard_map/convert_element_type | solution.py:63
  145.4 14.1 %reshape.195 = bf16[16,16,64,256]{3,2,1,0:T(8,128)(2,1)} reshape(bf16[256,64,2,128]{3,2,1,0:T(2,128)(2,1)} %copy.30) | data formatting | bytes 16777216 | tf_op jit(solution)/shard_map/reshape | solution.py:64
  159.6 6.7 all-to-all-start
  166.3 6.8 %gather_fusion.3 = bf16[1024]{0:T(1024)(128)(2,1)S(1)} fusion(bf16[1024]{0:T(1024)(128)(2,1)S(1)} %convert_element_type.187, s32[1024]{0:T(1024)S(1)} %fusion.81), kind=kCustom, calls=%fused_computation.3 | custom fusion | bytes 8192 | tf_op jit(solution)/shard_map/jit(_take)/gather | solution.py:68
  173.1 69.0 %cosine_convert_fusion = (bf16[16,256,1024]{2,1,0:T(8,128)(2,1)}, bf16[16,256,1024]{2,1,0:T(8,128)(2,1)}) fusion(s32[16]{0:T(128)S(1)} %iota_add_fusion.2, s32[256,1024]{1,0:T(8,128)S(1)} %copy-done), kind=kLoop, calls=%fused_computation.36 | loop fusion | flops 67108864 | bytes 17825856 | tf_op jit(solution)/shard_map/convert
  242.1 106.5 %all-to-all-done = bf16[16,16,64,256]{3,2,1,0:T(8,128)(2,1)} async-done(((bf16[16,16,64,256]{3,2,1,0:T(8,128)(2,1)}), bf16[16,16,64,256]{3,2,1,0:T(8,128)(2,1)}, u32[]{:S(2)}, u32[]{:S(2)}) %all-to-all-start) | async-done | bytes 8388640 | tf_op jit(solution)/shard_map/all_to_all | solution.py:84
  348.6 8.3 %copy.31 = bf16[1,16,16,64,256]{4,3,2,1,0:T(8,128)(2,1)} copy(bf16[1,16,16,64,256]{4,3,1,2,0:T(8,128)(2,1)} %bitcast.10) | data formatting | bytes 16777216 | tf_op jit(solution)/shard_map/all_to_all | solution.py:84
  356.9 12.3 %copy.34 = bf16[16,1024,256]{1,2,0:T(8,128)(2,1)} copy(bf16[16,1024,256]{2,1,0:T(8,128)(2,1)} %bitcast.95) | data formatting | bytes 16777216 | tf_op jit(solution)/shard_map/squeeze | solution.py:85
  369.1 11.4 %copy.32 = bf16[16,1024,256]{2,0,1:T(8,128)(2,1)} copy(bf16[16,1024,256]{2,1,0:T(8,128)(2,1)} %bitcast.96) | data formatting | bytes 16777216 | tf_op jit(solution)/shard_map/squeeze | solution.py:85
  380.5 7.1 %broadcast_multiply_fusion = bf16[16,1024,256]{1,2,0:T(8,128)(2,1)} fusion(bf16[16,1024,256]{1,2,0:T(8,128)(2,1)} %copy.34, bf16[1024]{0:T(1024)(128)(2,1)S(1)} %convert_element_type.187), kind=kLoop, calls=%fused_computation.47 | loop fusion | flops 4194304 | bytes 16779264 | tf_op jit(solution)/shard_map/mul | solution.py:88
  387.7 5.1 fusion.85
  392.7 11.3 %multiply_convert_fusion.1 = bf16[16,256,256]{1,2,0:T(8,128)(2,1)S(1)} fusion(bf16[16,1024,128]{1,2,0:T(8,128)(2,1)} %get-tuple-element.99, bf16[16,1024,128]{1,2,0:T(8,128)(2,1)S(1)} %get-tuple-element.98, bf16[16,1024,256]{1,2,0:T(8,128)(2,1)} %broadcast_multiply_fusion, bf16[16,256,1024]{2,1,0:T(8,128)(2,1)} %get-tuple-element.101, ...), kind=kOutput, calls=%fused_computation.46 | convolution fusion | flops 4380950528 | bytes 35651584 | tf_op jit(solution)/shard_map/cba,cas->cbs/dot_general | solution.py:97
  408.2 4.8 all-to-all-start.1
  413.0 13.1 %gather_fusion.2 = bf16[1024,16,256]{2,1,0:T(8,128)(2,1)} fusion(bf16[16,1024,256]{2,0,1:T(8,128)(2,1)} %copy.32, s32[1024]{0:T(1024)S(1)} %fusion.81), kind=kCustom, calls=%fused_computation.2 | custom fusion | bytes 16781312 | tf_op jit(solution)/shard_map/jit(_take)/gather | solution.py:86
  426.0 10.1 %multiply_bitcast_fusion = bf16[16,1024,256]{2,0,1:T(8,128)(2,1)} fusion(bf16[1024,16,256]{2,1,0:T(8,128)(2,1)} %gather_fusion.2, pred[1024]{0:T(1024)(128)(4,1)S(1)} %get-tuple-element.95, bf16[1024]{0:T(1024)(128)(2,1)S(1)} %get-tuple-element.94), kind=kLoop, calls=%fused_computation.42 | loop fusion | flops 8388608 | bytes 16780288 | tf_op jit(solution)/shard_map/mul | solution.py:86
  436.2 9.7 %copy.33 = bf16[16,1024,256]{2,1,0:T(8,128)(2,1)} copy(bf16[16,1024,256]{2,0,1:T(8,128)(2,1)} %multiply_bitcast_fusion) | data formatting | bytes 16777216
  445.8 205.1 %while.12 = (s32[]{:T(128)}, bf16[16,36,2,128,128]{4,3,2,1,0:T(8,128)(2,1)}, bf16[16,1024,256]{2,1,0:T(8,128)(2,1)}, s32[]{:T(128)}, s32[36]{0:T(128)S(1)}, /*index=5*/s32[36]{0:T(128)S(1)}) while((s32[]{:T(128)}, bf16[16,36,2,128,128]{4,3,2,1,0:T(8,128)(2,1)}, bf16[16,1024,256]{2,1,0:T(8,128)(2,1)}, s32[]{:T(128)}, ...), condition=%wide.region_1.2_spmd.clone.clone, body=%wide.region_0.1_spmd.sunk.clone.clone.sunk | while | flops 608045056 | bytes 29893772 | solution.py:87
  448.3 4.5 gather_fusion.1
  453.5 5.1 fusion.97
  461.1 4.5 gather_fusion.1
  466.3 5.1 fusion.97
  473.9 4.5 gather_fusion.1
  479.1 5.1 fusion.97
  486.7 4.5 gather_fusion.1
  491.9 5.1 fusion.97
  499.5 4.5 gather_fusion.1
  504.8 5.1 fusion.97
  512.3 4.5 gather_fusion.1
  517.6 5.1 fusion.97
  525.2 4.5 gather_fusion.1
  530.4 5.1 fusion.97
  538.0 4.5 gather_fusion.1
  543.2 5.1 fusion.97
  550.8 4.5 gather_fusion.1
  556.0 5.1 fusion.97
  563.6 4.5 gather_fusion.1
  568.8 5.1 fusion.97
  581.7 5.1 fusion.97
  594.5 5.1 fusion.97
  607.3 5.1 fusion.97
  620.1 5.1 fusion.97
  627.7 4.5 gather_fusion.1
  632.9 5.1 fusion.97
  640.5 4.5 gather_fusion.1
  645.8 5.1 fusion.97
  659.6 8.5 %add_convert_fusion.1 = bf16[16,2,113,256]{3,2,0,1:T(8,128)(2,1)S(1)} fusion(bf16[16,2,128,256]{3,2,0,1:T(8,128)(2,1)S(1)} %fusion.34, f32[256]{0:T(256)S(1)} %get-tuple-element.108, f32[256]{0:T(256)S(1)} %get-tuple-element.123, f32[256]{0:T(256)S(1)} %get-tuple-element.122, f32[256]{0:T(256)S(1)} %get-tuple-element.121, f32[256]{0:T(256)S(1)} %get-tuple-element.120, ...), kind=kLoop, calls=%fused_computation.48 | loop fusion | flops 44433408 | bytes 31490048 | tf_op jit(solution)/shard_map/convert_element_type | solution.py:111
  (163 shorter events, 86.7 us)
Async XLA Ops:
  159.6 6.7 copy-start.6
  159.6 6.7 copy-start.3
  159.6 13.6 %copy-start = (s32[256,1024]{1,0:T(8,128)S(1)}, s32[256,1024]{1,0:T(8,128)}, u32[]{:S(2)}) copy-start(s32[256,1024]{1,0:T(8,128)} %param.12) | copy-start | bytes 3145732
  159.6 189.0 %all-to-all-start = ((bf16[16,16,64,256]{3,2,1,0:T(8,128)(2,1)}), bf16[16,16,64,256]{3,2,1,0:T(8,128)(2,1)}, u32[]{:S(2)}, u32[]{:S(2)}) async-start(bf16[16,16,64,256]{3,2,1,0:T(8,128)(2,1)} %reshape.195), calls=%async_computation | async-start | bytes 16777216 | tf_op jit(solution)/shard_map/all_to_all | solution.py:84
  408.2 242.7 %all-to-all-start.1 = ((bf16[16,256,2,128]{3,2,0,1:T(2,128)(2,1)}), bf16[16,256,2,128]{3,2,0,1:T(2,128)(2,1)}, u32[]{:S(2)}, u32[]{:S(2)}) async-start(bf16[16,256,2,128]{3,2,0,1:T(2,128)(2,1)} %copy.35), calls=%async_computation.1 | async-start | bytes 4194304 | tf_op jit(solution)/shard_map/all_to_all | solution.py:104
  436.2 9.7 %copy-start.4 = (s32[36]{0:T(128)S(1)}, s32[36]{0:T(128)}, u32[]{:S(2)}) copy-start(s32[36]{0:T(128)} %constant.301) | copy-start | bytes 436
  436.2 9.7 %copy-start.5 = (s32[36]{0:T(128)S(1)}, s32[36]{0:T(128)}, u32[]{:S(2)}) copy-start(s32[36]{0:T(128)} %constant.302) | copy-start | bytes 436
  650.9 5.8 copy-start.1
  650.9 5.8 copy-start.2
where the time goes:
time: 675 us; the launch traced here: 671 us
  local copies, waits for them, and re-layouts  227 us (34%)
  other arithmetic  223 us (33%)
  waiting for transfers between devices  106 us (16%)
  matrix products  102 us (15%)
  starting transfers between devices  11.4 us (2%)
    convert_element_type x1, other arithmetic, per_device(): filtered_frames = filtered_frames.astype(jnp.bfloat16)  116 us
    all_to_all x1, waiting for transfers between devices, per_device(): lax.all_to_all(channel_spectra, 'chan', split_axis=0, concat_axis=2, tile...  106 us
    dot_general x16, matrix products, correlate_channel(): jnp.einsum('upis,pjs->puij', picked, columns, preferred_element_type=jnp....  82.2 us
    gather x16, local copies, waits for them, and re-layouts, correlate_channel(): picked = stacked[:, first_tiles]  72.6 us
    another operation x3, other arithmetic  71.1 us
    squeeze x2, local copies, waits for them, and re-layouts, per_device(): turned_rows = received[0]  23.7 us
    convert_element_type x1, local copies, waits for them, and re-layouts, per_device(): (channel_spectra * (1.0 / math.sqrt(CHANNEL_COUNT))).astype(jnp.bfloat16)  20.5 us
    dynamic_slice x16, local copies, waits for them, and re-layouts, per_device(): visibilities = lax.map(correlate_channel, permuted)  17.3 us
  transfers between devices with their start and end apart: 2, of which 1 were waited for; matrix products, arithmetic and copies ran while one was open for 47% of the time, Pallas kernels for 0%

commit v1 on v0

v1 whole, which is shorter than its diff:
```python
import functools
import math

import jax
import jax.numpy as jnp
import ml_dtypes
import numpy as np
from jax import lax
from jax.experimental import pallas as pl
from jax.experimental.pallas import tpu as pltpu
from jax.sharding import PartitionSpec as P

TAPS = 16
TILE_ANTENNAS = 128
BLOCK_ANTENNAS = 16
LANES = 128
VMEM_BYTES = 60 * 1024 * 1024


def prototype(tap_count, chan_count):
    length = tap_count * chan_count
    counter = np.arange(length, dtype=np.float32)
    shifted = (counter - np.float32((length - 1) / 2.0)) / np.float32(chan_count)
    window = 0.5 - 0.5 * np.cos(2.0 * math.pi * (counter + 0.5) / length)
    return (np.sinc(shifted) * window).astype(np.float32).reshape(tap_count, chan_count)


def dft_parts(chan_count):
    counter = np.arange(chan_count)
    angle = (counter[:, None] * counter[None, :] % chan_count) * (2.0 * math.pi / chan_count)
    return np.cos(angle), np.sin(angle)


def round_bf16(table):
    return table.astype(np.float32).astype(ml_dtypes.bfloat16)


def forward_table(chan_count):
    cosine, sine = dft_parts(chan_count)
    table = np.concatenate(
        [np.concatenate([cosine, sine], axis=1), np.concatenate([-sine, cosine], axis=1)], axis=0
    )
    return (round_bf16(table).astype(np.float32) / math.sqrt(chan_count)).astype(
        ml_dtypes.bfloat16
    )


def inverse_table(chan_count):
    cosine, sine = dft_parts(chan_count)
    table = np.concatenate(
        [np.concatenate([cosine, sine], axis=1), np.concatenate([-sine, cosine], axis=1)], axis=0
    )
    return (round_bf16(table).astype(np.float32) / math.sqrt(chan_count)).astype(
        ml_dtypes.bfloat16
    )


def channelize_kernel(samples_ref, proto_ref, table_ref, out_ref, frames, filtered, turned):
    block, _, in_frames, chans = samples_ref.shape
    spectra = turned.shape[2]

    def pair(step, carry):
        for half in range(2):
            ant = 2 * step + half
            for part in range(2):
                for lane in range(0, chans, LANES):
                    cols = slice(lane, lane + LANES)
                    frames[0:in_frames, :] = samples_ref[ant, part, :, cols].astype(jnp.float32)
                    total = proto_ref[0:1, cols] * frames[pl.ds(0, spectra), :]
                    for tap in range(1, TAPS):
                        total = total + proto_ref[tap : tap + 1, cols] * frames[pl.ds(tap, spectra), :]
                    filtered[
                        half * spectra : (half + 1) * spectra,
                        part * chans + lane : part * chans + lane + LANES,
                    ] = total.astype(jnp.bfloat16)
        product = lax.dot_general(
            table_ref[...],
            filtered[...],
            (((1,), (1,)), ((), ())),
            preferred_element_type=jnp.float32,
        )
        for half in range(2):
            for part in range(2):
                turned[part, pl.ds(2 * step + half, chans, stride=block), :] = product[
                    part * chans : (part + 1) * chans, half * spectra : (half + 1) * spectra
                ]
        return carry

    lax.fori_loop(0, block // 2, pair, 0)
    for part in range(2):
        out_ref[:, :, part * spectra : (part + 1) * spectra] = (
            turned[part].reshape(chans, block, spectra).astype(jnp.bfloat16)
        )


def channelize(samples, proto, table, first, count, block):
    _, _, in_frames, chans = samples.shape
    spectra = in_frames - TAPS + 1

    return pl.pallas_call(
        channelize_kernel,
        grid=(count // block,),
        in_specs=[
            pl.BlockSpec((block, 2, in_frames, chans), lambda i: (i + first // block, 0, 0, 0)),
            pl.BlockSpec((TAPS, chans), lambda i: (0, 0)),
            pl.BlockSpec((2 * chans, 2 * chans), lambda i: (0, 0)),
        ],
        out_specs=pl.BlockSpec((chans, block, 2 * spectra), lambda i: (0, i, 0)),
        out_shape=jax.ShapeDtypeStruct((chans, count, 2 * spectra), jnp.bfloat16),
        scratch_shapes=[
            pltpu.VMEM((in_frames + 1, LANES), jnp.float32),
            pltpu.VMEM((2 * spectra, 2 * chans), jnp.bfloat16),
            pltpu.VMEM((2, chans * block, spectra), jnp.float32),
        ],
        compiler_params=pltpu.CompilerParams(vmem_limit_bytes=VMEM_BYTES),
        cost_estimate=pl.CostEstimate(
            flops=count * spectra * 4 * chans * 2 * chans * 2,
            bytes_accessed=count * 2 * (in_frames + spectra) * chans * 2,
            transcendentals=0,
        ),
        name="channelize",
    )(samples, proto, table)


def beam_kernel(counts, *refs):
    x_refs = refs[: len(counts)]
    weights_ref, out_ref, turned = refs[len(counts) :]
    channel = pl.program_id(0)
    beams = out_ref.shape[0]
    local = out_ref.shape[1]
    spectra = turned.shape[2]
    product = None
    start = 0
    for x_ref, count in zip(x_refs, counts):
        rows = x_ref[:, 0].reshape(count, 2 * spectra)
        term = jnp.dot(
            weights_ref[0, :, start : start + count], rows, preferred_element_type=jnp.float32
        )
        product = term if product is None else product + term
        start += count
    turned[0, pl.ds(channel, beams, stride=local), :] = (
        product[:beams, :spectra] + product[beams:, spectra:]
    )
    turned[1, pl.ds(channel, beams, stride=local), :] = (
        product[:beams, spectra:] - product[beams:, :spectra]
    )

    @pl.when(channel == pl.num_programs(0) - 1)
    def _():
        for part in range(2):
            out_ref[:, :, part * spectra : (part + 1) * spectra] = (
                turned[part].reshape(beams, local, spectra).astype(jnp.bfloat16)
            )


def form_beams(blocks, weights):
    local, double_beams, antennas = weights.shape
    beams = double_beams // 2
    columns = blocks[0].shape[3]
    counts = tuple(x.shape[0] * x.shape[2] for x in blocks)
    return pl.pallas_call(
        functools.partial(beam_kernel, counts),
        grid=(local,),
        in_specs=[
            pl.BlockSpec((x.shape[0], 1, x.shape[2], columns), lambda c: (0, c, 0, 0))
            for x in blocks
        ]
        + [pl.BlockSpec((1, double_beams, antennas), lambda c: (c, 0, 0))],
        out_specs=pl.BlockSpec((beams, local, columns), lambda c: (0, 0, 0)),
        out_shape=jax.ShapeDtypeStruct((beams, local, columns), jnp.bfloat16),
        scratch_shapes=[pltpu.VMEM((2, beams * local, columns // 2), jnp.float32)],
        compiler_params=pltpu.CompilerParams(vmem_limit_bytes=VMEM_BYTES),
        cost_estimate=pl.CostEstimate(
            flops=2 * local * double_beams * antennas * columns,
            bytes_accessed=2 * local * (double_beams * antennas + antennas * columns + beams * columns),
            transcendentals=0,
        ),
        name="form_beams",
    )(*blocks, weights)


def visibility_kernel(counts, order_ref, ids_ref, flags_ref, *refs):
    x_refs = refs[: len(counts)]
    out_ref, select, permuted, turned = refs[len(counts) :]
    antennas, columns = permuted.shape
    spectra = columns // 2
    tile = TILE_ANTENNAS
    tiles = antennas // tile

    @pl.when(pl.program_id(0) == 0)
    def _():
        for t in range(tiles):
            rows = slice(t * tile, (t + 1) * tile)
            select[rows, :] = jnp.where(
                order_ref[rows, :] == ids_ref[...], flags_ref[...], 0.0
            ).astype(jnp.bfloat16)

    product = None
    start = 0
    for x_ref, count in zip(x_refs, counts):
        term = jnp.dot(
            select[:, start : start + count],
            x_ref[:, 0].reshape(count, columns),
            preferred_element_type=jnp.float32,
        )
        product = term if product is None else product + term
        start += count
    permuted[...] = product.astype(jnp.bfloat16)
    scaled = product * (1.0 / spectra)
    for t in range(tiles):
        block = scaled[t * tile : (t + 1) * tile, :]
        turned[2 * t * tile : (2 * t + 1) * tile, :] = block.astype(jnp.bfloat16)
        turned[(2 * t + 1) * tile : (2 * t + 2) * tile, :spectra] = block[:, spectra:].astype(jnp.bfloat16)
        turned[(2 * t + 1) * tile : (2 * t + 2) * tile, spectra:] = (-block[:, :spectra]).astype(jnp.bfloat16)
    pair = 0
    for p in range(tiles):
        left = turned[2 * p * tile : (2 * p + 2) * tile, :]
        result = lax.dot_general(
            left,
            permuted[p * tile :, :],
            (((1,), (1,)), ((), ())),
            preferred_element_type=jnp.float32,
        ).astype(jnp.bfloat16)
        for q in range(p, tiles):
            cols = slice((q - p) * tile, (q - p + 1) * tile)
            out_ref[0, pair, 0] = result[:tile, cols]
            out_ref[0, pair, 1] = result[tile:, cols]
            pair += 1


def correlate(blocks, order, ids, flags):
    antennas = order.shape[0]
    local, columns = blocks[0].shape[1], blocks[0].shape[3]
    counts = tuple(x.shape[0] * x.shape[2] for x in blocks)
    tiles = antennas // TILE_ANTENNAS
    pairs = tiles * (tiles + 1) // 2
    return pl.pallas_call(
        functools.partial(visibility_kernel, counts),
        grid=(local,),
        in_specs=[
            pl.BlockSpec((antennas, 1), lambda c: (0, 0)),
            pl.BlockSpec((1, antennas), lambda c: (0, 0)),
            pl.BlockSpec((1, antennas), lambda c: (0, 0)),
        ]
        + [
            pl.BlockSpec((x.shape[0], 1, x.shape[2], columns), lambda c: (0, c, 0, 0))
            for x in blocks
        ],
        out_specs=pl.BlockSpec(
            (1, pairs, 2, TILE_ANTENNAS, TILE_ANTENNAS), lambda c: (c, 0, 0, 0, 0)
        ),
        out_shape=jax.ShapeDtypeStruct(
            (local, pairs, 2, TILE_ANTENNAS, TILE_ANTENNAS), jnp.bfloat16
        ),
        scratch_shapes=[
            pltpu.VMEM((antennas, antennas), jnp.bfloat16),
            pltpu.VMEM((antennas, columns), jnp.bfloat16),
            pltpu.VMEM((2 * antennas, columns), jnp.bfloat16),
        ],
        compiler_params=pltpu.CompilerParams(vmem_limit_bytes=VMEM_BYTES),
        cost_estimate=pl.CostEstimate(
            flops=2 * local * columns * (antennas * antennas + pairs * 2 * TILE_ANTENNAS**2),
            bytes_accessed=2 * local * (antennas * columns + pairs * 2 * TILE_ANTENNAS**2),
            transcendentals=0,
        ),
        name="correlate",
    )(order[:, None], ids[None, :], flags[None, :], *blocks)


def synthesize_kernel(beams_ref, proto_ref, table_ref, out_ref, zeta):
    sources, _, local, columns = beams_ref.shape
    chans = sources * local
    spectra = columns // 2
    out_frames = out_ref.shape[2]
    rows = beams_ref[:, 0].reshape(chans, columns)
    for part in range(2):
        cols = slice(part * chans, (part + 1) * chans)
        value = None
        for source in range(2):
            term = lax.dot_general(
                rows[:, source * spectra : (source + 1) * spectra],
                table_ref[source * chans : (source + 1) * chans, cols],
                (((0,), (0,)), ((), ())),
                preferred_element_type=jnp.float32,
            )
            value = term if value is None else value + term
        value = value.astype(jnp.bfloat16).astype(jnp.float32)
        for lane in range(0, chans, LANES):
            zeta[...] = value[:, lane : lane + LANES]
            total = proto_ref[TAPS - 1 : TAPS, lane : lane + LANES] * zeta[pl.ds(0, out_frames), :]
            for tap in range(1, TAPS):
                total = total + (
                    proto_ref[TAPS - 1 - tap : TAPS - tap, lane : lane + LANES]
                    * zeta[pl.ds(tap, out_frames), :]
                )
            out_ref[0, part, :, lane : lane + LANES] = total.astype(jnp.bfloat16)


def synthesize(arranged, proto, table):
    sources, beams, local, columns = arranged.shape
    chans = sources * local
    spectra = columns // 2
    out_frames = spectra - TAPS + 1
    return pl.pallas_call(
        synthesize_kernel,
        grid=(beams,),
        in_specs=[
            pl.BlockSpec((sources, 1, local, columns), lambda b: (0, b, 0, 0)),
            pl.BlockSpec((TAPS, chans), lambda b: (0, 0)),
            pl.BlockSpec((2 * chans, 2 * chans), lambda b: (0, 0)),
        ],
        out_specs=pl.BlockSpec((1, 2, out_frames, chans), lambda b: (b, 0, 0, 0)),
        out_shape=jax.ShapeDtypeStruct((beams, 2, out_frames, chans), jnp.bfloat16),
        scratch_shapes=[pltpu.VMEM((spectra, LANES), jnp.float32)],
        compiler_params=pltpu.CompilerParams(vmem_limit_bytes=VMEM_BYTES),
        cost_estimate=pl.CostEstimate(
            flops=2 * beams * spectra * 4 * chans * chans,
            bytes_accessed=2 * beams * (columns + 2 * out_frames) * chans,
            transcendentals=0,
        ),
        name="synthesize",
    )(arranged, proto, table)


def per_device(samples, flags, delays, order):
    devices = lax.axis_size("chan")
    antennas_here, _, in_frames, chans = samples.shape
    local_channels = chans // devices
    spectra = in_frames - TAPS + 1
    antennas = antennas_here * devices
    beam_count = delays.shape[0]
    block = BLOCK_ANTENNAS if antennas_here % BLOCK_ANTENNAS == 0 else antennas_here
    sizes = [block, antennas_here - block] if antennas_here > block else [block]

    proto = jnp.asarray(prototype(TAPS, chans))
    forward = jnp.asarray(forward_table(chans))
    inverse = jnp.asarray(inverse_table(chans))

    blocks = []
    columns_of = []
    start = 0
    for size in sizes:
        part = channelize(samples, proto, forward, start, size, block)
        part = lax.all_to_all(part, "chan", split_axis=0, concat_axis=0, tiled=True)
        blocks.append(part.reshape(devices, local_channels, size, 2 * spectra))
        ids = np.arange(antennas, dtype=np.int32).reshape(devices, antennas_here)
        columns_of.append(ids[:, start : start + size].reshape(-1))
        start += size
    ids = np.concatenate(columns_of)

    def arrange(x):
        x = x.reshape(x.shape[:-1] + (devices, antennas_here))
        pieces = []
        at = 0
        for size in sizes:
            pieces.append(x[..., at : at + size].reshape(x.shape[:-2] + (devices * size,)))
            at += size
        return jnp.concatenate(pieces, axis=-1)

    flag_row = arrange(flags).astype(jnp.float32)
    channel_ids = lax.axis_index("chan") * local_channels + jnp.arange(
        local_channels, dtype=jnp.int32
    )
    phase = arrange(delays)[None, :, :] * channel_ids[:, None, None] % chans
    angle = phase.astype(jnp.float32) * (2.0 * math.pi / chans)
    keep = flag_row[None, None, :] * (1.0 / math.sqrt(antennas))
    weights = jnp.concatenate(
        [
            jnp.cos(angle).astype(jnp.bfloat16) * keep.astype(jnp.bfloat16),
            jnp.sin(angle).astype(jnp.bfloat16) * keep.astype(jnp.bfloat16),
        ],
        axis=1,
    )
    beams = form_beams(blocks, weights)
    arranged = lax.all_to_all(beams, "chan", split_axis=0, concat_axis=0, tiled=True)
    arranged = arranged.reshape(devices, beam_count // devices, local_channels, 2 * spectra)
    visibilities = correlate(blocks, order, jnp.asarray(ids), flag_row)
    voltages = synthesize(arranged, proto, inverse)
    return visibilities, voltages


def solution(mesh):
    in_specs = (P(("groups", "chan"), None, None, None), P("groups"), P(), P("groups"))
    out_specs = (
        P(("groups", "chan"), None, None, None, None),
        P(("groups", "chan"), None, None, None),
    )
    return jax.shard_map(
        per_device, mesh=mesh, in_specs=in_specs, out_specs=out_specs, check_vma=False
    )
```

time: 675 us -> 310 us (0.46)
  local copies, waits for them, and re-layouts: 227 us -> 20.4 us
  other arithmetic: 223 us -> 77.3 us
  Pallas kernels: 0 us -> 118 us
  matrix products: 102 us -> 0 us
  waiting for transfers between devices: 106 us -> 76 us
    convert_element_type x3 -> x2, other arithmetic: 124 us -> 0.61 us  [the longest x1 0.6 us: per_device(): flag_row = arrange(flags).astype(jnp.float32)]
    pallas_call x0 -> x5, Pallas kernels: none -> 118 us  [the longest x2 44.5 us: channelize(): pl.pallas_call(channelize_kernel, grid=(count // block,), in_specs=[pl.Bl...]
    gather x34 -> x0, local copies, waits for them, and re-layouts: 104 us -> none  [the longest x16 72.6 us: correlate_channel(): picked = stacked[:, first_tiles]]
    dot_general x19 -> x0, matrix products: 102 us -> none  [the longest x16 82.2 us: correlate_channel(): jnp.einsum('upis,pjs->puij', picked, columns, preferred_element_type=jnp....]
    another operation x20 -> x0, other arithmetic: 73.5 us -> none
    mul x3 -> x1, other arithmetic: 17.4 us -> 67.8 us  [per_device(): jnp.cos(angle).astype(jnp.bfloat16) * keep.astype(jnp.bfloat16)]
    squeeze x18 -> x0, local copies, waits for them, and re-layouts: 40.9 us -> none  [the longest x2 23.7 us: per_device(): turned_rows = received[0]]
    all_to_all x2 -> x3, waiting for transfers between devices: 106 us -> 76 us  [the longest x2 71.7 us: per_device(): part = lax.all_to_all(part, 'chan', split_axis=0, concat_axis=0, tiled=True)]
  transfers between devices with their start and end apart: 2 -> 3, of which waited for: 1 -> 3; matrix products, arithmetic and copies ran while one was open for 47% -> 27% of each run, Pallas kernels for 0% -> 24%
where the time goes in v1:
time: 310 us; the launch traced here: 309 us
  Pallas kernels  118 us (38%)
  other arithmetic  77.3 us (25%)
  waiting for transfers between devices  76 us (25%)
  local copies, waits for them, and re-layouts  20.4 us (7%)
  starting transfers between devices  16.1 us (5%)
    all_to_all x2, waiting for transfers between devices, per_device(): part = lax.all_to_all(part, 'chan', split_axis=0, concat_axis=0, tiled=True)  71.7 us
    mul x1, other arithmetic, per_device(): jnp.cos(angle).astype(jnp.bfloat16) * keep.astype(jnp.bfloat16)  67.8 us
    pallas_call x2, Pallas kernels, channelize(): pl.pallas_call(channelize_kernel, grid=(count // block,), in_specs=[pl.Bl...  44.5 us
    pallas_call x1, Pallas kernels, correlate(): pl.pallas_call(functools.partial(visibility_kernel, counts), grid=(local,...  41.4 us
    pallas_call x1, Pallas kernels, form_beams(): pl.pallas_call(functools.partial(beam_kernel, counts), grid=(local,), in_...  18.3 us
    unnamed x11, local copies, waits for them, and re-layouts  16.4 us
    pallas_call x1, Pallas kernels, synthesize(): pl.pallas_call(synthesize_kernel, grid=(beams,), in_specs=[pl.BlockSpec((...  13.9 us
    all_to_all x2, starting transfers between devices, per_device(): part = lax.all_to_all(part, 'chan', split_axis=0, concat_axis=0, tiled=True)  11.3 us
  transfers between devices with their start and end apart: 3, of which 3 were waited for; matrix products, arithmetic and copies ran while one was open for 27% of the time, Pallas kernels for 24%

profile of v1, /device:TPU:15, one launch (start us, length us, event | category | flops | bytes accessed | tf_op | source)
XLA Modules:
  0.0 308.6 jit_solution(7040300551880625406)
XLA Ops:
  0.6 9.3 %copy.13.samples_ref = bf16[64,2,143,256]{3,2,1,0:T(8,128)(2,1)} copy(bf16[64,2,143,256]{3,1,2,0:T(2,128)(2,1)} %param.8) | data formatting | bytes 18743296 | tf_op args[0]
  9.9 12.6 %channelize.2 = bf16[256,16,256]{2,1,0:T(8,128)(2,1)} custom-call(bf16[64,2,143,256]{3,2,1,0:T(8,128)(2,1)} %copy.13.samples_ref, f32[16,256]{1,0:T(8,128)} %constant.31.clone.proto_ref, bf16[512,512]{1,0:T(8,128)(2,1)} %constant.32.clone.table_ref), custom_call_target="tpu_custom_call" | custom-call | flops 2147483648 | bytes 4440064 | tf_op jit(solution)/shard_map/channelize/pallas_call | solution.py:100
  22.5 6.5 %all-to-all-start = ((bf16[256,16,256]{2,1,0:T(8,128)(2,1)}), bf16[256,16,256]{2,1,0:T(8,128)(2,1)S(1)}, u32[]{:S(2)}, u32[]{:S(2)}) async-start(bf16[256,16,256]{2,1,0:T(8,128)(2,1)} %channelize.2), calls=%async_computation | async-start | bytes 4194304 | tf_op jit(solution)/shard_map/all_to_all | solution.py:344
  29.0 0.0 copy-start.3
  29.0 31.9 %channelize.3 = bf16[256,48,256]{2,1,0:T(8,128)(2,1)} custom-call(bf16[64,2,143,256]{3,2,1,0:T(8,128)(2,1)} %copy.13.samples_ref, f32[16,256]{1,0:T(8,128)} %constant.31.clone.proto_ref, bf16[512,512]{1,0:T(8,128)(2,1)} %constant.32.clone.table_ref), custom_call_target="tpu_custom_call" | custom-call | flops 6442450944 | bytes 13320192 | tf_op jit(solution)/shard_map/channelize/pallas_call | solution.py:100
  61.0 15.5 %all-to-all-done = bf16[256,16,256]{2,1,0:T(8,128)(2,1)S(1)} async-done(((bf16[256,16,256]{2,1,0:T(8,128)(2,1)}), bf16[256,16,256]{2,1,0:T(8,128)(2,1)S(1)}, u32[]{:S(2)}, u32[]{:S(2)}) %all-to-all-start) | async-done | bytes 2097184 | tf_op jit(solution)/shard_map/all_to_all | solution.py:344
  76.4 0.0 copy-start.1
  76.4 4.8 %all-to-all-start.1 = ((bf16[256,48,256]{2,1,0:T(8,128)(2,1)}), bf16[256,48,256]{2,1,0:T(8,128)(2,1)}, u32[]{:S(2)}, u32[]{:S(2)}) async-start(bf16[256,48,256]{2,1,0:T(8,128)(2,1)} %channelize.3), calls=%async_computation.1 | async-start | bytes 12582912 | tf_op jit(solution)/shard_map/all_to_all | solution.py:344
  81.2 1.6 copy.16
  82.8 1.0 slice.19
  83.8 0.0 copy-done.3
  83.8 0.1 reshape.84
  83.8 0.1 slice.17
  83.9 0.1 concatenate.34
  84.0 0.1 concatenate.35
  84.1 2.2 pad_add_fusion
  86.2 1.6 copy.17
  87.8 67.8 %fusion.3 = (bf16[16,256,1024]{2,1,0:T(8,128)(2,1)S(1)}, bf16[16,256,1024]{2,1,0:T(8,128)(2,1)S(1)}) fusion(s32[16]{0:T(128)S(1)} %iota_add_fusion, s32[256,1024]{1,0:T(8,128)S(1)} %copy.17, bf16[1024]{0:T(1024)(128)(2,1)S(1)} %fusion.6), kind=kLoop, calls=%fused_computation.11 | loop fusion | flops 96468992 | bytes 17827904 | tf_op jit(solution)/shard_map/mul | solution.py:369
  155.7 0.0 copy-done.1
  155.7 6.7 %pad_maximum_fusion.refs_2_ = bf16[16,512,1024]{2,1,0:T(8,128)(2,1)} fusion(bf16[16,256,1024]{2,1,0:T(8,128)(2,1)S(1)} %get-tuple-element.7, bf16[16,256,1024]{2,1,0:T(8,128)(2,1)S(1)} %get-tuple-element.6), kind=kLoop, calls=%fused_computation.8 | loop fusion | flops 33554432 | bytes 33554432 | tf_op jit(solution)/shard_map/concatenate | solution.py:367
  162.4 0.0 copy-start.2
  162.4 56.3 %all-to-all-done.1 = bf16[256,48,256]{2,1,0:T(8,128)(2,1)} async-done(((bf16[256,48,256]{2,1,0:T(8,128)(2,1)}), bf16[256,48,256]{2,1,0:T(8,128)(2,1)}, u32[]{:S(2)}, u32[]{:S(2)}) %all-to-all-start.1) | async-done | bytes 6291488 | tf_op jit(solution)/shard_map/all_to_all | solution.py:344
  218.6 18.3 %form_beams.1 = bf16[256,16,256]{2,1,0:T(8,128)(2,1)} custom-call(bf16[16,16,16,256]{3,2,1,0:T(8,128)(2,1)} %bitcast.9, bf16[16,16,48,256]{3,2,1,0:T(8,128)(2,1)} %bitcast.2.refs_1_, bf16[16,512,1024]{2,1,0:T(8,128)(2,1)} %pad_maximum_fusion.refs_2_), custom_call_target="tpu_custom_call" | custom-call | flops 4294967296 | bytes 27262976 | tf_op jit(solution)/shard_map/form_beams/pallas_call | solution.py:161
  236.9 4.8 %all-to-all-start.2 = ((bf16[256,16,256]{2,1,0:T(8,128)(2,1)}), bf16[256,16,256]{2,1,0:T(8,128)(2,1)S(1)}, u32[]{:S(2)}, u32[]{:S(2)}) async-start(bf16[256,16,256]{2,1,0:T(8,128)(2,1)} %form_beams.1), calls=%async_computation.2 | async-start | bytes 4194304 | tf_op jit(solution)/shard_map/all_to_all | solution.py:375
  241.7 0.1 concatenate.30
  241.8 0.1 concatenate.31
  241.9 0.0 copy-done.2
  241.9 1.0 copy.15.order_ref
  242.9 0.6 add_convert_fusion.flags_ref
  243.5 41.4 %correlate.1 = bf16[16,36,2,128,128]{4,3,2,1,0:T(8,128)(2,1)} custom-call(s32[1024,1]{1,0:T(8,128)} %copy.15.order_ref, s32[1,1024]{1,0:T(1,128)} %constant.34.ids_ref, f32[1,1024]{1,0:T(1,128)} %add_convert_fusion.flags_ref, bf16[16,16,16,256]{3,2,1,0:T(8,128)(2,1)} %bitcast.10, bf16[16,16,48,256]{3,2,1,0:T(8,128)(2,1)} %bitcast.2.refs_1_), custom_call_target="tpu_custom_call" | custom-call | flops 18253611008 | bytes 46137344 | tf_op jit(solution)/shard_map/correlate/pallas_call | solution.py:237
  284.9 4.3 %all-to-all-done.2 = bf16[256,16,256]{2,1,0:T(8,128)(2,1)S(1)} async-done(((bf16[256,16,256]{2,1,0:T(8,128)(2,1)}), bf16[256,16,256]{2,1,0:T(8,128)(2,1)S(1)}, u32[]{:S(2)}, u32[]{:S(2)}) %all-to-all-start.2) | async-done | bytes 2097184 | tf_op jit(solution)/shard_map/all_to_all | solution.py:375
  289.1 0.0 copy-start
  289.1 1.3 copy-done
  290.5 13.9 %synthesize.1 = bf16[16,2,113,256]{3,2,1,0:T(8,128)(2,1)} custom-call(bf16[16,16,16,256]{3,2,1,0:T(8,128)(2,1)} %bitcast.8, f32[16,256]{1,0:T(8,128)} %constant.31.clone.proto_ref, bf16[512,512]{1,0:T(8,128)(2,1)} %constant.32.clone.table_ref), custom_call_target="tpu_custom_call" | custom-call | flops 1073741824 | bytes 3948544 | tf_op jit(solution)/shard_map/synthesize/pallas_call | solution.py:304
  304.4 4.2 %copy.18 = bf16[16,2,113,256]{3,1,2,0:T(2,128)(2,1)} copy(bf16[16,2,113,256]{3,2,1,0:T(8,128)(2,1)} %synthesize.1) | data formatting | bytes 3702784
  (3 shorter events, 0.0 us)
Async XLA Ops:
  22.5 53.9 %all-to-all-start = ((bf16[256,16,256]{2,1,0:T(8,128)(2,1)}), bf16[256,16,256]{2,1,0:T(8,128)(2,1)S(1)}, u32[]{:S(2)}, u32[]{:S(2)}) async-start(bf16[256,16,256]{2,1,0:T(8,128)(2,1)} %channelize.2), calls=%async_computation | async-start | bytes 4194304 | tf_op jit(solution)/shard_map/all_to_all | solution.py:344
  29.0 54.7 %copy-start.3 = (s32[1024]{0:T(1024)S(1)}, s32[1024]{0:T(1024)}, u32[]{:S(2)}) copy-start(s32[1024]{0:T(1024)} %param.9) | copy-start | bytes 12292
  76.4 79.2 %copy-start.1 = (bf16[256,16,256]{2,1,0:T(8,128)(2,1)}, bf16[256,16,256]{2,1,0:T(8,128)(2,1)S(1)}, u32[]{:S(2)}) copy-start(bf16[256,16,256]{2,1,0:T(8,128)(2,1)S(1)} %all-to-all-done) | copy-start | bytes 6291460
  76.4 142.2 %all-to-all-start.1 = ((bf16[256,48,256]{2,1,0:T(8,128)(2,1)}), bf16[256,48,256]{2,1,0:T(8,128)(2,1)}, u32[]{:S(2)}, u32[]{:S(2)}) async-start(bf16[256,48,256]{2,1,0:T(8,128)(2,1)} %channelize.3), calls=%async_computation.1 | async-start | bytes 12582912 | tf_op jit(solution)/shard_map/all_to_all | solution.py:344
  162.4 79.5 %copy-start.2 = (s32[1024]{0:T(1024)S(1)}, s32[1024]{0:T(1024)}, u32[]{:S(2)}) copy-start(s32[1024]{0:T(1024)} %param.11) | copy-start | bytes 12292
  236.9 52.2 %all-to-all-start.2 = ((bf16[256,16,256]{2,1,0:T(8,128)(2,1)}), bf16[256,16,256]{2,1,0:T(8,128)(2,1)S(1)}, u32[]{:S(2)}, u32[]{:S(2)}) async-start(bf16[256,16,256]{2,1,0:T(8,128)(2,1)} %form_beams.1), calls=%async_computation.2 | async-start | bytes 4194304 | tf_op jit(solution)/shard_map/all_to_all | solution.py:375
  289.1 1.3 copy-start

commit v2 on v1

--- a/solution.py
+++ b/solution.py
@@ -13,6 +13,8 @@
 TAPS = 16
 TILE_ANTENNAS = 128
 BLOCK_ANTENNAS = 16
+FILTER_ANTENNAS = 8
+BEAM_CHANNELS = 4
 LANES = 128
 VMEM_BYTES = 60 * 1024 * 1024
 
@@ -55,62 +57,89 @@
     )
 
 
-def channelize_kernel(samples_ref, proto_ref, table_ref, out_ref, frames, filtered, turned):
-    block, _, in_frames, chans = samples_ref.shape
-    spectra = turned.shape[2]
-
-    def pair(step, carry):
-        for half in range(2):
-            ant = 2 * step + half
+def channelize_kernel(samples_ref, proto_ref, table_ref, out_ref, planes, filtered, turned):
+    chans, block, columns = out_ref.shape
+    spectra = columns // 2
+    lane_tiles = chans // LANES
+    in_frames = spectra + TAPS - 1
+    group = filtered.shape[1] // spectra
+    words = 2 * lane_tiles
+    rows = in_frames * words
+    fold = turned.shape[2] // chans
+
+    def convolve(step):
+        planes[...] = samples_ref[step * group * rows : (step + 1) * group * rows, :].astype(jnp.float32)
+        for member in range(group):
             for part in range(2):
-                for lane in range(0, chans, LANES):
-                    cols = slice(lane, lane + LANES)
-                    frames[0:in_frames, :] = samples_ref[ant, part, :, cols].astype(jnp.float32)
-                    total = proto_ref[0:1, cols] * frames[pl.ds(0, spectra), :]
-                    for tap in range(1, TAPS):
-                        total = total + proto_ref[tap : tap + 1, cols] * frames[pl.ds(tap, spectra), :]
+                for tile in range(lane_tiles):
+                    cols = slice(tile * LANES, (tile + 1) * LANES)
+                    first = member * rows + 2 * tile + part
+                    total = None
+                    for tap in range(TAPS):
+                        term = (
+                            proto_ref[tap : tap + 1, cols]
+                            * planes[pl.ds(first + tap * words, spectra, stride=words), :]
+                        )
+                        total = term if total is None else total + term
                     filtered[
-                        half * spectra : (half + 1) * spectra,
-                        part * chans + lane : part * chans + lane + LANES,
+                        step % 2,
+                        member * spectra : (member + 1) * spectra,
+                        part * chans + tile * LANES : part * chans + (tile + 1) * LANES,
                     ] = total.astype(jnp.bfloat16)
+
+    def transform(step):
         product = lax.dot_general(
             table_ref[...],
-            filtered[...],
+            filtered[step % 2],
             (((1,), (1,)), ((), ())),
             preferred_element_type=jnp.float32,
         )
-        for half in range(2):
+        for member in range(group):
             for part in range(2):
-                turned[part, pl.ds(2 * step + half, chans, stride=block), :] = product[
-                    part * chans : (part + 1) * chans, half * spectra : (half + 1) * spectra
+                ant = group * step + member
+                turned[ant // fold, part, pl.ds(ant % fold, chans, stride=fold), :] = product[
+                    part * chans : (part + 1) * chans, member * spectra : (member + 1) * spectra
                 ]
-        return carry
-
-    lax.fori_loop(0, block // 2, pair, 0)
+
+    steps = block // group
+    convolve(0)
+    for step in range(steps):
+        if step + 1 < steps:
+            convolve(step + 1)
+        transform(step)
     for part in range(2):
-        out_ref[:, :, part * spectra : (part + 1) * spectra] = (
-            turned[part].reshape(chans, block, spectra).astype(jnp.bfloat16)
-        )
+        pieces = [turned[i, part].reshape(chans, fold, spectra) for i in range(block // fold)]
+        out_ref[:, :, part * spectra : (part + 1) * spectra] = jnp.concatenate(
+            pieces, axis=1
+        ).astype(jnp.bfloat16)
 
 
 def channelize(samples, proto, table, first, count, block):
-    _, _, in_frames, chans = samples.shape
+    antennas, _, in_frames, chans = samples.shape
     spectra = in_frames - TAPS + 1
-
+    lane_tiles = chans // LANES
+    rows = in_frames * lane_tiles * 2
+    fold = 8 if block % 8 == 0 else block
+    group = FILTER_ANTENNAS if block % FILTER_ANTENNAS == 0 else block
+    flat = (
+        samples.reshape(antennas, 2, in_frames, lane_tiles, LANES)
+        .transpose(0, 2, 3, 1, 4)
+        .reshape(antennas * rows, LANES)
+    )
     return pl.pallas_call(
         channelize_kernel,
         grid=(count // block,),
         in_specs=[
-            pl.BlockSpec((block, 2, in_frames, chans), lambda i: (i + first // block, 0, 0, 0)),
+            pl.BlockSpec((block * rows, LANES), lambda i: (i + first // block, 0)),
             pl.BlockSpec((TAPS, chans), lambda i: (0, 0)),
             pl.BlockSpec((2 * chans, 2 * chans), lambda i: (0, 0)),
         ],
         out_specs=pl.BlockSpec((chans, block, 2 * spectra), lambda i: (0, i, 0)),
         out_shape=jax.ShapeDtypeStruct((chans, count, 2 * spectra), jnp.bfloat16),
         scratch_shapes=[
-            pltpu.VMEM((in_frames + 1, LANES), jnp.float32),
-            pltpu.VMEM((2 * spectra, 2 * chans), jnp.bfloat16),
-            pltpu.VMEM((2, chans * block, spectra), jnp.float32),
+            pltpu.VMEM((group * rows, LANES), jnp.float32),
+            pltpu.VMEM((2, group * spectra, 2 * chans), jnp.bfloat16),
+            pltpu.VMEM((block // fold, 2, chans * fold, spectra), jnp.float32),
         ],
         compiler_params=pltpu.CompilerParams(vmem_limit_bytes=VMEM_BYTES),
         cost_estimate=pl.CostEstimate(
@@ -119,33 +148,32 @@
             transcendentals=0,
         ),
         name="channelize",
-    )(samples, proto, table)
+    )(flat, proto, table)
 
 
 def beam_kernel(counts, *refs):
     x_refs = refs[: len(counts)]
     weights_ref, out_ref, turned = refs[len(counts) :]
-    channel = pl.program_id(0)
-    beams = out_ref.shape[0]
-    local = out_ref.shape[1]
-    spectra = turned.shape[2]
-    product = None
-    start = 0
-    for x_ref, count in zip(x_refs, counts):
-        rows = x_ref[:, 0].reshape(count, 2 * spectra)
-        term = jnp.dot(
-            weights_ref[0, :, start : start + count], rows, preferred_element_type=jnp.float32
-        )
-        product = term if product is None else product + term
-        start += count
-    turned[0, pl.ds(channel, beams, stride=local), :] = (
-        product[:beams, :spectra] + product[beams:, spectra:]
-    )
-    turned[1, pl.ds(channel, beams, stride=local), :] = (
-        product[:beams, spectra:] - product[beams:, :spectra]
-    )
-
-    @pl.when(channel == pl.num_programs(0) - 1)
+    step = pl.program_id(0)
+    beams, local, columns = out_ref.shape
+    spectra = columns // 2
+    group = weights_ref.shape[0]
+    for member in range(group):
+        product = None
+        start = 0
+        for x_ref, count in zip(x_refs, counts):
+            term = jnp.dot(
+                weights_ref[member, :, start : start + count],
+                x_ref[:, member].reshape(count, columns),
+                preferred_element_type=jnp.float32,
+            )
+            product = term if product is None else product + term
+            start += count
+        rows = pl.ds(step * group + member, beams, stride=local)
+        turned[0, rows, :] = product[:beams, :spectra] + product[beams:, spectra:]
+        turned[1, rows, :] = product[:beams, spectra:] - product[beams:, :spectra]
+
+    @pl.when(step == pl.num_programs(0) - 1)
     def _():
         for part in range(2):
             out_ref[:, :, part * spectra : (part + 1) * spectra] = (
@@ -158,14 +186,15 @@
     beams = double_beams // 2
     columns = blocks[0].shape[3]
     counts = tuple(x.shape[0] * x.shape[2] for x in blocks)
+    group = BEAM_CHANNELS if local % BEAM_CHANNELS == 0 else 1
     return pl.pallas_call(
         functools.partial(beam_kernel, counts),
-        grid=(local,),
+        grid=(local // group,),
         in_specs=[
-            pl.BlockSpec((x.shape[0], 1, x.shape[2], columns), lambda c: (0, c, 0, 0))
+            pl.BlockSpec((x.shape[0], group, x.shape[2], columns), lambda c: (0, c, 0, 0))
             for x in blocks
         ]
-        + [pl.BlockSpec((1, double_beams, antennas), lambda c: (c, 0, 0))],
+        + [pl.BlockSpec((group, double_beams, antennas), lambda c: (c, 0, 0))],
         out_specs=pl.BlockSpec((beams, local, columns), lambda c: (0, 0, 0)),
         out_shape=jax.ShapeDtypeStruct((beams, local, columns), jnp.bfloat16),
         scratch_shapes=[pltpu.VMEM((2, beams * local, columns // 2), jnp.float32)],
@@ -267,51 +296,63 @@
     )(order[:, None], ids[None, :], flags[None, :], *blocks)
 
 
-def synthesize_kernel(beams_ref, proto_ref, table_ref, out_ref, zeta):
-    sources, _, local, columns = beams_ref.shape
+def synthesize_kernel(beams_ref, proto_ref, table_ref, out_ref, zeta, planes):
+    sources, group, local, columns = beams_ref.shape
     chans = sources * local
     spectra = columns // 2
-    out_frames = out_ref.shape[2]
-    rows = beams_ref[:, 0].reshape(chans, columns)
-    for part in range(2):
-        cols = slice(part * chans, (part + 1) * chans)
-        value = None
-        for source in range(2):
-            term = lax.dot_general(
-                rows[:, source * spectra : (source + 1) * spectra],
-                table_ref[source * chans : (source + 1) * chans, cols],
-                (((0,), (0,)), ((), ())),
-                preferred_element_type=jnp.float32,
-            )
-            value = term if value is None else value + term
-        value = value.astype(jnp.bfloat16).astype(jnp.float32)
-        for lane in range(0, chans, LANES):
-            zeta[...] = value[:, lane : lane + LANES]
-            total = proto_ref[TAPS - 1 : TAPS, lane : lane + LANES] * zeta[pl.ds(0, out_frames), :]
-            for tap in range(1, TAPS):
-                total = total + (
-                    proto_ref[TAPS - 1 - tap : TAPS - tap, lane : lane + LANES]
-                    * zeta[pl.ds(tap, out_frames), :]
+    lane_tiles = chans // LANES
+    words = 2 * lane_tiles
+    out_frames = planes.shape[0] // (group * words)
+    for member in range(group):
+        rows = beams_ref[:, member].reshape(chans, columns)
+        for part in range(2):
+            cols = slice(part * chans, (part + 1) * chans)
+            value = None
+            for source in range(2):
+                term = lax.dot_general(
+                    rows[:, source * spectra : (source + 1) * spectra],
+                    table_ref[source * chans : (source + 1) * chans, cols],
+                    (((0,), (0,)), ((), ())),
+                    preferred_element_type=jnp.float32,
                 )
-            out_ref[0, part, :, lane : lane + LANES] = total.astype(jnp.bfloat16)
+                value = term if value is None else value + term
+            value = value.astype(jnp.bfloat16).astype(jnp.float32)
+            for tile in range(lane_tiles):
+                lanes = slice(tile * LANES, (tile + 1) * LANES)
+                zeta[...] = value[:, lanes]
+                total = proto_ref[TAPS - 1 : TAPS, lanes] * zeta[pl.ds(0, out_frames), :]
+                for tap in range(1, TAPS):
+                    total = total + (
+                        proto_ref[TAPS - 1 - tap : TAPS - tap, lanes]
+                        * zeta[pl.ds(tap, out_frames), :]
+                    )
+                first = member * out_frames * words + 2 * tile + part
+                planes[pl.ds(first, out_frames, stride=words), :] = total
+    out_ref[...] = planes[...].astype(jnp.bfloat16)
 
 
 def synthesize(arranged, proto, table):
     sources, beams, local, columns = arranged.shape
     chans = sources * local
     spectra = columns // 2
+    lane_tiles = chans // LANES
     out_frames = spectra - TAPS + 1
-    return pl.pallas_call(
+    rows = out_frames * lane_tiles * 2
+    group = 4 if beams % 4 == 0 else beams
+    flat = pl.pallas_call(
         synthesize_kernel,
-        grid=(beams,),
+        grid=(beams // group,),
         in_specs=[
-            pl.BlockSpec((sources, 1, local, columns), lambda b: (0, b, 0, 0)),
+            pl.BlockSpec((sources, group, local, columns), lambda b: (0, b, 0, 0)),
             pl.BlockSpec((TAPS, chans), lambda b: (0, 0)),
             pl.BlockSpec((2 * chans, 2 * chans), lambda b: (0, 0)),
         ],
-        out_specs=pl.BlockSpec((1, 2, out_frames, chans), lambda b: (b, 0, 0, 0)),
-        out_shape=jax.ShapeDtypeStruct((beams, 2, out_frames, chans), jnp.bfloat16),
-        scratch_shapes=[pltpu.VMEM((spectra, LANES), jnp.float32)],
+        out_specs=pl.BlockSpec((group * rows, LANES), lambda b: (b, 0)),
+        out_shape=jax.ShapeDtypeStruct((beams * rows, LANES), jnp.bfloat16),
+        scratch_shapes=[
+            pltpu.VMEM((spectra, LANES), jnp.float32),
+            pltpu.VMEM((group * rows, LANES), jnp.float32),
+        ],
         compiler_params=pltpu.CompilerParams(vmem_limit_bytes=VMEM_BYTES),
         cost_estimate=pl.CostEstimate(
             flops=2 * beams * spectra * 4 * chans * chans,
@@ -320,6 +361,11 @@
         ),
         name="synthesize",
     )(arranged, proto, table)
+    return (
+        flat.reshape(beams, out_frames, lane_tiles, 2, LANES)
+        .transpose(0, 3, 1, 2, 4)
+        .reshape(beams, 2, out_frames, chans)
+    )
 
 
 def per_device(samples, flags, delays, order):

time: 310 us -> 283 us (0.913)
  Pallas kernels: 118 us -> 97.6 us
  local copies, waits for them, and re-layouts: 20.4 us -> 6.91 us
  waiting for transfers between devices: 76 us -> 83.3 us
    unnamed x11 -> x9, local copies, waits for them, and re-layouts: 16.4 us -> 2.9 us
    pallas_call x2, Pallas kernels: 32.2 us -> 21.5 us  [the longest x1 12.3 us: form_beams(): pl.pallas_call(functools.partial(beam_kernel, counts), grid=(local // gro...]
    pallas_call x2, Pallas kernels: 44.5 us -> 34.8 us  [channelize(): pl.pallas_call(channelize_kernel, grid=(count // block,), in_specs=[pl.Bl...]
    all_to_all x2, waiting for transfers between devices: 71.7 us -> 79.1 us  [per_device(): part = lax.all_to_all(part, 'chan', split_axis=0, concat_axis=0, tiled=True)]
  transfers between devices with their start and end apart: 3 -> 3, of which waited for: 3 -> 3; matrix products, arithmetic and copies ran while one was open for 27% -> 29% of each run, Pallas kernels for 24% -> 23%
where the time goes in v2:
time: 283 us; the launch traced here: 282 us
  Pallas kernels  97.6 us (34%)
  waiting for transfers between devices  83.3 us (29%)
  other arithmetic  77.3 us (27%)
  starting transfers between devices  16.1 us (6%)
  local copies, waits for them, and re-layouts  6.91 us (2%)
    all_to_all x2, waiting for transfers between devices, per_device(): part = lax.all_to_all(part, 'chan', split_axis=0, concat_axis=0, tiled=True)  79.1 us
    mul x1, other arithmetic, per_device(): jnp.cos(angle).astype(jnp.bfloat16) * keep.astype(jnp.bfloat16)  67.8 us
    pallas_call x1, Pallas kernels, correlate(): pl.pallas_call(functools.partial(visibility_kernel, counts), grid=(local,...  41.4 us
    pallas_call x2, Pallas kernels, channelize(): pl.pallas_call(channelize_kernel, grid=(count // block,), in_specs=[pl.Bl...  34.8 us
    pallas_call x1, Pallas kernels, form_beams(): pl.pallas_call(functools.partial(beam_kernel, counts), grid=(local // gro...  12.3 us
    all_to_all x2, starting transfers between devices, per_device(): part = lax.all_to_all(part, 'chan', split_axis=0, concat_axis=0, tiled=True)  11.3 us
    pallas_call x1, Pallas kernels, synthesize(): pl.pallas_call(synthesize_kernel, grid=(beams // group,), in_specs=[pl.Bl...  9.13 us
    concatenate x1, other arithmetic, per_device(): jnp.concatenate([jnp.cos(angle).astype(jnp.bfloat16) * keep.astype(jnp.bf...  6.69 us
  transfers between devices with their start and end apart: 3, of which 3 were waited for; matrix products, arithmetic and copies ran while one was open for 29% of the time, Pallas kernels for 23%

profile of v2, /device:TPU:15, one launch (start us, length us, event | category | flops | bytes accessed | tf_op | source)
XLA Modules:
  0.0 282.0 jit_solution(1518250429706654283)
XLA Ops:
  0.6 10.2 %channelize.2 = bf16[256,16,256]{2,1,0:T(8,128)(2,1)} custom-call(bf16[36608,128]{1,0:T(8,128)(2,1)} %bitcast.18, f32[16,256]{1,0:T(8,128)} %constant.31.clone.proto_ref, bf16[512,512]{1,0:T(8,128)(2,1)} %constant.32.clone.table_ref), custom_call_target="tpu_custom_call" | custom-call | flops 2147483648 | bytes 4440064 | tf_op jit(solution)/shard_map/channelize/pallas_call | solution.py:129
  10.8 6.5 %all-to-all-start = ((bf16[256,16,256]{2,1,0:T(8,128)(2,1)}), bf16[256,16,256]{2,1,0:T(8,128)(2,1)S(1)}, u32[]{:S(2)}, u32[]{:S(2)}) async-start(bf16[256,16,256]{2,1,0:T(8,128)(2,1)} %channelize.2), calls=%async_computation | async-start | bytes 4194304 | tf_op jit(solution)/shard_map/all_to_all | solution.py:390
  17.4 0.0 copy-start.3
  17.4 24.6 %channelize.3 = bf16[256,48,256]{2,1,0:T(8,128)(2,1)} custom-call(bf16[36608,128]{1,0:T(8,128)(2,1)} %bitcast.19, f32[16,256]{1,0:T(8,128)} %constant.31.clone.proto_ref, bf16[512,512]{1,0:T(8,128)(2,1)} %constant.32.clone.table_ref), custom_call_target="tpu_custom_call" | custom-call | flops 6442450944 | bytes 13320192 | tf_op jit(solution)/shard_map/channelize/pallas_call | solution.py:129
  42.0 22.8 %all-to-all-done = bf16[256,16,256]{2,1,0:T(8,128)(2,1)S(1)} async-done(((bf16[256,16,256]{2,1,0:T(8,128)(2,1)}), bf16[256,16,256]{2,1,0:T(8,128)(2,1)S(1)}, u32[]{:S(2)}, u32[]{:S(2)}) %all-to-all-start) | async-done | bytes 2097184 | tf_op jit(solution)/shard_map/all_to_all | solution.py:390
  64.8 0.0 copy-start.1
  64.8 4.8 %all-to-all-start.1 = ((bf16[256,48,256]{2,1,0:T(8,128)(2,1)}), bf16[256,48,256]{2,1,0:T(8,128)(2,1)}, u32[]{:S(2)}, u32[]{:S(2)}) async-start(bf16[256,48,256]{2,1,0:T(8,128)(2,1)} %channelize.3), calls=%async_computation.1 | async-start | bytes 12582912 | tf_op jit(solution)/shard_map/all_to_all | solution.py:390
  69.6 1.6 copy.14
  71.2 1.0 slice.19
  72.1 0.0 copy-done.3
  72.1 0.1 reshape.98
  72.2 0.1 slice.17
  72.3 0.1 concatenate.34
  72.3 0.1 concatenate.35
  72.4 2.2 pad_add_fusion
  74.6 1.6 copy.15
  76.2 67.8 %fusion.3 = (bf16[16,256,1024]{2,1,0:T(8,128)(2,1)S(1)}, bf16[16,256,1024]{2,1,0:T(8,128)(2,1)S(1)}) fusion(s32[16]{0:T(128)S(1)} %iota_add_fusion, s32[256,1024]{1,0:T(8,128)S(1)} %copy.15, bf16[1024]{0:T(1024)(128)(2,1)S(1)} %fusion.6), kind=kLoop, calls=%fused_computation.11 | loop fusion | flops 96468992 | bytes 17827904 | tf_op jit(solution)/shard_map/mul | solution.py:415
  144.0 0.0 copy-done.1
  144.0 6.7 %pad_maximum_fusion.refs_2_ = bf16[16,512,1024]{2,1,0:T(8,128)(2,1)} fusion(bf16[16,256,1024]{2,1,0:T(8,128)(2,1)S(1)} %get-tuple-element.3, bf16[16,256,1024]{2,1,0:T(8,128)(2,1)S(1)} %get-tuple-element.2), kind=kLoop, calls=%fused_computation.8 | loop fusion | flops 33554432 | bytes 33554432 | tf_op jit(solution)/shard_map/concatenate | solution.py:413
  150.7 0.0 copy-start.2
  150.7 56.3 %all-to-all-done.1 = bf16[256,48,256]{2,1,0:T(8,128)(2,1)} async-done(((bf16[256,48,256]{2,1,0:T(8,128)(2,1)}), bf16[256,48,256]{2,1,0:T(8,128)(2,1)}, u32[]{:S(2)}, u32[]{:S(2)}) %all-to-all-start.1) | async-done | bytes 6291488 | tf_op jit(solution)/shard_map/all_to_all | solution.py:390
  207.0 12.3 %form_beams.1 = bf16[256,16,256]{2,1,0:T(8,128)(2,1)} custom-call(bf16[16,16,16,256]{3,2,1,0:T(8,128)(2,1)} %bitcast.21, bf16[16,16,48,256]{3,2,1,0:T(8,128)(2,1)} %bitcast.7.refs_1_, bf16[16,512,1024]{2,1,0:T(8,128)(2,1)} %pad_maximum_fusion.refs_2_), custom_call_target="tpu_custom_call" | custom-call | flops 4294967296 | bytes 27262976 | tf_op jit(solution)/shard_map/form_beams/pallas_call | solution.py:190
  219.3 4.8 %all-to-all-start.2 = ((bf16[256,16,256]{2,1,0:T(8,128)(2,1)}), bf16[256,16,256]{2,1,0:T(8,128)(2,1)S(1)}, u32[]{:S(2)}, u32[]{:S(2)}) async-start(bf16[256,16,256]{2,1,0:T(8,128)(2,1)} %form_beams.1), calls=%async_computation.2 | async-start | bytes 4194304 | tf_op jit(solution)/shard_map/all_to_all | solution.py:421
  224.1 0.1 concatenate.30
  224.2 0.1 concatenate.31
  224.3 0.0 copy-done.2
  224.3 1.0 copy.13.order_ref
  225.3 0.6 add_convert_fusion.flags_ref
  225.9 41.4 %correlate.1 = bf16[16,36,2,128,128]{4,3,2,1,0:T(8,128)(2,1)} custom-call(s32[1024,1]{1,0:T(8,128)} %copy.13.order_ref, s32[1,1024]{1,0:T(1,128)} %constant.34.ids_ref, f32[1,1024]{1,0:T(1,128)} %add_convert_fusion.flags_ref, bf16[16,16,16,256]{3,2,1,0:T(8,128)(2,1)} %bitcast.22, bf16[16,16,48,256]{3,2,1,0:T(8,128)(2,1)} %bitcast.7.refs_1_), custom_call_target="tpu_custom_call" | custom-call | flops 18253611008 | bytes 46137344 | tf_op jit(solution)/shard_map/correlate/pallas_call | solution.py:266
  267.3 4.3 %all-to-all-done.2 = bf16[256,16,256]{2,1,0:T(8,128)(2,1)S(1)} async-done(((bf16[256,16,256]{2,1,0:T(8,128)(2,1)}), bf16[256,16,256]{2,1,0:T(8,128)(2,1)S(1)}, u32[]{:S(2)}, u32[]{:S(2)}) %all-to-all-start.2) | async-done | bytes 2097184 | tf_op jit(solution)/shard_map/all_to_all | solution.py:421
  271.5 0.0 copy-start
  271.5 1.3 copy-done
  272.9 9.1 %synthesize.1 = bf16[7232,128]{1,0:T(8,128)(2,1)} custom-call(bf16[16,16,16,256]{3,2,1,0:T(8,128)(2,1)} %bitcast.20, f32[16,256]{1,0:T(8,128)} %constant.31.clone.proto_ref, bf16[512,512]{1,0:T(8,128)(2,1)} %constant.32.clone.table_ref), custom_call_target="tpu_custom_call" | custom-call | flops 1073741824 | bytes 3948544 | tf_op jit(solution)/shard_map/synthesize/pallas_call | solution.py:342
  (3 shorter events, 0.0 us)
Async XLA Ops:
  10.8 53.9 %all-to-all-start = ((bf16[256,16,256]{2,1,0:T(8,128)(2,1)}), bf16[256,16,256]{2,1,0:T(8,128)(2,1)S(1)}, u32[]{:S(2)}, u32[]{:S(2)}) async-start(bf16[256,16,256]{2,1,0:T(8,128)(2,1)} %channelize.2), calls=%async_computation | async-start | bytes 4194304 | tf_op jit(solution)/shard_map/all_to_all | solution.py:390
  17.4 54.8 %copy-start.3 = (s32[1024]{0:T(1024)S(1)}, s32[1024]{0:T(1024)}, u32[]{:S(2)}) copy-start(s32[1024]{0:T(1024)} %param.9) | copy-start | bytes 12292
  64.8 79.2 %copy-start.1 = (bf16[256,16,256]{2,1,0:T(8,128)(2,1)}, bf16[256,16,256]{2,1,0:T(8,128)(2,1)S(1)}, u32[]{:S(2)}) copy-start(bf16[256,16,256]{2,1,0:T(8,128)(2,1)S(1)} %all-to-all-done) | copy-start | bytes 6291460
  64.8 142.2 %all-to-all-start.1 = ((bf16[256,48,256]{2,1,0:T(8,128)(2,1)}), bf16[256,48,256]{2,1,0:T(8,128)(2,1)}, u32[]{:S(2)}, u32[]{:S(2)}) async-start(bf16[256,48,256]{2,1,0:T(8,128)(2,1)} %channelize.3), calls=%async_computation.1 | async-start | bytes 12582912 | tf_op jit(solution)/shard_map/all_to_all | solution.py:390
  150.7 73.6 %copy-start.2 = (s32[1024]{0:T(1024)S(1)}, s32[1024]{0:T(1024)}, u32[]{:S(2)}) copy-start(s32[1024]{0:T(1024)} %param.11) | copy-start | bytes 12292
  219.3 52.2 %all-to-all-start.2 = ((bf16[256,16,256]{2,1,0:T(8,128)(2,1)}), bf16[256,16,256]{2,1,0:T(8,128)(2,1)S(1)}, u32[]{:S(2)}, u32[]{:S(2)}) async-start(bf16[256,16,256]{2,1,0:T(8,128)(2,1)} %form_beams.1), calls=%async_computation.2 | async-start | bytes 4194304 | tf_op jit(solution)/shard_map/all_to_all | solution.py:421
  271.5 1.3 copy-start

commit v3 on v2

--- a/solution.py
+++ b/solution.py
@@ -10,9 +10,10 @@
 from jax.experimental.pallas import tpu as pltpu
 from jax.sharding import PartitionSpec as P
 
+
 TAPS = 16
 TILE_ANTENNAS = 128
-BLOCK_ANTENNAS = 16
+CHUNK_ANTENNAS = 16
 FILTER_ANTENNAS = 8
 BEAM_CHANNELS = 4
 LANES = 128
@@ -37,17 +38,7 @@
     return table.astype(np.float32).astype(ml_dtypes.bfloat16)
 
 
-def forward_table(chan_count):
-    cosine, sine = dft_parts(chan_count)
-    table = np.concatenate(
-        [np.concatenate([cosine, sine], axis=1), np.concatenate([-sine, cosine], axis=1)], axis=0
-    )
-    return (round_bf16(table).astype(np.float32) / math.sqrt(chan_count)).astype(
-        ml_dtypes.bfloat16
-    )
-
-
-def inverse_table(chan_count):
+def transform_table(chan_count):
     cosine, sine = dft_parts(chan_count)
     table = np.concatenate(
         [np.concatenate([cosine, sine], axis=1), np.concatenate([-sine, cosine], axis=1)], axis=0
@@ -114,13 +105,14 @@
         ).astype(jnp.bfloat16)
 
 
-def channelize(samples, proto, table, first, count, block):
+def channelize(samples, proto, table, first, count):
     antennas, _, in_frames, chans = samples.shape
     spectra = in_frames - TAPS + 1
     lane_tiles = chans // LANES
     rows = in_frames * lane_tiles * 2
-    fold = 8 if block % 8 == 0 else block
-    group = FILTER_ANTENNAS if block % FILTER_ANTENNAS == 0 else block
+    block = FILTER_ANTENNAS if count % FILTER_ANTENNAS == 0 and first % FILTER_ANTENNAS == 0 else count
+    fold = block
+    group = block
     flat = (
         samples.reshape(antennas, 2, in_frames, lane_tiles, LANES)
         .transpose(0, 2, 3, 1, 4)
@@ -218,11 +210,14 @@
 
     @pl.when(pl.program_id(0) == 0)
     def _():
-        for t in range(tiles):
-            rows = slice(t * tile, (t + 1) * tile)
+        def fill(t, carry):
+            rows = pl.ds(pl.multiple_of(t * tile, tile), tile)
             select[rows, :] = jnp.where(
                 order_ref[rows, :] == ids_ref[...], flags_ref[...], 0.0
             ).astype(jnp.bfloat16)
+            return carry
+
+        lax.fori_loop(0, tiles, fill, 0)
 
     product = None
     start = 0
@@ -368,6 +363,36 @@
     )
 
 
+def turn(part):
+    return lax.all_to_all(part, "chan", split_axis=0, concat_axis=0, tiled=True)
+
+
+def exchange_early(first, second):
+    devices = lax.axis_size("chan")
+    me = lax.axis_index("chan")
+    chans = first.shape[0]
+
+    def send(source, mask):
+        split = source.reshape((devices, chans // devices) + source.shape[1:])
+        mine = lax.dynamic_index_in_dim(split, me ^ mask, 0, keepdims=False)
+        if mask == 0:
+            return mine
+        return lax.ppermute(mine, "chan", [(i, i ^ mask) for i in range(devices)])
+
+    far = [mask for mask in range(devices // 2, devices)]
+    near = [mask for mask in range(devices // 2)]
+    got = {mask: send(first, mask) for mask in far}
+    late, second = lax.optimization_barrier((first, second))
+    rest = turn(second)
+    got.update({mask: send(late, mask) for mask in near})
+    stacked = jnp.stack([got[mask] for mask in range(devices)])
+    ordered = [
+        lax.dynamic_index_in_dim(stacked, me ^ source, 0, keepdims=False)
+        for source in range(devices)
+    ]
+    return jnp.concatenate(ordered, axis=0), rest
+
+
 def per_device(samples, flags, delays, order):
     devices = lax.axis_size("chan")
     antennas_here, _, in_frames, chans = samples.shape
@@ -375,24 +400,29 @@
     spectra = in_frames - TAPS + 1
     antennas = antennas_here * devices
     beam_count = delays.shape[0]
-    block = BLOCK_ANTENNAS if antennas_here % BLOCK_ANTENNAS == 0 else antennas_here
+    block = CHUNK_ANTENNAS if antennas_here > CHUNK_ANTENNAS else antennas_here
     sizes = [block, antennas_here - block] if antennas_here > block else [block]
 
     proto = jnp.asarray(prototype(TAPS, chans))
-    forward = jnp.asarray(forward_table(chans))
-    inverse = jnp.asarray(inverse_table(chans))
-
-    blocks = []
+    table = jnp.asarray(transform_table(chans))
+
+    parts = []
     columns_of = []
     start = 0
     for size in sizes:
-        part = channelize(samples, proto, forward, start, size, block)
-        part = lax.all_to_all(part, "chan", split_axis=0, concat_axis=0, tiled=True)
-        blocks.append(part.reshape(devices, local_channels, size, 2 * spectra))
+        parts.append(channelize(samples, proto, table, start, size))
         ids = np.arange(antennas, dtype=np.int32).reshape(devices, antennas_here)
         columns_of.append(ids[:, start : start + size].reshape(-1))
         start += size
     ids = np.concatenate(columns_of)
+    if len(parts) > 1:
+        early, rest = exchange_early(parts[0], parts[1])
+        parts = [early, rest]
+    else:
+        parts = [turn(parts[0])]
+    blocks = [
+        x.reshape(devices, local_channels, size, 2 * spectra) for x, size in zip(parts, sizes)
+    ]
 
     def arrange(x):
         x = x.reshape(x.shape[:-1] + (devices, antennas_here))
@@ -418,10 +448,10 @@
         axis=1,
     )
     beams = form_beams(blocks, weights)
-    arranged = lax.all_to_all(beams, "chan", split_axis=0, concat_axis=0, tiled=True)
+    arranged = turn(beams)
     arranged = arranged.reshape(devices, beam_count // devices, local_channels, 2 * spectra)
     visibilities = correlate(blocks, order, jnp.asarray(ids), flag_row)
-    voltages = synthesize(arranged, proto, inverse)
+    voltages = synthesize(arranged, proto, table)
     return visibilities, voltages
 
 
@@ -431,6 +461,7 @@
         P(("groups", "chan"), None, None, None, None),
         P(("groups", "chan"), None, None, None),
     )
+
     return jax.shard_map(
         per_device, mesh=mesh, in_specs=in_specs, out_specs=out_specs, check_vma=False
     )

time: 283 us -> 323 us (1.14)
  starting transfers between devices: 16.1 us -> 49.8 us
  local copies, waits for them, and re-layouts: 6.91 us -> 13.4 us
    ppermute x0 -> x15, waiting for transfers between devices: none -> 82.1 us  [send(): return lax.ppermute(mine, 'chan', [(i, i ^ mask) for i in range(devices)])]
    all_to_all x3 -> x2, waiting for transfers between devices: 83.3 us -> 3.78 us  [turn(): return lax.all_to_all(part, 'chan', split_axis=0, concat_axis=0, tiled=True)]
    ppermute x0 -> x15, starting transfers between devices: none -> 26.5 us  [send(): return lax.ppermute(mine, 'chan', [(i, i ^ mask) for i in range(devices)])]
    all_to_all x3 -> x2, starting transfers between devices: 16.1 us -> 23.3 us  [turn(): return lax.all_to_all(part, 'chan', split_axis=0, concat_axis=0, tiled=True)]
    unnamed x9 -> x68, local copies, waits for them, and re-layouts: 2.9 us -> 7.64 us
  transfers between devices with their start and end apart: 3 -> 17, of which waited for: 3 -> 11; matrix products, arithmetic and copies ran while one was open for 29% -> 27% of each run, Pallas kernels for 23% -> 13%
where the time goes in v3:
time: 323 us; the launch traced here: 322 us
  Pallas kernels  96.7 us (30%)
  waiting for transfers between devices  85.9 us (27%)
  other arithmetic  75.3 us (23%)
  starting transfers between devices  49.8 us (15%)
  local copies, waits for them, and re-layouts  13.4 us (4%)
    ppermute x15, waiting for transfers between devices, send(): return lax.ppermute(mine, 'chan', [(i, i ^ mask) for i in range(devices)])  82.1 us
    mul x1, other arithmetic, per_device(): jnp.cos(angle).astype(jnp.bfloat16) * keep.astype(jnp.bfloat16)  67.8 us
    pallas_call x1, Pallas kernels, correlate(): pl.pallas_call(functools.partial(visibility_kernel, counts), grid=(local,...  41.9 us
    pallas_call x2, Pallas kernels, channelize(): pl.pallas_call(channelize_kernel, grid=(count // block,), in_specs=[pl.Bl...  33.3 us
    ppermute x15, starting transfers between devices, send(): return lax.ppermute(mine, 'chan', [(i, i ^ mask) for i in range(devices)])  26.5 us
    all_to_all x2, starting transfers between devices, turn(): return lax.all_to_all(part, 'chan', split_axis=0, concat_axis=0, tiled=True)  23.3 us
    pallas_call x1, Pallas kernels, form_beams(): pl.pallas_call(functools.partial(beam_kernel, counts), grid=(local // gro...  12.4 us
    pallas_call x1, Pallas kernels, synthesize(): pl.pallas_call(synthesize_kernel, grid=(beams // group,), in_specs=[pl.Bl...  9.13 us
  transfers between devices with their start and end apart: 17, of which 11 were waited for; matrix products, arithmetic and copies ran while one was open for 27% of the time, Pallas kernels for 13%

profile of v3, /device:TPU:15, one launch (start us, length us, event | category | flops | bytes accessed | tf_op | source)
XLA Modules:
  0.0 322.2 jit_solution(3095829513479152261)
XLA Ops:
  0.6 9.5 %channelize.2 = bf16[256,16,256]{2,1,0:T(8,128)(2,1)} custom-call(bf16[36608,128]{1,0:T(8,128)(2,1)} %bitcast.112, f32[16,256]{1,0:T(8,128)} %constant.127.clone.proto_ref, bf16[512,512]{1,0:T(8,128)(2,1)} %constant.128.clone.table_ref), custom_call_target="tpu_custom_call" | custom-call | flops 2147483648 | bytes 4440064 | tf_op jit(solution)/shard_map/channelize/pallas_call | solution.py:121
  10.1 23.8 %channelize.3 = bf16[256,48,256]{2,1,0:T(8,128)(2,1)} custom-call(bf16[36608,128]{1,0:T(8,128)(2,1)} %bitcast.113, f32[16,256]{1,0:T(8,128)} %constant.127.clone.proto_ref, bf16[512,512]{1,0:T(8,128)(2,1)} %constant.128.clone.table_ref), custom_call_target="tpu_custom_call" | custom-call | flops 6442450944 | bytes 13320192 | tf_op jit(solution)/shard_map/channelize/pallas_call | solution.py:121
  33.9 6.6 %all-to-all-start = ((bf16[256,48,256]{2,1,0:T(8,128)(2,1)}), bf16[256,48,256]{2,1,0:T(8,128)(2,1)}, u32[]{:S(2)}, u32[]{:S(2)}) async-start(bf16[256,48,256]{2,1,0:T(8,128)(2,1)} %channelize.3), calls=%async_computation | async-start | bytes 12582912 | tf_op jit(solution)/shard_map/all_to_all | solution.py:367
  40.6 0.9 dynamic-slice_bitcast_fusion
  41.4 1.5 collective-permute-start.14
  42.9 1.2 collective-permute-start.13
  44.1 1.5 collective-permute-start.12
  45.8 1.0 dynamic-slice_bitcast_fusion.8
  46.8 0.4 collective-permute-start
  47.2 0.3 copy.13
  48.0 0.6 concatenate.38
  48.7 0.7 concatenate.39
  49.4 0.3 copy.14
  50.1 67.8 %fusion.3 = (bf16[16,256,1024]{2,1,0:T(8,128)(2,1)S(1)}, bf16[16,256,1024]{2,1,0:T(8,128)(2,1)S(1)}) fusion(s32[16]{0:T(128)S(1)} %iota_add_fusion, s32[256,1024]{1,0:T(8,128)S(1)} %copy.14, bf16[1024]{0:T(1024)(128)(2,1)S(1)} %fusion.6), kind=kLoop, calls=%fused_computation.11 | loop fusion | flops 96468992 | bytes 17827904 | tf_op jit(solution)/shard_map/mul | solution.py:445
  118.0 6.8 %pad_maximum_fusion.refs_2_ = bf16[16,512,1024]{2,1,0:T(8,128)(2,1)} fusion(bf16[16,256,1024]{2,1,0:T(8,128)(2,1)S(1)} %get-tuple-element.23, bf16[16,256,1024]{2,1,0:T(8,128)(2,1)S(1)} %get-tuple-element.22), kind=kLoop, calls=%fused_computation.8 | loop fusion | flops 33554432 | bytes 33554432 | tf_op jit(solution)/shard_map/concatenate | solution.py:443
  124.8 0.3 collective-permute-start.1
  125.2 0.9 bitcast_dynamic-update-slice_fusion.30
  126.1 5.3 %collective-permute-done.1 = bf16[16,16,256]{2,1,0:T(8,128)(2,1)S(1)} collective-permute-done((bf16[16,16,256]{2,1,0:T(8,128)(2,1)S(1)}, bf16[16,16,256]{2,1,0:T(8,128)(2,1)S(1)}, u32[]{:S(2)}, u32[]{:S(2)}) %collective-permute-start.1) | collective-permute-done | bytes 131104 | tf_op jit(solution)/shard_map/ppermute | solution.py:380
  131.4 0.4 collective-permute-start.2
  131.9 13.5 %collective-permute-done.2 = bf16[16,16,256]{2,1,0:T(8,128)(2,1)S(1)} collective-permute-done((bf16[16,16,256]{2,1,0:T(8,128)(2,1)S(1)}, bf16[16,16,256]{2,1,0:T(8,128)(2,1)S(1)}, u32[]{:S(2)}, u32[]{:S(2)}) %collective-permute-start.2) | collective-permute-done | bytes 131104 | tf_op jit(solution)/shard_map/ppermute | solution.py:380
  145.4 7.4 %collective-permute-start.3 = (bf16[16,16,256]{2,1,0:T(8,128)(2,1)S(1)}, bf16[16,16,256]{2,1,0:T(8,128)(2,1)S(1)}, u32[]{:S(2)}, u32[]{:S(2)}) collective-permute-start(bf16[16,16,256]{2,1,0:T(8,128)(2,1)S(1)} %copy-done.12), channel_id=1, source_target_pairs={{0,4},{1,5},{2,6},{3,7},{4,0},{5,1},{6,2},{7,3},{8,12},{9,13},{10,... | collective-permute-start | bytes 393224 | tf_op jit(solution)/shard_map/ppermute | solution.py:380
  152.8 21.4 %collective-permute-done.3 = bf16[16,16,256]{2,1,0:T(8,128)(2,1)S(1)} collective-permute-done((bf16[16,16,256]{2,1,0:T(8,128)(2,1)S(1)}, bf16[16,16,256]{2,1,0:T(8,128)(2,1)S(1)}, u32[]{:S(2)}, u32[]{:S(2)}) %collective-permute-start.3) | collective-permute-done | bytes 131104 | tf_op jit(solution)/shard_map/ppermute | solution.py:380
  174.2 2.6 collective-permute-start.4
  176.8 3.8 %collective-permute-done.4 = bf16[16,16,256]{2,1,0:T(8,128)(2,1)S(1)} collective-permute-done((bf16[16,16,256]{2,1,0:T(8,128)(2,1)S(1)}, bf16[16,16,256]{2,1,0:T(8,128)(2,1)S(1)}, u32[]{:S(2)}, u32[]{:S(2)}) %collective-permute-start.4) | collective-permute-done | bytes 131104 | tf_op jit(solution)/shard_map/ppermute | solution.py:380
  180.6 1.5 collective-permute-start.5
  182.1 6.6 %collective-permute-done.5 = bf16[16,16,256]{2,1,0:T(8,128)(2,1)S(1)} collective-permute-done((bf16[16,16,256]{2,1,0:T(8,128)(2,1)S(1)}, bf16[16,16,256]{2,1,0:T(8,128)(2,1)S(1)}, u32[]{:S(2)}, u32[]{:S(2)}) %collective-permute-start.5) | collective-permute-done | bytes 131104 | tf_op jit(solution)/shard_map/ppermute | solution.py:380
  188.8 7.9 %collective-permute-done.6 = bf16[16,16,256]{2,1,0:T(8,128)(2,1)S(1)} collective-permute-done((bf16[16,16,256]{2,1,0:T(8,128)(2,1)S(1)}, bf16[16,16,256]{2,1,0:T(8,128)(2,1)S(1)}, u32[]{:S(2)}, u32[]{:S(2)}) %collective-permute-start.6) | collective-permute-done | bytes 131104 | tf_op jit(solution)/shard_map/ppermute | solution.py:380
  196.7 3.0 collective-permute-start.7
  199.8 7.6 %collective-permute-done.7 = bf16[16,16,256]{2,1,0:T(8,128)(2,1)S(1)} collective-permute-done((bf16[16,16,256]{2,1,0:T(8,128)(2,1)S(1)}, bf16[16,16,256]{2,1,0:T(8,128)(2,1)S(1)}, u32[]{:S(2)}, u32[]{:S(2)}) %collective-permute-start.7) | collective-permute-done | bytes 131104 | tf_op jit(solution)/shard_map/ppermute | solution.py:380
  207.4 4.0 %collective-permute-start.8 = (bf16[16,16,256]{2,1,0:T(8,128)(2,1)S(1)}, bf16[16,16,256]{2,1,0:T(8,128)(2,1)S(1)}, u32[]{:S(2)}, u32[]{:S(2)}) collective-permute-start(bf16[16,16,256]{2,1,0:T(8,128)(2,1)S(1)} %copy-done.7), channel_id=1, source_target_pairs={{0,9},{1,8},{2,11},{3,10},{4,13},{5,12},{6,15},{7,14},{8,1},{9,0},... | collective-permute-start | bytes 393224 | tf_op jit(solution)/shard_map/ppermute | solution.py:380
  211.4 4.2 %collective-permute-done.8 = bf16[16,16,256]{2,1,0:T(8,128)(2,1)S(1)} collective-permute-done((bf16[16,16,256]{2,1,0:T(8,128)(2,1)S(1)}, bf16[16,16,256]{2,1,0:T(8,128)(2,1)S(1)}, u32[]{:S(2)}, u32[]{:S(2)}) %collective-permute-start.8) | collective-permute-done | bytes 131104 | tf_op jit(solution)/shard_map/ppermute | solution.py:380
  215.6 0.7 collective-permute-start.9
  216.3 5.9 %collective-permute-done.9 = bf16[16,16,256]{2,1,0:T(8,128)(2,1)S(1)} collective-permute-done((bf16[16,16,256]{2,1,0:T(8,128)(2,1)S(1)}, bf16[16,16,256]{2,1,0:T(8,128)(2,1)S(1)}, u32[]{:S(2)}, u32[]{:S(2)}) %collective-permute-start.9) | collective-permute-done | bytes 131104 | tf_op jit(solution)/shard_map/ppermute | solution.py:380
  222.2 1.7 collective-permute-start.10
  223.9 5.8 %collective-permute-done.10 = bf16[16,16,256]{2,1,0:T(8,128)(2,1)S(1)} collective-permute-done((bf16[16,16,256]{2,1,0:T(8,128)(2,1)S(1)}, bf16[16,16,256]{2,1,0:T(8,128)(2,1)S(1)}, u32[]{:S(2)}, u32[]{:S(2)}) %collective-permute-start.10) | collective-permute-done | bytes 131104 | tf_op jit(solution)/shard_map/ppermute | solution.py:380
  229.8 0.9 bitcast_dynamic-update-slice_fusion.19
  230.7 0.9 bitcast_dynamic-update-slice_fusion.18
  231.6 0.9 bitcast_dynamic-update-slice_fusion.17
  232.6 0.9 bitcast_dynamic-update-slice_fusion.16
  233.9 1.3 copy-done.3
  235.2 12.4 %form_beams.1 = bf16[256,16,256]{2,1,0:T(8,128)(2,1)} custom-call(bf16[16,16,16,256]{3,2,1,0:T(8,128)(2,1)} %bitcast.120, bf16[16,16,48,256]{3,2,1,0:T(8,128)(2,1)} %bitcast.55.refs_1_, bf16[16,512,1024]{2,1,0:T(8,128)(2,1)} %pad_maximum_fusion.refs_2_), custom_call_target="tpu_custom_call" | custom-call | flops 4294967296 | bytes 27262976 | tf_op jit(solution)/shard_map/form_beams/pallas_call | solution.py:182
  247.6 16.7 %all-to-all-start.1 = ((bf16[256,16,256]{2,1,0:T(8,128)(2,1)}), bf16[256,16,256]{2,1,0:T(8,128)(2,1)S(1)}, u32[]{:S(2)}, u32[]{:S(2)}) async-start(bf16[256,16,256]{2,1,0:T(8,128)(2,1)} %form_beams.1), calls=%async_computation.1 | async-start | bytes 4194304 | tf_op jit(solution)/shard_map/all_to_all | solution.py:367
  264.5 1.0 copy.12.order_ref
  265.5 0.6 add_convert_fusion.flags_ref
  266.1 41.9 %correlate.1 = bf16[16,36,2,128,128]{4,3,2,1,0:T(8,128)(2,1)} custom-call(s32[1024,1]{1,0:T(8,128)} %copy.12.order_ref, s32[1,1024]{1,0:T(1,128)} %constant.130.ids_ref, f32[1,1024]{1,0:T(1,128)} %add_convert_fusion.flags_ref, bf16[16,16,16,256]{3,2,1,0:T(8,128)(2,1)} %bitcast.121, bf16[16,16,48,256]{3,2,1,0:T(8,128)(2,1)} %bitcast.55.refs_1_), custom_call_target="tpu_custom_call" | custom-call | flops 18253611008 | bytes 46137344 | tf_op jit(solution)/shard_map/correlate/pallas_call | solution.py:261
  307.9 3.8 %all-to-all-done.1 = bf16[256,16,256]{2,1,0:T(8,128)(2,1)S(1)} async-done(((bf16[256,16,256]{2,1,0:T(8,128)(2,1)}), bf16[256,16,256]{2,1,0:T(8,128)(2,1)S(1)}, u32[]{:S(2)}, u32[]{:S(2)}) %all-to-all-start.1) | async-done | bytes 2097184 | tf_op jit(solution)/shard_map/all_to_all | solution.py:367
  311.7 1.4 copy-done
  313.1 9.1 %synthesize.1 = bf16[7232,128]{1,0:T(8,128)(2,1)} custom-call(bf16[16,16,16,256]{3,2,1,0:T(8,128)(2,1)} %bitcast.114, f32[16,256]{1,0:T(8,128)} %constant.127.clone.proto_ref, bf16[512,512]{1,0:T(8,128)(2,1)} %constant.128.clone.table_ref), custom_call_target="tpu_custom_call" | custom-call | flops 1073741824 | bytes 3948544 | tf_op jit(solution)/shard_map/synthesize/pallas_call | solution.py:337
  (79 shorter events, 1.9 us)
Async XLA Ops:
  33.9 6.7 %copy-start.1 = (bf16[256,16,256]{2,1,0:T(8,128)(2,1)S(1)}, bf16[256,16,256]{2,1,0:T(8,128)(2,1)}, u32[]{:S(2)}) copy-start(bf16[256,16,256]{2,1,0:T(8,128)(2,1)} %channelize.2) | copy-start | bytes 6291460
  33.9 200.0 %all-to-all-start = ((bf16[256,48,256]{2,1,0:T(8,128)(2,1)}), bf16[256,48,256]{2,1,0:T(8,128)(2,1)}, u32[]{:S(2)}, u32[]{:S(2)}) async-start(bf16[256,48,256]{2,1,0:T(8,128)(2,1)} %channelize.3), calls=%async_computation | async-start | bytes 12582912 | tf_op jit(solution)/shard_map/all_to_all | solution.py:367
  40.6 6.7 %copy-start.4 = (s32[256,1024]{1,0:T(8,128)S(1)}, s32[256,1024]{1,0:T(8,128)}, u32[]{:S(2)}) copy-start(s32[256,1024]{1,0:T(8,128)} %param.9) | copy-start | bytes 3145732
  41.4 191.1 %collective-permute-start.14 = (bf16[16,16,256]{2,1,0:T(8,128)(2,1)S(1)}, bf16[16,16,256]{2,1,0:T(8,128)(2,1)}, u32[]{:S(2)}, u32[]{:S(2)}) collective-permute-start(bf16[16,16,256]{2,1,0:T(8,128)(2,1)S(1)} %get-tuple-element.6), channel_id=1, source_target_pairs={{0,15},{1,14},{2,13},{3,12},{4,11},{5,10},{6,9},{7,8},{8,7},{9,6},... | collective-permute-start | bytes 393224 | tf_op jit(solution)/shard_map/ppermute | solution.py:380
  42.9 188.7 %collective-permute-start.13 = (bf16[16,16,256]{2,1,0:T(8,128)(2,1)S(1)}, bf16[16,16,256]{2,1,0:T(8,128)(2,1)}, u32[]{:S(2)}, u32[]{:S(2)}) collective-permute-start(bf16[16,16,256]{2,1,0:T(8,128)(2,1)S(1)} %get-tuple-element.7), channel_id=1, source_target_pairs={{0,14},{1,15},{2,12},{3,13},{4,10},{5,11},{6,8},{7,9},{8,6},{9,7},... | collective-permute-start | bytes 393224 | tf_op jit(solution)/shard_map/ppermute | solution.py:380
  44.1 186.6 %collective-permute-start.12 = (bf16[16,16,256]{2,1,0:T(8,128)(2,1)S(1)}, bf16[16,16,256]{2,1,0:T(8,128)(2,1)}, u32[]{:S(2)}, u32[]{:S(2)}) collective-permute-start(bf16[16,16,256]{2,1,0:T(8,128)(2,1)S(1)} %get-tuple-element.8), channel_id=1, source_target_pairs={{0,13},{1,12},{2,15},{3,14},{4,9},{5,8},{6,11},{7,10},{8,5},{9,4},... | collective-permute-start | bytes 393224 | tf_op jit(solution)/shard_map/ppermute | solution.py:380
  45.6 184.2 %collective-permute-start.11 = (bf16[16,16,256]{2,1,0:T(8,128)(2,1)}, bf16[16,16,256]{2,1,0:T(8,128)(2,1)}, u32[]{:S(2)}, u32[]{:S(2)}) collective-permute-start(bf16[16,16,256]{2,1,0:T(8,128)(2,1)} %get-tuple-element.9), channel_id=1, source_target_pairs={{0,12},{1,13},{2,14},{3,15},{4,8},{5,9},{6,10},{7,11},{8,4},{9,5},... | collective-permute-start | bytes 393224 | tf_op jit(solution)/shard_map/ppermute | solution.py:380
  46.8 78.0 %collective-permute-start = (bf16[16,16,256]{2,1,0:T(8,128)(2,1)}, bf16[16,16,256]{2,1,0:T(8,128)(2,1)}, u32[]{:S(2)}, u32[]{:S(2)}) collective-permute-start(bf16[16,16,256]{2,1,0:T(8,128)(2,1)} %get-tuple-element.20), channel_id=1, source_target_pairs={{0,1},{1,0},{2,3},{3,2},{4,5},{5,4},{6,7},{7,6},{8,9},{9,8},{10,11... | collective-permute-start | bytes 393224 | tf_op jit(solution)/shard_map/ppermute | solution.py:380
  47.2 0.7 copy-start.17
  49.4 0.7 copy-start.15
  49.4 0.7 copy-start.18
  117.9 6.9 %copy-start.14 = (bf16[16,16,256]{2,1,0:T(8,128)(2,1)S(1)}, bf16[16,16,256]{2,1,0:T(8,128)(2,1)}, u32[]{:S(2)}) copy-start(bf16[16,16,256]{2,1,0:T(8,128)(2,1)} %get-tuple-element.19) | copy-start | bytes 393220
  117.9 7.3 %copy-start.2 = (bf16[16,16,16,256]{3,2,1,0:T(8,128)(2,1)S(1)}, bf16[16,16,16,256]{3,2,1,0:T(8,128)(2,1)}, u32[]{:S(2)}) copy-start(bf16[16,16,16,256]{3,2,1,0:T(8,128)(2,1)} %get-tuple-element.21) | copy-start | bytes 6291460
  117.9 13.5 %copy-start.13 = (bf16[16,16,256]{2,1,0:T(8,128)(2,1)S(1)}, bf16[16,16,256]{2,1,0:T(8,128)(2,1)}, u32[]{:S(2)}) copy-start(bf16[16,16,256]{2,1,0:T(8,128)(2,1)} %get-tuple-element.18) | copy-start | bytes 393220
  118.0 27.4 %copy-start.12 = (bf16[16,16,256]{2,1,0:T(8,128)(2,1)S(1)}, bf16[16,16,256]{2,1,0:T(8,128)(2,1)}, u32[]{:S(2)}) copy-start(bf16[16,16,256]{2,1,0:T(8,128)(2,1)} %get-tuple-element.17) | copy-start | bytes 393220
  118.0 56.3 %copy-start.11 = (bf16[16,16,256]{2,1,0:T(8,128)(2,1)S(1)}, bf16[16,16,256]{2,1,0:T(8,128)(2,1)}, u32[]{:S(2)}) copy-start(bf16[16,16,256]{2,1,0:T(8,128)(2,1)} %get-tuple-element.16) | copy-start | bytes 393220
  118.0 62.6 %copy-start.10 = (bf16[16,16,256]{2,1,0:T(8,128)(2,1)S(1)}, bf16[16,16,256]{2,1,0:T(8,128)(2,1)}, u32[]{:S(2)}) copy-start(bf16[16,16,256]{2,1,0:T(8,128)(2,1)} %get-tuple-element.15) | copy-start | bytes 393220
  118.0 70.8 %copy-start.9 = (bf16[16,16,256]{2,1,0:T(8,128)(2,1)S(1)}, bf16[16,16,256]{2,1,0:T(8,128)(2,1)}, u32[]{:S(2)}) copy-start(bf16[16,16,256]{2,1,0:T(8,128)(2,1)} %get-tuple-element.14) | copy-start | bytes 393220
  118.0 78.7 %copy-start.8 = (bf16[16,16,256]{2,1,0:T(8,128)(2,1)S(1)}, bf16[16,16,256]{2,1,0:T(8,128)(2,1)}, u32[]{:S(2)}) copy-start(bf16[16,16,256]{2,1,0:T(8,128)(2,1)} %get-tuple-element.13) | copy-start | bytes 393220
  118.0 89.4 %copy-start.7 = (bf16[16,16,256]{2,1,0:T(8,128)(2,1)S(1)}, bf16[16,16,256]{2,1,0:T(8,128)(2,1)}, u32[]{:S(2)}) copy-start(bf16[16,16,256]{2,1,0:T(8,128)(2,1)} %get-tuple-element.12) | copy-start | bytes 393220
  124.8 90.8 %copy-start.6 = (bf16[16,16,256]{2,1,0:T(8,128)(2,1)S(1)}, bf16[16,16,256]{2,1,0:T(8,128)(2,1)}, u32[]{:S(2)}) copy-start(bf16[16,16,256]{2,1,0:T(8,128)(2,1)} %get-tuple-element.11) | copy-start | bytes 393220
  124.8 97.4 %copy-start.5 = (bf16[16,16,256]{2,1,0:T(8,128)(2,1)S(1)}, bf16[16,16,256]{2,1,0:T(8,128)(2,1)}, u32[]{:S(2)}) copy-start(bf16[16,16,256]{2,1,0:T(8,128)(2,1)} %get-tuple-element.10) | copy-start | bytes 393220
  124.8 6.6 %collective-permute-start.1 = (bf16[16,16,256]{2,1,0:T(8,128)(2,1)S(1)}, bf16[16,16,256]{2,1,0:T(8,128)(2,1)S(1)}, u32[]{:S(2)}, u32[]{:S(2)}) collective-permute-start(bf16[16,16,256]{2,1,0:T(8,128)(2,1)S(1)} %copy-done.14), channel_id=1, source_target_pairs={{0,2},{1,3},{2,0},{3,1},{4,6},{5,7},{6,4},{7,5},{8,10},{9,11},{10,... | collective-permute-start | bytes 393224 | tf_op jit(solution)/shard_map/ppermute | solution.py:380
  131.4 13.9 %collective-permute-start.2 = (bf16[16,16,256]{2,1,0:T(8,128)(2,1)S(1)}, bf16[16,16,256]{2,1,0:T(8,128)(2,1)S(1)}, u32[]{:S(2)}, u32[]{:S(2)}) collective-permute-start(bf16[16,16,256]{2,1,0:T(8,128)(2,1)S(1)} %copy-done.13), channel_id=1, source_target_pairs={{0,3},{1,2},{2,1},{3,0},{4,7},{5,6},{6,5},{7,4},{8,11},{9,10},{10,... | collective-permute-start | bytes 393224 | tf_op jit(solution)/shard_map/ppermute | solution.py:380
  145.4 28.9 %collective-permute-start.3 = (bf16[16,16,256]{2,1,0:T(8,128)(2,1)S(1)}, bf16[16,16,256]{2,1,0:T(8,128)(2,1)S(1)}, u32[]{:S(2)}, u32[]{:S(2)}) collective-permute-start(bf16[16,16,256]{2,1,0:T(8,128)(2,1)S(1)} %copy-done.12), channel_id=1, source_target_pairs={{0,4},{1,5},{2,6},{3,7},{4,0},{5,1},{6,2},{7,3},{8,12},{9,13},{10,... | collective-permute-start | bytes 393224 | tf_op jit(solution)/shard_map/ppermute | solution.py:380
  174.2 6.4 %collective-permute-start.4 = (bf16[16,16,256]{2,1,0:T(8,128)(2,1)S(1)}, bf16[16,16,256]{2,1,0:T(8,128)(2,1)S(1)}, u32[]{:S(2)}, u32[]{:S(2)}) collective-permute-start(bf16[16,16,256]{2,1,0:T(8,128)(2,1)S(1)} %copy-done.11), channel_id=1, source_target_pairs={{0,5},{1,4},{2,7},{3,6},{4,1},{5,0},{6,3},{7,2},{8,13},{9,12},{10,... | collective-permute-start | bytes 393224 | tf_op jit(solution)/shard_map/ppermute | solution.py:380
  180.6 8.1 %collective-permute-start.5 = (bf16[16,16,256]{2,1,0:T(8,128)(2,1)S(1)}, bf16[16,16,256]{2,1,0:T(8,128)(2,1)S(1)}, u32[]{:S(2)}, u32[]{:S(2)}) collective-permute-start(bf16[16,16,256]{2,1,0:T(8,128)(2,1)S(1)} %copy-done.10), channel_id=1, source_target_pairs={{0,6},{1,7},{2,4},{3,5},{4,2},{5,3},{6,0},{7,1},{8,14},{9,15},{10,... | collective-permute-start | bytes 393224 | tf_op jit(solution)/shard_map/ppermute | solution.py:380
  188.7 8.0 %collective-permute-start.6 = (bf16[16,16,256]{2,1,0:T(8,128)(2,1)S(1)}, bf16[16,16,256]{2,1,0:T(8,128)(2,1)S(1)}, u32[]{:S(2)}, u32[]{:S(2)}) collective-permute-start(bf16[16,16,256]{2,1,0:T(8,128)(2,1)S(1)} %copy-done.9), channel_id=1, source_target_pairs={{0,7},{1,6},{2,5},{3,4},{4,3},{5,2},{6,1},{7,0},{8,15},{9,14},{10,... | collective-permute-start | bytes 393224 | tf_op jit(solution)/shard_map/ppermute | solution.py:380
  196.7 10.7 %collective-permute-start.7 = (bf16[16,16,256]{2,1,0:T(8,128)(2,1)S(1)}, bf16[16,16,256]{2,1,0:T(8,128)(2,1)S(1)}, u32[]{:S(2)}, u32[]{:S(2)}) collective-permute-start(bf16[16,16,256]{2,1,0:T(8,128)(2,1)S(1)} %copy-done.8), channel_id=1, source_target_pairs={{0,8},{1,9},{2,10},{3,11},{4,12},{5,13},{6,14},{7,15},{8,0},{9,1},... | collective-permute-start | bytes 393224 | tf_op jit(solution)/shard_map/ppermute | solution.py:380
  207.4 8.2 %collective-permute-start.8 = (bf16[16,16,256]{2,1,0:T(8,128)(2,1)S(1)}, bf16[16,16,256]{2,1,0:T(8,128)(2,1)S(1)}, u32[]{:S(2)}, u32[]{:S(2)}) collective-permute-start(bf16[16,16,256]{2,1,0:T(8,128)(2,1)S(1)} %copy-done.7), channel_id=1, source_target_pairs={{0,9},{1,8},{2,11},{3,10},{4,13},{5,12},{6,15},{7,14},{8,1},{9,0},... | collective-permute-start | bytes 393224 | tf_op jit(solution)/shard_map/ppermute | solution.py:380
  215.6 6.6 %collective-permute-start.9 = (bf16[16,16,256]{2,1,0:T(8,128)(2,1)S(1)}, bf16[16,16,256]{2,1,0:T(8,128)(2,1)S(1)}, u32[]{:S(2)}, u32[]{:S(2)}) collective-permute-start(bf16[16,16,256]{2,1,0:T(8,128)(2,1)S(1)} %copy-done.6), channel_id=1, source_target_pairs={{0,10},{1,11},{2,8},{3,9},{4,14},{5,15},{6,12},{7,13},{8,2},{9,3},... | collective-permute-start | bytes 393224 | tf_op jit(solution)/shard_map/ppermute | solution.py:380
  222.2 7.6 %collective-permute-start.10 = (bf16[16,16,256]{2,1,0:T(8,128)(2,1)S(1)}, bf16[16,16,256]{2,1,0:T(8,128)(2,1)S(1)}, u32[]{:S(2)}, u32[]{:S(2)}) collective-permute-start(bf16[16,16,256]{2,1,0:T(8,128)(2,1)S(1)} %copy-done.5), channel_id=1, source_target_pairs={{0,11},{1,10},{2,9},{3,8},{4,15},{5,14},{6,13},{7,12},{8,3},{9,2},... | collective-permute-start | bytes 393224 | tf_op jit(solution)/shard_map/ppermute | solution.py:380
  233.9 1.3 copy-start.3
  247.6 16.8 %copy-start.16 = (s32[1024]{0:T(1024)S(1)}, s32[1024]{0:T(1024)}, u32[]{:S(2)}) copy-start(s32[1024]{0:T(1024)} %param.10) | copy-start | bytes 12292
  247.6 64.1 %all-to-all-start.1 = ((bf16[256,16,256]{2,1,0:T(8,128)(2,1)}), bf16[256,16,256]{2,1,0:T(8,128)(2,1)S(1)}, u32[]{:S(2)}, u32[]{:S(2)}) async-start(bf16[256,16,256]{2,1,0:T(8,128)(2,1)} %form_beams.1), calls=%async_computation.1 | async-start | bytes 4194304 | tf_op jit(solution)/shard_map/all_to_all | solution.py:367
  311.7 1.4 copy-start

commit v4 on v3

--- a/solution.py
+++ b/solution.py
@@ -15,7 +15,6 @@
 TILE_ANTENNAS = 128
 CHUNK_ANTENNAS = 16
 FILTER_ANTENNAS = 8
-BEAM_CHANNELS = 4
 LANES = 128
 VMEM_BYTES = 60 * 1024 * 1024
 
@@ -143,34 +142,97 @@
     )(flat, proto, table)
 
 
+def weights_kernel(start_cos, start_sin, turn_cos, turn_sin, keep_ref, out_ref, cosine, sine):
+    local, double_beams, _ = out_ref.shape
+    beams = double_beams // 2
+    rows = 8 if beams % 8 == 0 else beams
+    cosine[...] = start_cos[...]
+    sine[...] = start_sin[...]
+
+    def channel(c, carry):
+        def strip(i, inner):
+            here = pl.ds(pl.multiple_of(i * 2 * rows, 2 * rows), 2 * rows)
+            there = pl.ds(pl.multiple_of(i * 2 * rows + beams, 2 * rows), 2 * rows)
+            co, si = cosine[here, :], sine[here, :]
+            tc, ts = turn_cos[here, :], turn_sin[here, :]
+            out_ref[c, here, :] = (co * keep_ref[...]).astype(jnp.bfloat16)
+            out_ref[c, there, :] = (si * keep_ref[...]).astype(jnp.bfloat16)
+            cosine[here, :] = co * tc - si * ts
+            sine[here, :] = si * tc + co * ts
+            return inner
+
+        return lax.fori_loop(0, beams // (2 * rows), strip, carry)
+
+    lax.fori_loop(0, local, channel, 0)
+
+
+def make_weights(delays, keep, first_channel, local, chans):
+    beams, antennas = delays.shape
+    step = 2.0 * math.pi / chans
+    start = (delays * first_channel % chans).astype(jnp.float32) * step
+    turns = delays.astype(jnp.float32) * step
+    vmem = pl.BlockSpec(memory_space=pltpu.VMEM)
+    return pl.pallas_call(
+        weights_kernel,
+        in_specs=[vmem] * 5,
+        out_specs=vmem,
+        out_shape=jax.ShapeDtypeStruct((local, 2 * beams, antennas), jnp.bfloat16),
+        scratch_shapes=[pltpu.VMEM((beams, antennas), jnp.float32)] * 2,
+        compiler_params=pltpu.CompilerParams(vmem_limit_bytes=40 * 1024 * 1024),
+        cost_estimate=pl.CostEstimate(
+            flops=10 * local * beams * antennas,
+            bytes_accessed=4 * 4 * beams * antennas + 4 * local * beams * antennas,
+            transcendentals=0,
+        ),
+        name="make_weights",
+    )(jnp.cos(start), jnp.sin(start), jnp.cos(turns), jnp.sin(turns), keep)
+
+
 def beam_kernel(counts, *refs):
-    x_refs = refs[: len(counts)]
-    weights_ref, out_ref, turned = refs[len(counts) :]
-    step = pl.program_id(0)
+    kinds = len(counts) + 1
+    sources, (out_ref, turned), holds, sems = (
+        refs[:kinds], refs[kinds : kinds + 2], refs[kinds + 2 : -1], refs[-1]
+    )
     beams, local, columns = out_ref.shape
     spectra = columns // 2
-    group = weights_ref.shape[0]
-    for member in range(group):
+
+    def copies(channel):
+        views = [x.at[:, channel] for x in sources[:-1]] + [sources[-1].at[channel]]
+        return [
+            pltpu.make_async_copy(view, hold.at[channel], sems.at[kind, channel])
+            for kind, (view, hold) in enumerate(zip(views, holds))
+        ]
+
+    def begin(channel, carry):
+        for copy in copies(channel):
+            copy.start()
+        return carry
+
+    lax.fori_loop(0, local, begin, 0)
+
+    def form(channel, carry):
+        for copy in copies(channel):
+            copy.wait()
         product = None
         start = 0
-        for x_ref, count in zip(x_refs, counts):
+        for hold, count in zip(holds, counts):
             term = jnp.dot(
-                weights_ref[member, :, start : start + count],
-                x_ref[:, member].reshape(count, columns),
+                holds[-1][channel, :, start : start + count],
+                hold[channel].reshape(count, columns),
                 preferred_element_type=jnp.float32,
             )
             product = term if product is None else product + term
             start += count
-        rows = pl.ds(step * group + member, beams, stride=local)
+        rows = pl.ds(channel, beams, stride=local)
         turned[0, rows, :] = product[:beams, :spectra] + product[beams:, spectra:]
         turned[1, rows, :] = product[:beams, spectra:] - product[beams:, :spectra]
-
-    @pl.when(step == pl.num_programs(0) - 1)
-    def _():
-        for part in range(2):
-            out_ref[:, :, part * spectra : (part + 1) * spectra] = (
-                turned[part].reshape(beams, local, spectra).astype(jnp.bfloat16)
-            )
+        return carry
+
+    lax.fori_loop(0, local, form, 0)
+    for part in range(2):
+        out_ref[:, :, part * spectra : (part + 1) * spectra] = (
+            turned[part].reshape(beams, local, spectra).astype(jnp.bfloat16)
+        )
 
 
 def form_beams(blocks, weights):
@@ -178,18 +240,17 @@
     beams = double_beams // 2
     columns = blocks[0].shape[3]
     counts = tuple(x.shape[0] * x.shape[2] for x in blocks)
-    group = BEAM_CHANNELS if local % BEAM_CHANNELS == 0 else 1
     return pl.pallas_call(
         functools.partial(beam_kernel, counts),
-        grid=(local // group,),
-        in_specs=[
-            pl.BlockSpec((x.shape[0], group, x.shape[2], columns), lambda c: (0, c, 0, 0))
-            for x in blocks
-        ]
-        + [pl.BlockSpec((group, double_beams, antennas), lambda c: (c, 0, 0))],
-        out_specs=pl.BlockSpec((beams, local, columns), lambda c: (0, 0, 0)),
+        in_specs=[pl.BlockSpec(memory_space=pl.ANY)] * (len(blocks) + 1),
+        out_specs=pl.BlockSpec(memory_space=pltpu.VMEM),
         out_shape=jax.ShapeDtypeStruct((beams, local, columns), jnp.bfloat16),
-        scratch_shapes=[pltpu.VMEM((2, beams * local, columns // 2), jnp.float32)],
+        scratch_shapes=[pltpu.VMEM((2, beams * local, columns // 2), jnp.float32)]
+        + [pltpu.VMEM((local, x.shape[0], x.shape[2], columns), jnp.bfloat16) for x in blocks]
+        + [
+            pltpu.VMEM((local, double_beams, antennas), jnp.bfloat16),
+            pltpu.SemaphoreType.DMA((len(blocks) + 1, local)),
+        ],
         compiler_params=pltpu.CompilerParams(vmem_limit_bytes=VMEM_BYTES),
         cost_estimate=pl.CostEstimate(
             flops=2 * local * double_beams * antennas * columns,
@@ -292,14 +353,16 @@
 
 
 def synthesize_kernel(beams_ref, proto_ref, table_ref, out_ref, zeta, planes):
-    sources, group, local, columns = beams_ref.shape
+    sources, _, local, columns = beams_ref.shape
     chans = sources * local
     spectra = columns // 2
     lane_tiles = chans // LANES
     words = 2 * lane_tiles
-    out_frames = planes.shape[0] // (group * words)
+    out_frames = spectra - TAPS + 1
+    group = planes.shape[0] // (out_frames * words)
+    first_beam = pl.program_id(0) * group
     for member in range(group):
-        rows = beams_ref[:, member].reshape(chans, columns)
+        rows = beams_ref[:, first_beam + member].reshape(chans, columns)
         for part in range(2):
             cols = slice(part * chans, (part + 1) * chans)
             value = None
@@ -338,7 +401,7 @@
         synthesize_kernel,
         grid=(beams // group,),
         in_specs=[
-            pl.BlockSpec((sources, group, local, columns), lambda b: (0, b, 0, 0)),
+            pl.BlockSpec(memory_space=pltpu.VMEM),
             pl.BlockSpec((TAPS, chans), lambda b: (0, 0)),
             pl.BlockSpec((2 * chans, 2 * chans), lambda b: (0, 0)),
         ],
@@ -348,14 +411,14 @@
             pltpu.VMEM((spectra, LANES), jnp.float32),
             pltpu.VMEM((group * rows, LANES), jnp.float32),
         ],
-        compiler_params=pltpu.CompilerParams(vmem_limit_bytes=VMEM_BYTES),
+        compiler_params=pltpu.CompilerParams(vmem_limit_bytes=32 * 1024 * 1024),
         cost_estimate=pl.CostEstimate(
             flops=2 * beams * spectra * 4 * chans * chans,
             bytes_accessed=2 * beams * (columns + 2 * out_frames) * chans,
             transcendentals=0,
         ),
         name="synthesize",
-    )(arranged, proto, table)
+    )(pltpu.with_memory_space_constraint(arranged, pltpu.VMEM), proto, table)
     return (
         flat.reshape(beams, out_frames, lane_tiles, 2, LANES)
         .transpose(0, 3, 1, 2, 4)
@@ -434,18 +497,9 @@
         return jnp.concatenate(pieces, axis=-1)
 
     flag_row = arrange(flags).astype(jnp.float32)
-    channel_ids = lax.axis_index("chan") * local_channels + jnp.arange(
-        local_channels, dtype=jnp.int32
-    )
-    phase = arrange(delays)[None, :, :] * channel_ids[:, None, None] % chans
-    angle = phase.astype(jnp.float32) * (2.0 * math.pi / chans)
-    keep = flag_row[None, None, :] * (1.0 / math.sqrt(antennas))
-    weights = jnp.concatenate(
-        [
-            jnp.cos(angle).astype(jnp.bfloat16) * keep.astype(jnp.bfloat16),
-            jnp.sin(angle).astype(jnp.bfloat16) * keep.astype(jnp.bfloat16),
-        ],
-        axis=1,
+    keep = flag_row[None, :] * (1.0 / math.sqrt(antennas))
+    weights = make_weights(
+        arrange(delays), keep, lax.axis_index("chan") * local_channels, local_channels, chans
     )
     beams = form_beams(blocks, weights)
     arranged = turn(beams)

time: 323 us -> 313 us (0.969)
  other arithmetic: 75.3 us -> 10.1 us
  waiting for transfers between devices: 85.9 us -> 125 us
  Pallas kernels: 96.7 us -> 108 us
  starting transfers between devices: 49.8 us -> 55.8 us
    mul x1, other arithmetic: 67.8 us -> 0.59 us  [per_device(): keep = flag_row[None, :] * (1.0 / math.sqrt(antennas))]
    ppermute x15, waiting for transfers between devices: 82.1 us -> 120 us  [send(): return lax.ppermute(mine, 'chan', [(i, i ^ mask) for i in range(devices)])]
    ppermute x15, starting transfers between devices: 26.5 us -> 40.1 us  [send(): return lax.ppermute(mine, 'chan', [(i, i ^ mask) for i in range(devices)])]
    pallas_call x1 -> x2, Pallas kernels: 12.4 us -> 25.1 us  [the longest x1 13.2 us: make_weights(): pl.pallas_call(weights_kernel, in_specs=[vmem] * 5, out_specs=vmem, out_s...]
    sin x0 -> x1, other arithmetic: none -> 9.51 us  [make_weights(): jnp.sin(turns)]
    all_to_all x2, starting transfers between devices: 23.3 us -> 15.7 us  [turn(): return lax.all_to_all(part, 'chan', split_axis=0, concat_axis=0, tiled=True)]
    concatenate x2 -> x0, other arithmetic: 6.88 us -> none  [the longest x1 6.81 us: per_device(): jnp.concatenate([jnp.cos(angle).astype(jnp.bfloat16) * keep.astype(jnp.bf...]
  transfers between devices with their start and end apart: 17 -> 17, of which waited for: 11 -> 11; matrix products, arithmetic and copies ran while one was open for 27% -> 6% of each run, Pallas kernels for 13% -> 18%
where the time goes in v4:
time: 313 us
  waiting for transfers between devices  125 us (40%)
  Pallas kernels  108 us (35%)
  starting transfers between devices  55.8 us (18%)
  local copies, waits for them, and re-layouts  12.5 us (4%)
  other arithmetic  10.1 us (3%)
    ppermute x15, waiting for transfers between devices, send(): return lax.ppermute(mine, 'chan', [(i, i ^ mask) for i in range(devices)])  120 us
    pallas_call x1, Pallas kernels, correlate(): pl.pallas_call(functools.partial(visibility_kernel, counts), grid=(local,...  41.9 us
    ppermute x15, starting transfers between devices, send(): return lax.ppermute(mine, 'chan', [(i, i ^ mask) for i in range(devices)])  40.1 us
    pallas_call x2, Pallas kernels, channelize(): pl.pallas_call(channelize_kernel, grid=(count // block,), in_specs=[pl.Bl...  33.2 us
    all_to_all x2, starting transfers between devices, turn(): return lax.all_to_all(part, 'chan', split_axis=0, concat_axis=0, tiled=True)  15.7 us
    pallas_call x1, Pallas kernels, make_weights(): pl.pallas_call(weights_kernel, in_specs=[vmem] * 5, out_specs=vmem, out_s...  13.2 us
    pallas_call x1, Pallas kernels, form_beams(): pl.pallas_call(functools.partial(beam_kernel, counts), in_specs=[pl.Block...  11.8 us
    sin x1, other arithmetic, make_weights(): jnp.sin(turns)  9.51 us
  transfers between devices with their start and end apart: 17, of which 11 were waited for; matrix products, arithmetic and copies ran while one was open for 6% of the time, Pallas kernels for 18%

profile of v4, /device:TPU:15, one launch (start us, length us, event | category | flops | bytes accessed | tf_op | source)
XLA Modules:
  0.0 312.5 jit_solution(14877566922964526902)
XLA Ops:
  0.6 9.5 %channelize.2 = bf16[256,16,256]{2,1,0:T(8,128)(2,1)} custom-call(bf16[36608,128]{1,0:T(8,128)(2,1)} %bitcast.113, f32[16,256]{1,0:T(8,128)} %constant.127.clone.proto_ref, bf16[512,512]{1,0:T(8,128)(2,1)} %constant.128.clone.table_ref), custom_call_target="tpu_custom_call" | custom-call | flops 2147483648 | bytes 4440064 | tf_op jit(solution)/shard_map/channelize/pallas_call | solution.py:120
  10.1 23.8 %channelize.3 = bf16[256,48,256]{2,1,0:T(8,128)(2,1)} custom-call(bf16[36608,128]{1,0:T(8,128)(2,1)} %bitcast.114, f32[16,256]{1,0:T(8,128)} %constant.127.clone.proto_ref, bf16[512,512]{1,0:T(8,128)(2,1)} %constant.128.clone.table_ref), custom_call_target="tpu_custom_call" | custom-call | flops 6442450944 | bytes 13320192 | tf_op jit(solution)/shard_map/channelize/pallas_call | solution.py:120
  33.9 6.6 %all-to-all-start = ((bf16[256,48,256]{2,1,0:T(8,128)(2,1)}), bf16[256,48,256]{2,1,0:T(8,128)(2,1)}, u32[]{:S(2)}, u32[]{:S(2)}) async-start(bf16[256,48,256]{2,1,0:T(8,128)(2,1)} %channelize.3), calls=%async_computation | async-start | bytes 12582912 | tf_op jit(solution)/shard_map/all_to_all | solution.py:430
  40.5 1.0 dynamic-slice_bitcast_fusion
  41.5 1.5 collective-permute-start.14
  43.0 1.2 collective-permute-start.13
  44.2 1.5 collective-permute-start.12
  45.6 0.3 collective-permute-start.11
  45.9 1.0 dynamic-slice_bitcast_fusion.8
  46.9 0.4 collective-permute-start
  47.3 0.3 copy.13
  47.8 1.1 copy.15
  48.9 0.1 copy.14
  49.0 9.5 %fusion.3 = (f32[256,1024]{1,0:T(8,128)S(1)}, f32[256,1024]{1,0:T(8,128)S(1)}, f32[256,1024]{1,0:T(8,128)S(1)}, f32[256,1024]{1,0:T(8,128)}) fusion(s32[256,768]{1,0:T(8,128)} %copy.15, s32[256,256]{1,0:T(8,128)S(1)} %copy.14, s32[]{:T(128)S(6)} %mul.21), kind=kLoop, calls=%fused_computation.8 | loop fusion | flops 4456448 | bytes 5242884 | tf_op jit(solution)/shard_map/sin | solution.py:188
  58.9 0.6 broadcast_multiply_fusion
  59.5 1.2 copy-done
  60.8 13.2 %make_weights.1.refs_2_ = bf16[16,512,1024]{2,1,0:T(8,128)(2,1)} custom-call(f32[256,1024]{1,0:T(8,128)S(1)} %copy-done, f32[256,1024]{1,0:T(8,128)S(1)} %get-tuple-element.25.start_sin, f32[256,1024]{1,0:T(8,128)S(1)} %get-tuple-element.26.turn_cos, f32[256,1024]{1,0:T(8,128)S(1)} %get-tuple-element.24.turn_sin, f32[1,1024]{1,0:T(1,128)S(1)} %get-tuple-element.6.keep_ref), custom_call_target="tpu_custom_call" | custom-call | flops 41943040 | bytes 20971520 | tf_op jit(solution)/shard_map/make_weights/pallas_call | solution.py:175
  74.0 0.3 collective-permute-start.1
  74.4 0.9 bitcast_dynamic-update-slice_fusion.30
  75.3 5.4 %collective-permute-done.1 = bf16[16,16,256]{2,1,0:T(8,128)(2,1)S(1)} collective-permute-done((bf16[16,16,256]{2,1,0:T(8,128)(2,1)S(1)}, bf16[16,16,256]{2,1,0:T(8,128)(2,1)S(1)}, u32[]{:S(2)}, u32[]{:S(2)}) %collective-permute-start.1) | collective-permute-done | bytes 131104 | tf_op jit(solution)/shard_map/ppermute | solution.py:443
  80.7 5.6 %collective-permute-done.2 = bf16[16,16,256]{2,1,0:T(8,128)(2,1)S(1)} collective-permute-done((bf16[16,16,256]{2,1,0:T(8,128)(2,1)S(1)}, bf16[16,16,256]{2,1,0:T(8,128)(2,1)S(1)}, u32[]{:S(2)}, u32[]{:S(2)}) %collective-permute-start.2) | collective-permute-done | bytes 131104 | tf_op jit(solution)/shard_map/ppermute | solution.py:443
  86.3 11.1 %collective-permute-start.3 = (bf16[16,16,256]{2,1,0:T(8,128)(2,1)S(1)}, bf16[16,16,256]{2,1,0:T(8,128)(2,1)S(1)}, u32[]{:S(2)}, u32[]{:S(2)}) collective-permute-start(bf16[16,16,256]{2,1,0:T(8,128)(2,1)S(1)} %copy-done.14), channel_id=1, source_target_pairs={{0,4},{1,5},{2,6},{3,7},{4,0},{5,1},{6,2},{7,3},{8,12},{9,13},{10,... | collective-permute-start | bytes 393224 | tf_op jit(solution)/shard_map/ppermute | solution.py:443
  97.5 60.6 %collective-permute-done.3 = bf16[16,16,256]{2,1,0:T(8,128)(2,1)S(1)} collective-permute-done((bf16[16,16,256]{2,1,0:T(8,128)(2,1)S(1)}, bf16[16,16,256]{2,1,0:T(8,128)(2,1)S(1)}, u32[]{:S(2)}, u32[]{:S(2)}) %collective-permute-start.3) | collective-permute-done | bytes 131104 | tf_op jit(solution)/shard_map/ppermute | solution.py:443
  158.0 0.1 collective-permute-start.4
  158.2 16.0 %collective-permute-done.4 = bf16[16,16,256]{2,1,0:T(8,128)(2,1)S(1)} collective-permute-done((bf16[16,16,256]{2,1,0:T(8,128)(2,1)S(1)}, bf16[16,16,256]{2,1,0:T(8,128)(2,1)S(1)}, u32[]{:S(2)}, u32[]{:S(2)}) %collective-permute-start.4) | collective-permute-done | bytes 131104 | tf_op jit(solution)/shard_map/ppermute | solution.py:443
  174.2 2.3 collective-permute-start.5
  176.5 3.2 %collective-permute-done.5 = bf16[16,16,256]{2,1,0:T(8,128)(2,1)S(1)} collective-permute-done((bf16[16,16,256]{2,1,0:T(8,128)(2,1)S(1)}, bf16[16,16,256]{2,1,0:T(8,128)(2,1)S(1)}, u32[]{:S(2)}, u32[]{:S(2)}) %collective-permute-start.5) | collective-permute-done | bytes 131104 | tf_op jit(solution)/shard_map/ppermute | solution.py:443
  179.7 3.5 %collective-permute-start.6 = (bf16[16,16,256]{2,1,0:T(8,128)(2,1)S(1)}, bf16[16,16,256]{2,1,0:T(8,128)(2,1)S(1)}, u32[]{:S(2)}, u32[]{:S(2)}) collective-permute-start(bf16[16,16,256]{2,1,0:T(8,128)(2,1)S(1)} %copy-done.11), channel_id=1, source_target_pairs={{0,7},{1,6},{2,5},{3,4},{4,3},{5,2},{6,1},{7,0},{8,15},{9,14},{10,... | collective-permute-start | bytes 393224 | tf_op jit(solution)/shard_map/ppermute | solution.py:443
  183.2 6.7 %collective-permute-done.6 = bf16[16,16,256]{2,1,0:T(8,128)(2,1)S(1)} collective-permute-done((bf16[16,16,256]{2,1,0:T(8,128)(2,1)S(1)}, bf16[16,16,256]{2,1,0:T(8,128)(2,1)S(1)}, u32[]{:S(2)}, u32[]{:S(2)}) %collective-permute-start.6) | collective-permute-done | bytes 131104 | tf_op jit(solution)/shard_map/ppermute | solution.py:443
  189.9 4.3 %collective-permute-start.7 = (bf16[16,16,256]{2,1,0:T(8,128)(2,1)S(1)}, bf16[16,16,256]{2,1,0:T(8,128)(2,1)S(1)}, u32[]{:S(2)}, u32[]{:S(2)}) collective-permute-start(bf16[16,16,256]{2,1,0:T(8,128)(2,1)S(1)} %copy-done.10), channel_id=1, source_target_pairs={{0,8},{1,9},{2,10},{3,11},{4,12},{5,13},{6,14},{7,15},{8,0},{9,1},... | collective-permute-start | bytes 393224 | tf_op jit(solution)/shard_map/ppermute | solution.py:443
  194.2 9.5 %collective-permute-done.7 = bf16[16,16,256]{2,1,0:T(8,128)(2,1)S(1)} collective-permute-done((bf16[16,16,256]{2,1,0:T(8,128)(2,1)S(1)}, bf16[16,16,256]{2,1,0:T(8,128)(2,1)S(1)}, u32[]{:S(2)}, u32[]{:S(2)}) %collective-permute-start.7) | collective-permute-done | bytes 131104 | tf_op jit(solution)/shard_map/ppermute | solution.py:443
  203.7 4.0 %collective-permute-start.8 = (bf16[16,16,256]{2,1,0:T(8,128)(2,1)S(1)}, bf16[16,16,256]{2,1,0:T(8,128)(2,1)S(1)}, u32[]{:S(2)}, u32[]{:S(2)}) collective-permute-start(bf16[16,16,256]{2,1,0:T(8,128)(2,1)S(1)} %copy-done.9), channel_id=1, source_target_pairs={{0,9},{1,8},{2,11},{3,10},{4,13},{5,12},{6,15},{7,14},{8,1},{9,0},... | collective-permute-start | bytes 393224 | tf_op jit(solution)/shard_map/ppermute | solution.py:443
  207.6 5.8 %collective-permute-done.8 = bf16[16,16,256]{2,1,0:T(8,128)(2,1)S(1)} collective-permute-done((bf16[16,16,256]{2,1,0:T(8,128)(2,1)S(1)}, bf16[16,16,256]{2,1,0:T(8,128)(2,1)S(1)}, u32[]{:S(2)}, u32[]{:S(2)}) %collective-permute-start.8) | collective-permute-done | bytes 131104 | tf_op jit(solution)/shard_map/ppermute | solution.py:443
  213.5 5.2 %collective-permute-start.9 = (bf16[16,16,256]{2,1,0:T(8,128)(2,1)S(1)}, bf16[16,16,256]{2,1,0:T(8,128)(2,1)S(1)}, u32[]{:S(2)}, u32[]{:S(2)}) collective-permute-start(bf16[16,16,256]{2,1,0:T(8,128)(2,1)S(1)} %copy-done.8), channel_id=1, source_target_pairs={{0,10},{1,11},{2,8},{3,9},{4,14},{5,15},{6,12},{7,13},{8,2},{9,3},... | collective-permute-start | bytes 393224 | tf_op jit(solution)/shard_map/ppermute | solution.py:443
  218.7 3.5 %collective-permute-done.9 = bf16[16,16,256]{2,1,0:T(8,128)(2,1)S(1)} collective-permute-done((bf16[16,16,256]{2,1,0:T(8,128)(2,1)S(1)}, bf16[16,16,256]{2,1,0:T(8,128)(2,1)S(1)}, u32[]{:S(2)}, u32[]{:S(2)}) %collective-permute-start.9) | collective-permute-done | bytes 131104 | tf_op jit(solution)/shard_map/ppermute | solution.py:443
  222.2 4.5 %collective-permute-start.10 = (bf16[16,16,256]{2,1,0:T(8,128)(2,1)S(1)}, bf16[16,16,256]{2,1,0:T(8,128)(2,1)S(1)}, u32[]{:S(2)}, u32[]{:S(2)}) collective-permute-start(bf16[16,16,256]{2,1,0:T(8,128)(2,1)S(1)} %copy-done.7), channel_id=1, source_target_pairs={{0,11},{1,10},{2,9},{3,8},{4,15},{5,14},{6,13},{7,12},{8,3},{9,2},... | collective-permute-start | bytes 393224 | tf_op jit(solution)/shard_map/ppermute | solution.py:443
  226.7 4.2 %collective-permute-done.10 = bf16[16,16,256]{2,1,0:T(8,128)(2,1)S(1)} collective-permute-done((bf16[16,16,256]{2,1,0:T(8,128)(2,1)S(1)}, bf16[16,16,256]{2,1,0:T(8,128)(2,1)S(1)}, u32[]{:S(2)}, u32[]{:S(2)}) %collective-permute-start.10) | collective-permute-done | bytes 131104 | tf_op jit(solution)/shard_map/ppermute | solution.py:443
  230.9 0.9 bitcast_dynamic-update-slice_fusion.19
  231.8 0.9 bitcast_dynamic-update-slice_fusion.18
  232.7 0.9 bitcast_dynamic-update-slice_fusion.17
  233.6 0.9 bitcast_dynamic-update-slice_fusion.16
  235.0 1.3 copy-done.5
  236.3 11.8 %form_beams.1 = bf16[256,16,256]{2,1,0:T(8,128)(2,1)} custom-call(bf16[16,16,16,256]{3,2,1,0:T(8,128)(2,1)} %bitcast.120, bf16[16,16,48,256]{3,2,1,0:T(8,128)(2,1)} %bitcast.55.refs_1_, bf16[16,512,1024]{2,1,0:T(8,128)(2,1)} %make_weights.1.refs_2_), custom_call_target="tpu_custom_call" | custom-call | flops 4294967296 | bytes 27262976 | tf_op jit(solution)/shard_map/form_beams/pallas_call | solution.py:243
  248.1 9.1 %all-to-all-start.1 = ((bf16[256,16,256]{2,1,0:T(8,128)(2,1)}), bf16[256,16,256]{2,1,0:T(8,128)(2,1)S(1)}, u32[]{:S(2)}, u32[]{:S(2)}) async-start(bf16[256,16,256]{2,1,0:T(8,128)(2,1)} %form_beams.1), calls=%async_computation.1 | async-start | bytes 4194304 | tf_op jit(solution)/shard_map/all_to_all | solution.py:430
  257.2 1.0 copy.12.order_ref
  258.3 41.9 %correlate.1 = bf16[16,36,2,128,128]{4,3,2,1,0:T(8,128)(2,1)} custom-call(s32[1024,1]{1,0:T(8,128)} %copy.12.order_ref, s32[1,1024]{1,0:T(1,128)} %constant.130.ids_ref, f32[1,1024]{1,0:T(1,128)} %get-tuple-element.7.flags_ref, bf16[16,16,16,256]{3,2,1,0:T(8,128)(2,1)} %bitcast.121, bf16[16,16,48,256]{3,2,1,0:T(8,128)(2,1)} %bitcast.55.refs_1_), custom_call_target="tpu_custom_call" | custom-call | flops 18253611008 | bytes 46137344 | tf_op jit(solution)/shard_map/correlate/pallas_call | solution.py:322
  300.2 4.5 %all-to-all-done.1 = bf16[256,16,256]{2,1,0:T(8,128)(2,1)S(1)} async-done(((bf16[256,16,256]{2,1,0:T(8,128)(2,1)}), bf16[256,16,256]{2,1,0:T(8,128)(2,1)S(1)}, u32[]{:S(2)}, u32[]{:S(2)}) %all-to-all-start.1) | async-done | bytes 2097184 | tf_op jit(solution)/shard_map/all_to_all | solution.py:430
  304.7 7.9 %synthesize.1 = bf16[7232,128]{1,0:T(8,128)(2,1)} custom-call(bf16[16,16,16,256]{3,2,1,0:T(8,128)(2,1)S(1)} %bitcast.112, f32[16,256]{1,0:T(8,128)S(1)} %copy-done.2, bf16[512,512]{1,0:T(8,128)(2,1)S(1)} %copy-done.1), custom_call_target="tpu_custom_call" | custom-call | flops 1073741824 | bytes 3948544 | tf_op jit(solution)/shard_map/synthesize/pallas_call | solution.py:400
  (75 shorter events, 0.9 us)
Async XLA Ops:
  33.9 6.7 %copy-start.3 = (bf16[256,16,256]{2,1,0:T(8,128)(2,1)S(1)}, bf16[256,16,256]{2,1,0:T(8,128)(2,1)}, u32[]{:S(2)}) copy-start(bf16[256,16,256]{2,1,0:T(8,128)(2,1)} %channelize.2) | copy-start | bytes 6291460
  33.9 201.1 %all-to-all-start = ((bf16[256,48,256]{2,1,0:T(8,128)(2,1)}), bf16[256,48,256]{2,1,0:T(8,128)(2,1)}, u32[]{:S(2)}, u32[]{:S(2)}) async-start(bf16[256,48,256]{2,1,0:T(8,128)(2,1)} %channelize.3), calls=%async_computation | async-start | bytes 12582912 | tf_op jit(solution)/shard_map/all_to_all | solution.py:430
  40.5 6.8 %copy-start.6 = (s32[256,1024]{1,0:T(8,128)S(1)}, s32[256,1024]{1,0:T(8,128)}, u32[]{:S(2)}) copy-start(s32[256,1024]{1,0:T(8,128)} %param.9) | copy-start | bytes 3145732
  41.5 192.1 %collective-permute-start.14 = (bf16[16,16,256]{2,1,0:T(8,128)(2,1)S(1)}, bf16[16,16,256]{2,1,0:T(8,128)(2,1)}, u32[]{:S(2)}, u32[]{:S(2)}) collective-permute-start(bf16[16,16,256]{2,1,0:T(8,128)(2,1)S(1)} %get-tuple-element.8), channel_id=1, source_target_pairs={{0,15},{1,14},{2,13},{3,12},{4,11},{5,10},{6,9},{7,8},{8,7},{9,6},... | collective-permute-start | bytes 393224 | tf_op jit(solution)/shard_map/ppermute | solution.py:443
  43.0 189.7 %collective-permute-start.13 = (bf16[16,16,256]{2,1,0:T(8,128)(2,1)}, bf16[16,16,256]{2,1,0:T(8,128)(2,1)}, u32[]{:S(2)}, u32[]{:S(2)}) collective-permute-start(bf16[16,16,256]{2,1,0:T(8,128)(2,1)} %get-tuple-element.9), channel_id=1, source_target_pairs={{0,14},{1,15},{2,12},{3,13},{4,10},{5,11},{6,8},{7,9},{8,6},{9,7},... | collective-permute-start | bytes 393224 | tf_op jit(solution)/shard_map/ppermute | solution.py:443
  44.2 187.6 %collective-permute-start.12 = (bf16[16,16,256]{2,1,0:T(8,128)(2,1)}, bf16[16,16,256]{2,1,0:T(8,128)(2,1)}, u32[]{:S(2)}, u32[]{:S(2)}) collective-permute-start(bf16[16,16,256]{2,1,0:T(8,128)(2,1)} %get-tuple-element.10), channel_id=1, source_target_pairs={{0,13},{1,12},{2,15},{3,14},{4,9},{5,8},{6,11},{7,10},{8,5},{9,4},... | collective-permute-start | bytes 393224 | tf_op jit(solution)/shard_map/ppermute | solution.py:443
  45.6 185.2 %collective-permute-start.11 = (bf16[16,16,256]{2,1,0:T(8,128)(2,1)}, bf16[16,16,256]{2,1,0:T(8,128)(2,1)}, u32[]{:S(2)}, u32[]{:S(2)}) collective-permute-start(bf16[16,16,256]{2,1,0:T(8,128)(2,1)} %get-tuple-element.11), channel_id=1, source_target_pairs={{0,12},{1,13},{2,14},{3,15},{4,8},{5,9},{6,10},{7,11},{8,4},{9,5},... | collective-permute-start | bytes 393224 | tf_op jit(solution)/shard_map/ppermute | solution.py:443
  46.9 27.1 %collective-permute-start = (bf16[16,16,256]{2,1,0:T(8,128)(2,1)}, bf16[16,16,256]{2,1,0:T(8,128)(2,1)}, u32[]{:S(2)}, u32[]{:S(2)}) collective-permute-start(bf16[16,16,256]{2,1,0:T(8,128)(2,1)} %get-tuple-element.22), channel_id=1, source_target_pairs={{0,1},{1,0},{2,3},{3,2},{4,5},{5,4},{6,7},{7,6},{8,9},{9,8},{10,11... | collective-permute-start | bytes 393224 | tf_op jit(solution)/shard_map/ppermute | solution.py:443
  49.0 9.5 %copy-start.18 = (s32[1024]{0:T(1024)S(1)}, s32[1024]{0:T(1024)}, u32[]{:S(2)}) copy-start(s32[1024]{0:T(1024)} %param.8) | copy-start | bytes 12292
  59.5 1.2 copy-start
  60.7 13.3 %copy-start.16 = (bf16[16,16,256]{2,1,0:T(8,128)(2,1)S(1)}, bf16[16,16,256]{2,1,0:T(8,128)(2,1)}, u32[]{:S(2)}) copy-start(bf16[16,16,256]{2,1,0:T(8,128)(2,1)} %get-tuple-element.21) | copy-start | bytes 393220
  60.7 13.7 %copy-start.4 = (bf16[16,16,16,256]{3,2,1,0:T(8,128)(2,1)S(1)}, bf16[16,16,16,256]{3,2,1,0:T(8,128)(2,1)}, u32[]{:S(2)}) copy-start(bf16[16,16,16,256]{3,2,1,0:T(8,128)(2,1)} %get-tuple-element.23) | copy-start | bytes 6291460
  60.7 20.0 %copy-start.15 = (bf16[16,16,256]{2,1,0:T(8,128)(2,1)S(1)}, bf16[16,16,256]{2,1,0:T(8,128)(2,1)}, u32[]{:S(2)}) copy-start(bf16[16,16,256]{2,1,0:T(8,128)(2,1)} %get-tuple-element.20) | copy-start | bytes 393220
  60.7 25.6 %copy-start.14 = (bf16[16,16,256]{2,1,0:T(8,128)(2,1)S(1)}, bf16[16,16,256]{2,1,0:T(8,128)(2,1)}, u32[]{:S(2)}) copy-start(bf16[16,16,256]{2,1,0:T(8,128)(2,1)} %get-tuple-element.19) | copy-start | bytes 393220
  60.7 97.3 %copy-start.13 = (bf16[16,16,256]{2,1,0:T(8,128)(2,1)S(1)}, bf16[16,16,256]{2,1,0:T(8,128)(2,1)}, u32[]{:S(2)}) copy-start(bf16[16,16,256]{2,1,0:T(8,128)(2,1)} %get-tuple-element.18) | copy-start | bytes 393220
  60.7 113.5 %copy-start.12 = (bf16[16,16,256]{2,1,0:T(8,128)(2,1)S(1)}, bf16[16,16,256]{2,1,0:T(8,128)(2,1)}, u32[]{:S(2)}) copy-start(bf16[16,16,256]{2,1,0:T(8,128)(2,1)} %get-tuple-element.17) | copy-start | bytes 393220
  60.7 118.9 %copy-start.11 = (bf16[16,16,256]{2,1,0:T(8,128)(2,1)S(1)}, bf16[16,16,256]{2,1,0:T(8,128)(2,1)}, u32[]{:S(2)}) copy-start(bf16[16,16,256]{2,1,0:T(8,128)(2,1)} %get-tuple-element.16) | copy-start | bytes 393220
  60.7 129.2 %copy-start.10 = (bf16[16,16,256]{2,1,0:T(8,128)(2,1)S(1)}, bf16[16,16,256]{2,1,0:T(8,128)(2,1)}, u32[]{:S(2)}) copy-start(bf16[16,16,256]{2,1,0:T(8,128)(2,1)} %get-tuple-element.15) | copy-start | bytes 393220
  60.7 142.9 %copy-start.9 = (bf16[16,16,256]{2,1,0:T(8,128)(2,1)S(1)}, bf16[16,16,256]{2,1,0:T(8,128)(2,1)}, u32[]{:S(2)}) copy-start(bf16[16,16,256]{2,1,0:T(8,128)(2,1)} %get-tuple-element.14) | copy-start | bytes 393220
  74.0 139.5 %copy-start.8 = (bf16[16,16,256]{2,1,0:T(8,128)(2,1)S(1)}, bf16[16,16,256]{2,1,0:T(8,128)(2,1)}, u32[]{:S(2)}) copy-start(bf16[16,16,256]{2,1,0:T(8,128)(2,1)} %get-tuple-element.13) | copy-start | bytes 393220
  74.0 148.2 %copy-start.7 = (bf16[16,16,256]{2,1,0:T(8,128)(2,1)S(1)}, bf16[16,16,256]{2,1,0:T(8,128)(2,1)}, u32[]{:S(2)}) copy-start(bf16[16,16,256]{2,1,0:T(8,128)(2,1)} %get-tuple-element.12) | copy-start | bytes 393220
  74.0 6.7 %collective-permute-start.1 = (bf16[16,16,256]{2,1,0:T(8,128)(2,1)S(1)}, bf16[16,16,256]{2,1,0:T(8,128)(2,1)S(1)}, u32[]{:S(2)}, u32[]{:S(2)}) collective-permute-start(bf16[16,16,256]{2,1,0:T(8,128)(2,1)S(1)} %copy-done.16), channel_id=1, source_target_pairs={{0,2},{1,3},{2,0},{3,1},{4,6},{5,7},{6,4},{7,5},{8,10},{9,11},{10,... | collective-permute-start | bytes 393224 | tf_op jit(solution)/shard_map/ppermute | solution.py:443
  80.7 5.6 %collective-permute-start.2 = (bf16[16,16,256]{2,1,0:T(8,128)(2,1)S(1)}, bf16[16,16,256]{2,1,0:T(8,128)(2,1)S(1)}, u32[]{:S(2)}, u32[]{:S(2)}) collective-permute-start(bf16[16,16,256]{2,1,0:T(8,128)(2,1)S(1)} %copy-done.15), channel_id=1, source_target_pairs={{0,3},{1,2},{2,1},{3,0},{4,7},{5,6},{6,5},{7,4},{8,11},{9,10},{10,... | collective-permute-start | bytes 393224 | tf_op jit(solution)/shard_map/ppermute | solution.py:443
  86.3 71.7 %collective-permute-start.3 = (bf16[16,16,256]{2,1,0:T(8,128)(2,1)S(1)}, bf16[16,16,256]{2,1,0:T(8,128)(2,1)S(1)}, u32[]{:S(2)}, u32[]{:S(2)}) collective-permute-start(bf16[16,16,256]{2,1,0:T(8,128)(2,1)S(1)} %copy-done.14), channel_id=1, source_target_pairs={{0,4},{1,5},{2,6},{3,7},{4,0},{5,1},{6,2},{7,3},{8,12},{9,13},{10,... | collective-permute-start | bytes 393224 | tf_op jit(solution)/shard_map/ppermute | solution.py:443
  158.0 16.2 %collective-permute-start.4 = (bf16[16,16,256]{2,1,0:T(8,128)(2,1)S(1)}, bf16[16,16,256]{2,1,0:T(8,128)(2,1)S(1)}, u32[]{:S(2)}, u32[]{:S(2)}) collective-permute-start(bf16[16,16,256]{2,1,0:T(8,128)(2,1)S(1)} %copy-done.13), channel_id=1, source_target_pairs={{0,5},{1,4},{2,7},{3,6},{4,1},{5,0},{6,3},{7,2},{8,13},{9,12},{10,... | collective-permute-start | bytes 393224 | tf_op jit(solution)/shard_map/ppermute | solution.py:443
  174.2 5.5 %collective-permute-start.5 = (bf16[16,16,256]{2,1,0:T(8,128)(2,1)S(1)}, bf16[16,16,256]{2,1,0:T(8,128)(2,1)S(1)}, u32[]{:S(2)}, u32[]{:S(2)}) collective-permute-start(bf16[16,16,256]{2,1,0:T(8,128)(2,1)S(1)} %copy-done.12), channel_id=1, source_target_pairs={{0,6},{1,7},{2,4},{3,5},{4,2},{5,3},{6,0},{7,1},{8,14},{9,15},{10,... | collective-permute-start | bytes 393224 | tf_op jit(solution)/shard_map/ppermute | solution.py:443
  179.7 10.2 %collective-permute-start.6 = (bf16[16,16,256]{2,1,0:T(8,128)(2,1)S(1)}, bf16[16,16,256]{2,1,0:T(8,128)(2,1)S(1)}, u32[]{:S(2)}, u32[]{:S(2)}) collective-permute-start(bf16[16,16,256]{2,1,0:T(8,128)(2,1)S(1)} %copy-done.11), channel_id=1, source_target_pairs={{0,7},{1,6},{2,5},{3,4},{4,3},{5,2},{6,1},{7,0},{8,15},{9,14},{10,... | collective-permute-start | bytes 393224 | tf_op jit(solution)/shard_map/ppermute | solution.py:443
  189.9 13.7 %collective-permute-start.7 = (bf16[16,16,256]{2,1,0:T(8,128)(2,1)S(1)}, bf16[16,16,256]{2,1,0:T(8,128)(2,1)S(1)}, u32[]{:S(2)}, u32[]{:S(2)}) collective-permute-start(bf16[16,16,256]{2,1,0:T(8,128)(2,1)S(1)} %copy-done.10), channel_id=1, source_target_pairs={{0,8},{1,9},{2,10},{3,11},{4,12},{5,13},{6,14},{7,15},{8,0},{9,1},... | collective-permute-start | bytes 393224 | tf_op jit(solution)/shard_map/ppermute | solution.py:443
  203.7 9.8 %collective-permute-start.8 = (bf16[16,16,256]{2,1,0:T(8,128)(2,1)S(1)}, bf16[16,16,256]{2,1,0:T(8,128)(2,1)S(1)}, u32[]{:S(2)}, u32[]{:S(2)}) collective-permute-start(bf16[16,16,256]{2,1,0:T(8,128)(2,1)S(1)} %copy-done.9), channel_id=1, source_target_pairs={{0,9},{1,8},{2,11},{3,10},{4,13},{5,12},{6,15},{7,14},{8,1},{9,0},... | collective-permute-start | bytes 393224 | tf_op jit(solution)/shard_map/ppermute | solution.py:443
  213.5 8.7 %collective-permute-start.9 = (bf16[16,16,256]{2,1,0:T(8,128)(2,1)S(1)}, bf16[16,16,256]{2,1,0:T(8,128)(2,1)S(1)}, u32[]{:S(2)}, u32[]{:S(2)}) collective-permute-start(bf16[16,16,256]{2,1,0:T(8,128)(2,1)S(1)} %copy-done.8), channel_id=1, source_target_pairs={{0,10},{1,11},{2,8},{3,9},{4,14},{5,15},{6,12},{7,13},{8,2},{9,3},... | collective-permute-start | bytes 393224 | tf_op jit(solution)/shard_map/ppermute | solution.py:443
  222.2 8.6 %collective-permute-start.10 = (bf16[16,16,256]{2,1,0:T(8,128)(2,1)S(1)}, bf16[16,16,256]{2,1,0:T(8,128)(2,1)S(1)}, u32[]{:S(2)}, u32[]{:S(2)}) collective-permute-start(bf16[16,16,256]{2,1,0:T(8,128)(2,1)S(1)} %copy-done.7), channel_id=1, source_target_pairs={{0,11},{1,10},{2,9},{3,8},{4,15},{5,14},{6,13},{7,12},{8,3},{9,2},... | collective-permute-start | bytes 393224 | tf_op jit(solution)/shard_map/ppermute | solution.py:443
  235.0 1.3 copy-start.5
  248.1 9.1 %copy-start.17 = (s32[1024]{0:T(1024)S(1)}, s32[1024]{0:T(1024)}, u32[]{:S(2)}) copy-start(s32[1024]{0:T(1024)} %param.10) | copy-start | bytes 12292
  248.1 56.5 %all-to-all-start.1 = ((bf16[256,16,256]{2,1,0:T(8,128)(2,1)}), bf16[256,16,256]{2,1,0:T(8,128)(2,1)S(1)}, u32[]{:S(2)}, u32[]{:S(2)}) async-start(bf16[256,16,256]{2,1,0:T(8,128)(2,1)} %form_beams.1), calls=%async_computation.1 | async-start | bytes 4194304 | tf_op jit(solution)/shard_map/all_to_all | solution.py:430
  258.3 46.4 %copy-start.1 = (bf16[512,512]{1,0:T(8,128)(2,1)S(1)}, bf16[512,512]{1,0:T(8,128)(2,1)}, u32[]{:S(2)}) copy-start(bf16[512,512]{1,0:T(8,128)(2,1)} %constant.128.clone.table_ref) | copy-start | bytes 1572868
  258.3 46.4 %copy-start.2 = (f32[16,256]{1,0:T(8,128)S(1)}, f32[16,256]{1,0:T(8,128)}, u32[]{:S(2)}) copy-start(f32[16,256]{1,0:T(8,128)} %constant.127.clone.proto_ref) | copy-start | bytes 49156

commit v5 on v4

--- a/solution.py
+++ b/solution.py
@@ -47,15 +47,17 @@
     )
 
 
-def channelize_kernel(samples_ref, proto_ref, table_ref, out_ref, planes, filtered, turned):
-    chans, block, columns = out_ref.shape
+def channelize_kernel(me_ref, samples_ref, proto_ref, table_ref, *refs):
+    out_refs, (planes, filtered, turned) = refs[:-3], refs[-3:]
+    local, block, columns = out_refs[0].shape
+    chans = local * len(out_refs)
     spectra = columns // 2
     lane_tiles = chans // LANES
     in_frames = spectra + TAPS - 1
     group = filtered.shape[1] // spectra
     words = 2 * lane_tiles
     rows = in_frames * words
-    fold = turned.shape[2] // chans
+    fold = block
 
     def convolve(step):
         planes[...] = samples_ref[step * group * rows : (step + 1) * group * rows, :].astype(jnp.float32)
@@ -87,7 +89,7 @@
         for member in range(group):
             for part in range(2):
                 ant = group * step + member
-                turned[ant // fold, part, pl.ds(ant % fold, chans, stride=fold), :] = product[
+                turned[part, pl.ds(ant, chans, stride=fold), :] = product[
                     part * chans : (part + 1) * chans, member * spectra : (member + 1) * spectra
                 ]
 
@@ -97,21 +99,23 @@
         if step + 1 < steps:
             convolve(step + 1)
         transform(step)
-    for part in range(2):
-        pieces = [turned[i, part].reshape(chans, fold, spectra) for i in range(block // fold)]
-        out_ref[:, :, part * spectra : (part + 1) * spectra] = jnp.concatenate(
-            pieces, axis=1
-        ).astype(jnp.bfloat16)
-
-
-def channelize(samples, proto, table, first, count):
+    for mask, out_ref in enumerate(out_refs):
+        target = (me_ref[0] ^ mask) if len(out_refs) > 1 else 0
+        here = pl.ds(pl.multiple_of(target * local * fold, local * fold), local * fold)
+        for part in range(2):
+            out_ref[:, :, part * spectra : (part + 1) * spectra] = (
+                turned[part, here, :].reshape(local, fold, spectra).astype(jnp.bfloat16)
+            )
+
+
+def channelize(me, samples, proto, table, first, count, pieces):
     antennas, _, in_frames, chans = samples.shape
     spectra = in_frames - TAPS + 1
     lane_tiles = chans // LANES
     rows = in_frames * lane_tiles * 2
     block = FILTER_ANTENNAS if count % FILTER_ANTENNAS == 0 and first % FILTER_ANTENNAS == 0 else count
-    fold = block
     group = block
+    local = chans // pieces
     flat = (
         samples.reshape(antennas, 2, in_frames, lane_tiles, LANES)
         .transpose(0, 2, 3, 1, 4)
@@ -121,16 +125,17 @@
         channelize_kernel,
         grid=(count // block,),
         in_specs=[
+            pl.BlockSpec(memory_space=pltpu.SMEM),
             pl.BlockSpec((block * rows, LANES), lambda i: (i + first // block, 0)),
             pl.BlockSpec((TAPS, chans), lambda i: (0, 0)),
             pl.BlockSpec((2 * chans, 2 * chans), lambda i: (0, 0)),
         ],
-        out_specs=pl.BlockSpec((chans, block, 2 * spectra), lambda i: (0, i, 0)),
-        out_shape=jax.ShapeDtypeStruct((chans, count, 2 * spectra), jnp.bfloat16),
+        out_specs=[pl.BlockSpec((local, block, 2 * spectra), lambda i: (0, i, 0))] * pieces,
+        out_shape=[jax.ShapeDtypeStruct((local, count, 2 * spectra), jnp.bfloat16)] * pieces,
         scratch_shapes=[
             pltpu.VMEM((group * rows, LANES), jnp.float32),
             pltpu.VMEM((2, group * spectra, 2 * chans), jnp.bfloat16),
-            pltpu.VMEM((block // fold, 2, chans * fold, spectra), jnp.float32),
+            pltpu.VMEM((2, chans * block, spectra), jnp.float32),
         ],
         compiler_params=pltpu.CompilerParams(vmem_limit_bytes=VMEM_BYTES),
         cost_estimate=pl.CostEstimate(
@@ -139,7 +144,7 @@
             transcendentals=0,
         ),
         name="channelize",
-    )(flat, proto, table)
+    )(me.reshape(1), flat, proto, table)
 
 
 def weights_kernel(start_cos, start_sin, turn_cos, turn_sin, keep_ref, out_ref, cosine, sine):
@@ -430,30 +435,24 @@
     return lax.all_to_all(part, "chan", split_axis=0, concat_axis=0, tiled=True)
 
 
-def exchange_early(first, second):
+def exchange_early(pieces, second):
     devices = lax.axis_size("chan")
     me = lax.axis_index("chan")
-    chans = first.shape[0]
-
-    def send(source, mask):
-        split = source.reshape((devices, chans // devices) + source.shape[1:])
-        mine = lax.dynamic_index_in_dim(split, me ^ mask, 0, keepdims=False)
-        if mask == 0:
-            return mine
-        return lax.ppermute(mine, "chan", [(i, i ^ mask) for i in range(devices)])
-
-    far = [mask for mask in range(devices // 2, devices)]
-    near = [mask for mask in range(devices // 2)]
-    got = {mask: send(first, mask) for mask in far}
-    late, second = lax.optimization_barrier((first, second))
+
+    def send(piece, mask):
+        return lax.ppermute(piece, "chan", [(i, i ^ mask) for i in range(devices)])
+
+    half = devices // 2
+    far = [send(pieces[mask], mask) for mask in range(half, devices)]
+    late, second = lax.optimization_barrier((pieces[:half], second))
     rest = turn(second)
-    got.update({mask: send(late, mask) for mask in near})
-    stacked = jnp.stack([got[mask] for mask in range(devices)])
+    near = [late[0]] + [send(late[mask], mask) for mask in range(1, half)]
+    stacked = jnp.stack(near + far)
     ordered = [
         lax.dynamic_index_in_dim(stacked, me ^ source, 0, keepdims=False)
         for source in range(devices)
     ]
-    return jnp.concatenate(ordered, axis=0), rest
+    return [jnp.concatenate(ordered, axis=0), rest]
 
 
 def per_device(samples, flags, delays, order):
@@ -464,25 +463,27 @@
     antennas = antennas_here * devices
     beam_count = delays.shape[0]
     block = CHUNK_ANTENNAS if antennas_here > CHUNK_ANTENNAS else antennas_here
-    sizes = [block, antennas_here - block] if antennas_here > block else [block]
+    paired = devices & (devices - 1) == 0 and antennas_here > block
+    sizes = [block, antennas_here - block] if paired else [antennas_here]
 
     proto = jnp.asarray(prototype(TAPS, chans))
     table = jnp.asarray(transform_table(chans))
 
+    me = lax.axis_index("chan")
     parts = []
     columns_of = []
     start = 0
     for size in sizes:
-        parts.append(channelize(samples, proto, table, start, size))
+        pieces = devices if len(sizes) > 1 and start == 0 else 1
+        parts.append(channelize(me, samples, proto, table, start, size, pieces))
         ids = np.arange(antennas, dtype=np.int32).reshape(devices, antennas_here)
         columns_of.append(ids[:, start : start + size].reshape(-1))
         start += size
     ids = np.concatenate(columns_of)
     if len(parts) > 1:
-        early, rest = exchange_early(parts[0], parts[1])
-        parts = [early, rest]
+        parts = exchange_early(parts[0], parts[1][0])
     else:
-        parts = [turn(parts[0])]
+        parts = [turn(parts[0][0])]
     blocks = [
         x.reshape(devices, local_channels, size, 2 * spectra) for x, size in zip(parts, sizes)
     ]

time: 313 us -> 302 us (0.965)
  starting transfers between devices: 55.8 us -> 41.5 us
  waiting for transfers between devices: 125 us -> 138 us
  local copies, waits for them, and re-layouts: 12.5 us -> 4.2 us
    ppermute x15, waiting for transfers between devices: 120 us -> 133 us  [send(): return lax.ppermute(piece, 'chan', [(i, i ^ mask) for i in range(devices)])]
    ppermute x15, starting transfers between devices: 40.1 us -> 29.7 us  [send(): return lax.ppermute(piece, 'chan', [(i, i ^ mask) for i in range(devices)])]
    unnamed x68 -> x75, local copies, waits for them, and re-layouts: 6.94 us -> 2.37 us
    all_to_all x2, starting transfers between devices: 15.7 us -> 11.9 us  [turn(): return lax.all_to_all(part, 'chan', split_axis=0, concat_axis=0, tiled=True)]
  transfers between devices with their start and end apart: 17 -> 17, of which waited for: 11 -> 10; matrix products, arithmetic and copies ran while one was open for 6% -> 4% of each run, Pallas kernels for 18% -> 18%
where the time goes in v5:
time: 302 us; the launch traced here: 301 us
  waiting for transfers between devices  138 us (46%)
  Pallas kernels  108 us (36%)
  starting transfers between devices  41.5 us (14%)
  other arithmetic  8.37 us (3%)
  local copies, waits for them, and re-layouts  4.2 us (1%)
    ppermute x15, waiting for transfers between devices, send(): return lax.ppermute(piece, 'chan', [(i, i ^ mask) for i in range(devices)])  133 us
    pallas_call x1, Pallas kernels, correlate(): pl.pallas_call(functools.partial(visibility_kernel, counts), grid=(local,...  41.9 us
    pallas_call x2, Pallas kernels, channelize(): pl.pallas_call(channelize_kernel, grid=(count // block,), in_specs=[pl.Bl...  33.3 us
    ppermute x15, starting transfers between devices, send(): return lax.ppermute(piece, 'chan', [(i, i ^ mask) for i in range(devices)])  29.7 us
    pallas_call x1, Pallas kernels, make_weights(): pl.pallas_call(weights_kernel, in_specs=[vmem] * 5, out_specs=vmem, out_s...  13.2 us
    all_to_all x2, starting transfers between devices, turn(): return lax.all_to_all(part, 'chan', split_axis=0, concat_axis=0, tiled=True)  11.9 us
    pallas_call x1, Pallas kernels, form_beams(): pl.pallas_call(functools.partial(beam_kernel, counts), in_specs=[pl.Block...  11.8 us
    pallas_call x1, Pallas kernels, synthesize(): pl.pallas_call(synthesize_kernel, grid=(beams // group,), in_specs=[pl.Bl...  7.87 us
  transfers between devices with their start and end apart: 17, of which 10 were waited for; matrix products, arithmetic and copies ran while one was open for 4% of the time, Pallas kernels for 18%

profile of v5, /device:TPU:15, one launch (start us, length us, event | category | flops | bytes accessed | tf_op | source)
XLA Modules:
  0.0 301.3 jit_solution(287012110683780474)
XLA Ops:
  0.6 9.5 %channelize.2 = (bf16[16,16,256]{2,1,0:T(8,128)(2,1)}, bf16[16,16,256]{2,1,0:T(8,128)(2,1)}, bf16[16,16,256]{2,1,0:T(8,128)(2,1)}, bf16[16,16,256]{2,1,0:T(8,128...) custom-call(s32[1]{0:T(128)} %bitcast.1.me_ref, ...), custom_call_target="tpu_custom_call" | custom-call | flops 2147483648 | bytes 4440064 | tf_op jit(solution)/shard_map/channelize/pallas_call | solution.py:124
  10.1 23.8 %channelize.3 = bf16[256,48,256]{2,1,0:T(8,128)(2,1)} custom-call(s32[1]{0:T(128)} %bitcast.1.me_ref, bf16[36608,128]{1,0:T(8,128)(2,1)} %bitcast.85, f32[16,256]{1,0:T(8,128)} %constant.95.clone.proto_ref, bf16[512,512]{1,0:T(8,128)(2,1)} %constant.96.clone.table_ref), custom_call_target="tpu_custom_call" | custom-call | flops 6442450944 | bytes 13320192 | tf_op jit(solution)/shard_map/channelize/pallas_call | solution.py:124
  33.9 0.0 copy-start.21
  34.0 0.0 copy-start.3
  34.0 6.7 %all-to-all-start = ((bf16[256,48,256]{2,1,0:T(8,128)(2,1)}), bf16[256,48,256]{2,1,0:T(8,128)(2,1)}, u32[]{:S(2)}, u32[]{:S(2)}) async-start(bf16[256,48,256]{2,1,0:T(8,128)(2,1)} %channelize.3), calls=%async_computation | async-start | bytes 12582912 | tf_op jit(solution)/shard_map/all_to_all | solution.py:435
  40.6 2.2 collective-permute-start.7
  42.8 0.8 collective-permute-start.8
  43.6 2.1 collective-permute-start.9
  45.7 1.3 collective-permute-start.10
  47.0 0.3 collective-permute-start
  47.3 0.3 copy.13
  47.7 0.1 slice.19
  47.7 0.3 copy-done.6
  48.0 0.1 reshape.96
  48.1 0.1 slice.17
  48.1 0.1 concatenate.24
  48.2 0.1 concatenate.25
  48.3 0.3 copy.15
  48.6 0.1 copy.14
  48.8 0.6 broadcast_multiply_fusion
  49.4 7.8 %fusion.3 = (f32[256,1024]{1,0:T(8,128)S(1)}, f32[256,1024]{1,0:T(8,128)S(1)}, f32[256,1024]{1,0:T(8,128)S(1)}, f32[256,1024]{1,0:T(8,128)S(1)}) fusion(s32[256,768]{1,0:T(8,128)S(1)} %copy.15, s32[256,256]{1,0:T(8,128)S(1)} %copy.14, s32[]{:T(128)S(6)} %mul.21), kind=kLoop, calls=%fused_computation.8 | loop fusion | flops 4456448 | bytes 5242884 | tf_op jit(solution)/shard_map/sin | solution.py:193
  57.3 13.2 %make_weights.1.refs_2_ = bf16[16,512,1024]{2,1,0:T(8,128)(2,1)} custom-call(f32[256,1024]{1,0:T(8,128)S(1)} %get-tuple-element.57.start_cos, f32[256,1024]{1,0:T(8,128)S(1)} %get-tuple-element.55.start_sin, f32[256,1024]{1,0:T(8,128)S(1)} %get-tuple-element.56.turn_cos, f32[256,1024]{1,0:T(8,128)S(1)} %get-tuple-element.54.turn_sin, ...), custom_call_target="tpu_custom_call" | custom-call | flops 41943040 | bytes 20971520 | tf_op jit(solution)/shard_map/make_weights/pallas_call | solution.py:180
  70.5 0.3 collective-permute-start.1
  70.9 9.9 %collective-permute-done.1 = bf16[16,16,256]{2,1,0:T(8,128)(2,1)S(1)} collective-permute-done((bf16[16,16,256]{2,1,0:T(8,128)(2,1)S(1)}, bf16[16,16,256]{2,1,0:T(8,128)(2,1)S(1)}, u32[]{:S(2)}, u32[]{:S(2)}) %collective-permute-start.1) | collective-permute-done | bytes 131104 | tf_op jit(solution)/shard_map/ppermute | solution.py:443
  80.8 5.6 %collective-permute-done.2 = bf16[16,16,256]{2,1,0:T(8,128)(2,1)S(1)} collective-permute-done((bf16[16,16,256]{2,1,0:T(8,128)(2,1)S(1)}, bf16[16,16,256]{2,1,0:T(8,128)(2,1)S(1)}, u32[]{:S(2)}, u32[]{:S(2)}) %collective-permute-start.2) | collective-permute-done | bytes 131104 | tf_op jit(solution)/shard_map/ppermute | solution.py:443
  86.4 1.1 collective-permute-start.3
  87.6 70.6 %collective-permute-done.3 = bf16[16,16,256]{2,1,0:T(8,128)(2,1)S(1)} collective-permute-done((bf16[16,16,256]{2,1,0:T(8,128)(2,1)S(1)}, bf16[16,16,256]{2,1,0:T(8,128)(2,1)S(1)}, u32[]{:S(2)}, u32[]{:S(2)}) %collective-permute-start.3) | collective-permute-done | bytes 131104 | tf_op jit(solution)/shard_map/ppermute | solution.py:443
  158.2 0.1 collective-permute-start.4
  158.3 16.1 %collective-permute-done.4 = bf16[16,16,256]{2,1,0:T(8,128)(2,1)S(1)} collective-permute-done((bf16[16,16,256]{2,1,0:T(8,128)(2,1)S(1)}, bf16[16,16,256]{2,1,0:T(8,128)(2,1)S(1)}, u32[]{:S(2)}, u32[]{:S(2)}) %collective-permute-start.4) | collective-permute-done | bytes 131104 | tf_op jit(solution)/shard_map/ppermute | solution.py:443
  174.4 2.2 collective-permute-start.5
  176.6 3.2 %collective-permute-done.5 = bf16[16,16,256]{2,1,0:T(8,128)(2,1)S(1)} collective-permute-done((bf16[16,16,256]{2,1,0:T(8,128)(2,1)S(1)}, bf16[16,16,256]{2,1,0:T(8,128)(2,1)S(1)}, u32[]{:S(2)}, u32[]{:S(2)}) %collective-permute-start.5) | collective-permute-done | bytes 131104 | tf_op jit(solution)/shard_map/ppermute | solution.py:443
  179.8 3.5 %collective-permute-start.6 = (bf16[16,16,256]{2,1,0:T(8,128)(2,1)S(1)}, bf16[16,16,256]{2,1,0:T(8,128)(2,1)S(1)}, u32[]{:S(2)}, u32[]{:S(2)}) collective-permute-start(bf16[16,16,256]{2,1,0:T(8,128)(2,1)S(1)} %copy-done.15), channel_id=1, source_target_pairs={{0,7},{1,6},{2,5},{3,4},{4,3},{5,2},{6,1},{7,0},{8,15},{9,14},{10,... | collective-permute-start | bytes 393224 | tf_op jit(solution)/shard_map/ppermute | solution.py:443
  183.3 6.8 %collective-permute-done.6 = bf16[16,16,256]{2,1,0:T(8,128)(2,1)S(1)} collective-permute-done((bf16[16,16,256]{2,1,0:T(8,128)(2,1)S(1)}, bf16[16,16,256]{2,1,0:T(8,128)(2,1)S(1)}, u32[]{:S(2)}, u32[]{:S(2)}) %collective-permute-start.6) | collective-permute-done | bytes 131104 | tf_op jit(solution)/shard_map/ppermute | solution.py:443
  190.1 10.5 %collective-permute-start.11 = (bf16[16,16,256]{2,1,0:T(8,128)(2,1)S(1)}, bf16[16,16,256]{2,1,0:T(8,128)(2,1)S(1)}, u32[]{:S(2)}, u32[]{:S(2)}) collective-permute-start(bf16[16,16,256]{2,1,0:T(8,128)(2,1)S(1)} %copy-done.10), channel_id=1, source_target_pairs={{0,12},{1,13},{2,14},{3,15},{4,8},{5,9},{6,10},{7,11},{8,4},{9,5},... | collective-permute-start | bytes 393224 | tf_op jit(solution)/shard_map/ppermute | solution.py:443
  200.6 0.7 collective-permute-start.12
  201.4 4.5 %collective-permute-start.13 = (bf16[16,16,256]{2,1,0:T(8,128)(2,1)S(1)}, bf16[16,16,256]{2,1,0:T(8,128)(2,1)S(1)}, u32[]{:S(2)}, u32[]{:S(2)}) collective-permute-start(bf16[16,16,256]{2,1,0:T(8,128)(2,1)S(1)} %copy-done.8), channel_id=1, source_target_pairs={{0,14},{1,15},{2,12},{3,13},{4,10},{5,11},{6,8},{7,9},{8,6},{9,7},... | collective-permute-start | bytes 393224 | tf_op jit(solution)/shard_map/ppermute | solution.py:443
  205.9 0.1 collective-permute-start.14
  206.1 13.6 %collective-permute-done.12 = bf16[16,16,256]{2,1,0:T(8,128)(2,1)S(1)} collective-permute-done((bf16[16,16,256]{2,1,0:T(8,128)(2,1)S(1)}, bf16[16,16,256]{2,1,0:T(8,128)(2,1)S(1)}, u32[]{:S(2)}, u32[]{:S(2)}) %collective-permute-start.12) | collective-permute-done | bytes 131104 | tf_op jit(solution)/shard_map/ppermute | solution.py:443
  219.7 4.7 %collective-permute-done.13 = bf16[16,16,256]{2,1,0:T(8,128)(2,1)S(1)} collective-permute-done((bf16[16,16,256]{2,1,0:T(8,128)(2,1)S(1)}, bf16[16,16,256]{2,1,0:T(8,128)(2,1)S(1)}, u32[]{:S(2)}, u32[]{:S(2)}) %collective-permute-start.13) | collective-permute-done | bytes 131104 | tf_op jit(solution)/shard_map/ppermute | solution.py:443
  224.4 2.8 collective-permute-done.14
  227.7 1.3 copy-done.2
  228.9 11.8 %form_beams.1 = bf16[256,16,256]{2,1,0:T(8,128)(2,1)} custom-call(bf16[16,16,16,256]{3,2,1,0:T(8,128)(2,1)} %bitcast.89, bf16[16,16,48,256]{3,2,1,0:T(8,128)(2,1)} %bitcast.40.refs_1_, bf16[16,512,1024]{2,1,0:T(8,128)(2,1)} %make_weights.1.refs_2_), custom_call_target="tpu_custom_call" | custom-call | flops 4294967296 | bytes 27262976 | tf_op jit(solution)/shard_map/form_beams/pallas_call | solution.py:248
  240.8 0.0 copy-start.5
  240.8 5.2 %all-to-all-start.1 = ((bf16[256,16,256]{2,1,0:T(8,128)(2,1)}), bf16[256,16,256]{2,1,0:T(8,128)(2,1)S(1)}, u32[]{:S(2)}, u32[]{:S(2)}) async-start(bf16[256,16,256]{2,1,0:T(8,128)(2,1)} %form_beams.1), calls=%async_computation.1 | async-start | bytes 4194304 | tf_op jit(solution)/shard_map/all_to_all | solution.py:435
  246.0 1.0 copy.12.order_ref
  247.0 41.9 %correlate.1 = bf16[16,36,2,128,128]{4,3,2,1,0:T(8,128)(2,1)} custom-call(s32[1024,1]{1,0:T(8,128)} %copy.12.order_ref, s32[1,1024]{1,0:T(1,128)} %constant.98.ids_ref, f32[1,1024]{1,0:T(1,128)} %get-tuple-element.53.flags_ref, bf16[16,16,16,256]{3,2,1,0:T(8,128)(2,1)} %bitcast.90, bf16[16,16,48,256]{3,2,1,0:T(8,128)(2,1)} %bitcast.40.refs_1_), custom_call_target="tpu_custom_call" | custom-call | flops 18253611008 | bytes 46137344 | tf_op jit(solution)/shard_map/correlate/pallas_call | solution.py:327
  288.9 4.5 %all-to-all-done.1 = bf16[256,16,256]{2,1,0:T(8,128)(2,1)S(1)} async-done(((bf16[256,16,256]{2,1,0:T(8,128)(2,1)}), bf16[256,16,256]{2,1,0:T(8,128)(2,1)S(1)}, u32[]{:S(2)}, u32[]{:S(2)}) %all-to-all-start.1) | async-done | bytes 2097184 | tf_op jit(solution)/shard_map/all_to_all | solution.py:435
  293.4 7.9 %synthesize.1 = bf16[7232,128]{1,0:T(8,128)(2,1)} custom-call(bf16[16,16,16,256]{3,2,1,0:T(8,128)(2,1)S(1)} %bitcast.83, f32[16,256]{1,0:T(8,128)S(1)} %copy-done.1, bf16[512,512]{1,0:T(8,128)(2,1)S(1)} %copy-done), custom_call_target="tpu_custom_call" | custom-call | flops 1073741824 | bytes 3948544 | tf_op jit(solution)/shard_map/synthesize/pallas_call | solution.py:405
  (80 shorter events, 0.6 us)
Async XLA Ops:
  33.9 6.7 %copy-start.14 = (bf16[16,16,256]{2,1,0:T(8,128)(2,1)S(1)}, bf16[16,16,256]{2,1,0:T(8,128)(2,1)}, u32[]{:S(2)}) copy-start(bf16[16,16,256]{2,1,0:T(8,128)(2,1)} %get-tuple-element.43) | copy-start | bytes 393220
  33.9 8.9 %copy-start.13 = (bf16[16,16,256]{2,1,0:T(8,128)(2,1)S(1)}, bf16[16,16,256]{2,1,0:T(8,128)(2,1)}, u32[]{:S(2)}) copy-start(bf16[16,16,256]{2,1,0:T(8,128)(2,1)} %get-tuple-element.44) | copy-start | bytes 393220
  33.9 9.7 %copy-start.12 = (bf16[16,16,256]{2,1,0:T(8,128)(2,1)S(1)}, bf16[16,16,256]{2,1,0:T(8,128)(2,1)}, u32[]{:S(2)}) copy-start(bf16[16,16,256]{2,1,0:T(8,128)(2,1)} %get-tuple-element.45) | copy-start | bytes 393220
  33.9 11.8 %copy-start.11 = (bf16[16,16,256]{2,1,0:T(8,128)(2,1)S(1)}, bf16[16,16,256]{2,1,0:T(8,128)(2,1)}, u32[]{:S(2)}) copy-start(bf16[16,16,256]{2,1,0:T(8,128)(2,1)} %get-tuple-element.46) | copy-start | bytes 393220
  33.9 13.0 %copy-start.21 = (bf16[16,16,256]{2,1,0:T(8,128)(2,1)S(1)}, bf16[16,16,256]{2,1,0:T(8,128)(2,1)}, u32[]{:S(2)}) copy-start(bf16[16,16,256]{2,1,0:T(8,128)(2,1)} %get-tuple-element.36) | copy-start | bytes 393220
  34.0 13.3 %copy-start.3 = (s32[256,1024]{1,0:T(8,128)S(1)}, s32[256,1024]{1,0:T(8,128)}, u32[]{:S(2)}) copy-start(s32[256,1024]{1,0:T(8,128)} %param.9) | copy-start | bytes 3145732
  34.0 193.7 %all-to-all-start = ((bf16[256,48,256]{2,1,0:T(8,128)(2,1)}), bf16[256,48,256]{2,1,0:T(8,128)(2,1)}, u32[]{:S(2)}, u32[]{:S(2)}) async-start(bf16[256,48,256]{2,1,0:T(8,128)(2,1)} %channelize.3), calls=%async_computation | async-start | bytes 12582912 | tf_op jit(solution)/shard_map/all_to_all | solution.py:435
  40.6 160.0 %collective-permute-start.7 = (bf16[16,16,256]{2,1,0:T(8,128)(2,1)S(1)}, bf16[16,16,256]{2,1,0:T(8,128)(2,1)S(1)}, u32[]{:S(2)}, u32[]{:S(2)}) collective-permute-start(bf16[16,16,256]{2,1,0:T(8,128)(2,1)S(1)} %copy-done.14), channel_id=1, source_target_pairs={{0,8},{1,9},{2,10},{3,11},{4,12},{5,13},{6,14},{7,15},{8,0},{9,1},... | collective-permute-start | bytes 393224 | tf_op jit(solution)/shard_map/ppermute | solution.py:443
  42.8 158.6 %collective-permute-start.8 = (bf16[16,16,256]{2,1,0:T(8,128)(2,1)S(1)}, bf16[16,16,256]{2,1,0:T(8,128)(2,1)S(1)}, u32[]{:S(2)}, u32[]{:S(2)}) collective-permute-start(bf16[16,16,256]{2,1,0:T(8,128)(2,1)S(1)} %copy-done.13), channel_id=1, source_target_pairs={{0,9},{1,8},{2,11},{3,10},{4,13},{5,12},{6,15},{7,14},{8,1},{9,0},... | collective-permute-start | bytes 393224 | tf_op jit(solution)/shard_map/ppermute | solution.py:443
  43.6 162.2 %collective-permute-start.9 = (bf16[16,16,256]{2,1,0:T(8,128)(2,1)S(1)}, bf16[16,16,256]{2,1,0:T(8,128)(2,1)S(1)}, u32[]{:S(2)}, u32[]{:S(2)}) collective-permute-start(bf16[16,16,256]{2,1,0:T(8,128)(2,1)S(1)} %copy-done.12), channel_id=1, source_target_pairs={{0,10},{1,11},{2,8},{3,9},{4,14},{5,15},{6,12},{7,13},{8,2},{9,3},... | collective-permute-start | bytes 393224 | tf_op jit(solution)/shard_map/ppermute | solution.py:443
  45.7 160.3 %collective-permute-start.10 = (bf16[16,16,256]{2,1,0:T(8,128)(2,1)S(1)}, bf16[16,16,256]{2,1,0:T(8,128)(2,1)S(1)}, u32[]{:S(2)}, u32[]{:S(2)}) collective-permute-start(bf16[16,16,256]{2,1,0:T(8,128)(2,1)S(1)} %copy-done.11), channel_id=1, source_target_pairs={{0,11},{1,10},{2,9},{3,8},{4,15},{5,14},{6,13},{7,12},{8,3},{9,2},... | collective-permute-start | bytes 393224 | tf_op jit(solution)/shard_map/ppermute | solution.py:443
  47.0 23.5 %collective-permute-start = (bf16[16,16,256]{2,1,0:T(8,128)(2,1)S(1)}, bf16[16,16,256]{2,1,0:T(8,128)(2,1)S(1)}, u32[]{:S(2)}, u32[]{:S(2)}) collective-permute-start(bf16[16,16,256]{2,1,0:T(8,128)(2,1)S(1)} %copy-done.21), channel_id=1, source_target_pairs={{0,1},{1,0},{2,3},{3,2},{4,5},{5,4},{6,7},{7,6},{8,9},{9,8},{10,11... | collective-permute-start | bytes 393224 | tf_op jit(solution)/shard_map/ppermute | solution.py:443
  47.3 0.7 copy-start.6
  57.2 13.3 %copy-start.4 = (bf16[16,16,256]{2,1,0:T(8,128)(2,1)S(1)}, bf16[16,16,256]{2,1,0:T(8,128)(2,1)}, u32[]{:S(2)}) copy-start(bf16[16,16,256]{2,1,0:T(8,128)(2,1)} %get-tuple-element.35) | copy-start | bytes 393220
  57.2 13.3 %copy-start.20 = (bf16[16,16,256]{2,1,0:T(8,128)(2,1)S(1)}, bf16[16,16,256]{2,1,0:T(8,128)(2,1)}, u32[]{:S(2)}) copy-start(bf16[16,16,256]{2,1,0:T(8,128)(2,1)} %get-tuple-element.37) | copy-start | bytes 393220
  57.2 23.6 %copy-start.19 = (bf16[16,16,256]{2,1,0:T(8,128)(2,1)S(1)}, bf16[16,16,256]{2,1,0:T(8,128)(2,1)}, u32[]{:S(2)}) copy-start(bf16[16,16,256]{2,1,0:T(8,128)(2,1)} %get-tuple-element.38) | copy-start | bytes 393220
  57.2 29.2 %copy-start.18 = (bf16[16,16,256]{2,1,0:T(8,128)(2,1)S(1)}, bf16[16,16,256]{2,1,0:T(8,128)(2,1)}, u32[]{:S(2)}) copy-start(bf16[16,16,256]{2,1,0:T(8,128)(2,1)} %get-tuple-element.39) | copy-start | bytes 393220
  57.2 100.9 %copy-start.17 = (bf16[16,16,256]{2,1,0:T(8,128)(2,1)S(1)}, bf16[16,16,256]{2,1,0:T(8,128)(2,1)}, u32[]{:S(2)}) copy-start(bf16[16,16,256]{2,1,0:T(8,128)(2,1)} %get-tuple-element.40) | copy-start | bytes 393220
  57.2 117.1 %copy-start.16 = (bf16[16,16,256]{2,1,0:T(8,128)(2,1)S(1)}, bf16[16,16,256]{2,1,0:T(8,128)(2,1)}, u32[]{:S(2)}) copy-start(bf16[16,16,256]{2,1,0:T(8,128)(2,1)} %get-tuple-element.41) | copy-start | bytes 393220
  57.2 122.6 %copy-start.15 = (bf16[16,16,256]{2,1,0:T(8,128)(2,1)S(1)}, bf16[16,16,256]{2,1,0:T(8,128)(2,1)}, u32[]{:S(2)}) copy-start(bf16[16,16,256]{2,1,0:T(8,128)(2,1)} %get-tuple-element.42) | copy-start | bytes 393220
  57.2 132.8 %copy-start.10 = (bf16[16,16,256]{2,1,0:T(8,128)(2,1)S(1)}, bf16[16,16,256]{2,1,0:T(8,128)(2,1)}, u32[]{:S(2)}) copy-start(bf16[16,16,256]{2,1,0:T(8,128)(2,1)} %get-tuple-element.47) | copy-start | bytes 393220
  70.5 130.1 %copy-start.9 = (bf16[16,16,256]{2,1,0:T(8,128)(2,1)S(1)}, bf16[16,16,256]{2,1,0:T(8,128)(2,1)}, u32[]{:S(2)}) copy-start(bf16[16,16,256]{2,1,0:T(8,128)(2,1)} %get-tuple-element.48) | copy-start | bytes 393220
  70.5 130.9 %copy-start.8 = (bf16[16,16,256]{2,1,0:T(8,128)(2,1)S(1)}, bf16[16,16,256]{2,1,0:T(8,128)(2,1)}, u32[]{:S(2)}) copy-start(bf16[16,16,256]{2,1,0:T(8,128)(2,1)} %get-tuple-element.49) | copy-start | bytes 393220
  70.5 135.4 %copy-start.7 = (bf16[16,16,256]{2,1,0:T(8,128)(2,1)S(1)}, bf16[16,16,256]{2,1,0:T(8,128)(2,1)}, u32[]{:S(2)}) copy-start(bf16[16,16,256]{2,1,0:T(8,128)(2,1)} %get-tuple-element.50) | copy-start | bytes 393220
  70.5 10.3 %collective-permute-start.1 = (bf16[16,16,256]{2,1,0:T(8,128)(2,1)S(1)}, bf16[16,16,256]{2,1,0:T(8,128)(2,1)S(1)}, u32[]{:S(2)}, u32[]{:S(2)}) collective-permute-start(bf16[16,16,256]{2,1,0:T(8,128)(2,1)S(1)} %copy-done.20), channel_id=1, source_target_pairs={{0,2},{1,3},{2,0},{3,1},{4,6},{5,7},{6,4},{7,5},{8,10},{9,11},{10,... | collective-permute-start | bytes 393224 | tf_op jit(solution)/shard_map/ppermute | solution.py:443
  80.8 5.6 %collective-permute-start.2 = (bf16[16,16,256]{2,1,0:T(8,128)(2,1)S(1)}, bf16[16,16,256]{2,1,0:T(8,128)(2,1)S(1)}, u32[]{:S(2)}, u32[]{:S(2)}) collective-permute-start(bf16[16,16,256]{2,1,0:T(8,128)(2,1)S(1)} %copy-done.19), channel_id=1, source_target_pairs={{0,3},{1,2},{2,1},{3,0},{4,7},{5,6},{6,5},{7,4},{8,11},{9,10},{10,... | collective-permute-start | bytes 393224 | tf_op jit(solution)/shard_map/ppermute | solution.py:443
  86.4 71.7 %collective-permute-start.3 = (bf16[16,16,256]{2,1,0:T(8,128)(2,1)S(1)}, bf16[16,16,256]{2,1,0:T(8,128)(2,1)S(1)}, u32[]{:S(2)}, u32[]{:S(2)}) collective-permute-start(bf16[16,16,256]{2,1,0:T(8,128)(2,1)S(1)} %copy-done.18), channel_id=1, source_target_pairs={{0,4},{1,5},{2,6},{3,7},{4,0},{5,1},{6,2},{7,3},{8,12},{9,13},{10,... | collective-permute-start | bytes 393224 | tf_op jit(solution)/shard_map/ppermute | solution.py:443
  158.2 16.2 %collective-permute-start.4 = (bf16[16,16,256]{2,1,0:T(8,128)(2,1)S(1)}, bf16[16,16,256]{2,1,0:T(8,128)(2,1)S(1)}, u32[]{:S(2)}, u32[]{:S(2)}) collective-permute-start(bf16[16,16,256]{2,1,0:T(8,128)(2,1)S(1)} %copy-done.17), channel_id=1, source_target_pairs={{0,5},{1,4},{2,7},{3,6},{4,1},{5,0},{6,3},{7,2},{8,13},{9,12},{10,... | collective-permute-start | bytes 393224 | tf_op jit(solution)/shard_map/ppermute | solution.py:443
  174.4 5.5 %collective-permute-start.5 = (bf16[16,16,256]{2,1,0:T(8,128)(2,1)S(1)}, bf16[16,16,256]{2,1,0:T(8,128)(2,1)S(1)}, u32[]{:S(2)}, u32[]{:S(2)}) collective-permute-start(bf16[16,16,256]{2,1,0:T(8,128)(2,1)S(1)} %copy-done.16), channel_id=1, source_target_pairs={{0,6},{1,7},{2,4},{3,5},{4,2},{5,3},{6,0},{7,1},{8,14},{9,15},{10,... | collective-permute-start | bytes 393224 | tf_op jit(solution)/shard_map/ppermute | solution.py:443
  179.8 10.3 %collective-permute-start.6 = (bf16[16,16,256]{2,1,0:T(8,128)(2,1)S(1)}, bf16[16,16,256]{2,1,0:T(8,128)(2,1)S(1)}, u32[]{:S(2)}, u32[]{:S(2)}) collective-permute-start(bf16[16,16,256]{2,1,0:T(8,128)(2,1)S(1)} %copy-done.15), channel_id=1, source_target_pairs={{0,7},{1,6},{2,5},{3,4},{4,3},{5,2},{6,1},{7,0},{8,15},{9,14},{10,... | collective-permute-start | bytes 393224 | tf_op jit(solution)/shard_map/ppermute | solution.py:443
  190.1 15.9 %collective-permute-start.11 = (bf16[16,16,256]{2,1,0:T(8,128)(2,1)S(1)}, bf16[16,16,256]{2,1,0:T(8,128)(2,1)S(1)}, u32[]{:S(2)}, u32[]{:S(2)}) collective-permute-start(bf16[16,16,256]{2,1,0:T(8,128)(2,1)S(1)} %copy-done.10), channel_id=1, source_target_pairs={{0,12},{1,13},{2,14},{3,15},{4,8},{5,9},{6,10},{7,11},{8,4},{9,5},... | collective-permute-start | bytes 393224 | tf_op jit(solution)/shard_map/ppermute | solution.py:443
  200.6 19.1 %collective-permute-start.12 = (bf16[16,16,256]{2,1,0:T(8,128)(2,1)S(1)}, bf16[16,16,256]{2,1,0:T(8,128)(2,1)S(1)}, u32[]{:S(2)}, u32[]{:S(2)}) collective-permute-start(bf16[16,16,256]{2,1,0:T(8,128)(2,1)S(1)} %copy-done.9), channel_id=1, source_target_pairs={{0,13},{1,12},{2,15},{3,14},{4,9},{5,8},{6,11},{7,10},{8,5},{9,4},... | collective-permute-start | bytes 393224 | tf_op jit(solution)/shard_map/ppermute | solution.py:443
  201.4 23.0 %collective-permute-start.13 = (bf16[16,16,256]{2,1,0:T(8,128)(2,1)S(1)}, bf16[16,16,256]{2,1,0:T(8,128)(2,1)S(1)}, u32[]{:S(2)}, u32[]{:S(2)}) collective-permute-start(bf16[16,16,256]{2,1,0:T(8,128)(2,1)S(1)} %copy-done.8), channel_id=1, source_target_pairs={{0,14},{1,15},{2,12},{3,13},{4,10},{5,11},{6,8},{7,9},{8,6},{9,7},... | collective-permute-start | bytes 393224 | tf_op jit(solution)/shard_map/ppermute | solution.py:443
  205.9 21.3 %collective-permute-start.14 = (bf16[16,16,256]{2,1,0:T(8,128)(2,1)S(1)}, bf16[16,16,256]{2,1,0:T(8,128)(2,1)S(1)}, u32[]{:S(2)}, u32[]{:S(2)}) collective-permute-start(bf16[16,16,256]{2,1,0:T(8,128)(2,1)S(1)} %copy-done.7), channel_id=1, source_target_pairs={{0,15},{1,14},{2,13},{3,12},{4,11},{5,10},{6,9},{7,8},{8,7},{9,6},... | collective-permute-start | bytes 393224 | tf_op jit(solution)/shard_map/ppermute | solution.py:443
  227.6 1.3 copy-start.2
  240.8 5.2 %copy-start.5 = (s32[1024]{0:T(1024)S(1)}, s32[1024]{0:T(1024)}, u32[]{:S(2)}) copy-start(s32[1024]{0:T(1024)} %param.10) | copy-start | bytes 12292
  240.8 52.6 %all-to-all-start.1 = ((bf16[256,16,256]{2,1,0:T(8,128)(2,1)}), bf16[256,16,256]{2,1,0:T(8,128)(2,1)S(1)}, u32[]{:S(2)}, u32[]{:S(2)}) async-start(bf16[256,16,256]{2,1,0:T(8,128)(2,1)} %form_beams.1), calls=%async_computation.1 | async-start | bytes 4194304 | tf_op jit(solution)/shard_map/all_to_all | solution.py:435
  247.0 46.4 %copy-start = (bf16[512,512]{1,0:T(8,128)(2,1)S(1)}, bf16[512,512]{1,0:T(8,128)(2,1)}, u32[]{:S(2)}) copy-start(bf16[512,512]{1,0:T(8,128)(2,1)} %constant.96.clone.table_ref) | copy-start | bytes 1572868
  247.0 46.4 %copy-start.1 = (f32[16,256]{1,0:T(8,128)S(1)}, f32[16,256]{1,0:T(8,128)}, u32[]{:S(2)}) copy-start(f32[16,256]{1,0:T(8,128)} %constant.95.clone.proto_ref) | copy-start | bytes 49156

commit v6 on v5

--- a/solution.py
+++ b/solution.py
@@ -195,8 +195,8 @@
 
 def beam_kernel(counts, *refs):
     kinds = len(counts) + 1
-    sources, (out_ref, turned), holds, sems = (
-        refs[:kinds], refs[kinds : kinds + 2], refs[kinds + 2 : -1], refs[-1]
+    sources, (out_ref, turned, rounded), holds, (sems, out_sems) = (
+        refs[:kinds], refs[kinds : kinds + 3], refs[kinds + 3 : -2], refs[-2:]
     )
     beams, local, columns = out_ref.shape
     spectra = columns // 2
@@ -234,10 +234,23 @@
         return carry
 
     lax.fori_loop(0, local, form, 0)
-    for part in range(2):
-        out_ref[:, :, part * spectra : (part + 1) * spectra] = (
-            turned[part].reshape(beams, local, spectra).astype(jnp.bfloat16)
+    slices = rounded.shape[0]
+    count = beams // slices
+    writes = []
+    for i in range(slices):
+        for part in range(2):
+            rounded[i, :, :, part * spectra : (part + 1) * spectra] = (
+                turned[part, i * count * local : (i + 1) * count * local, :]
+                .reshape(count, local, spectra)
+                .astype(jnp.bfloat16)
+            )
+        write = pltpu.make_async_copy(
+            rounded.at[i], out_ref.at[i * count : (i + 1) * count], out_sems.at[i]
         )
+        write.start()
+        writes.append(write)
+    for write in writes:
+        write.wait()
 
 
 def form_beams(blocks, weights):
@@ -245,16 +258,21 @@
     beams = double_beams // 2
     columns = blocks[0].shape[3]
     counts = tuple(x.shape[0] * x.shape[2] for x in blocks)
+    slices = 4 if beams % 4 == 0 else 1
     return pl.pallas_call(
         functools.partial(beam_kernel, counts),
         in_specs=[pl.BlockSpec(memory_space=pl.ANY)] * (len(blocks) + 1),
-        out_specs=pl.BlockSpec(memory_space=pltpu.VMEM),
+        out_specs=pl.BlockSpec(memory_space=pl.ANY),
         out_shape=jax.ShapeDtypeStruct((beams, local, columns), jnp.bfloat16),
-        scratch_shapes=[pltpu.VMEM((2, beams * local, columns // 2), jnp.float32)]
+        scratch_shapes=[
+            pltpu.VMEM((2, beams * local, columns // 2), jnp.float32),
+            pltpu.VMEM((slices, beams // slices, local, columns), jnp.bfloat16),
+        ]
         + [pltpu.VMEM((local, x.shape[0], x.shape[2], columns), jnp.bfloat16) for x in blocks]
         + [
             pltpu.VMEM((local, double_beams, antennas), jnp.bfloat16),
             pltpu.SemaphoreType.DMA((len(blocks) + 1, local)),
+            pltpu.SemaphoreType.DMA((slices,)),
         ],
         compiler_params=pltpu.CompilerParams(vmem_limit_bytes=VMEM_BYTES),
         cost_estimate=pl.CostEstimate(
@@ -368,30 +386,24 @@
     first_beam = pl.program_id(0) * group
     for member in range(group):
         rows = beams_ref[:, first_beam + member].reshape(chans, columns)
+        left = jnp.concatenate([rows[:, :spectra].T, rows[:, spectra:].T], axis=1)
+        both = jnp.dot(left, table_ref[...], preferred_element_type=jnp.float32)
         for part in range(2):
-            cols = slice(part * chans, (part + 1) * chans)
-            value = None
-            for source in range(2):
-                term = lax.dot_general(
-                    rows[:, source * spectra : (source + 1) * spectra],
-                    table_ref[source * chans : (source + 1) * chans, cols],
-                    (((0,), (0,)), ((), ())),
-                    preferred_element_type=jnp.float32,
-                )
-                value = term if value is None else value + term
+            value = both[:, part * chans : (part + 1) * chans]
             value = value.astype(jnp.bfloat16).astype(jnp.float32)
             for tile in range(lane_tiles):
                 lanes = slice(tile * LANES, (tile + 1) * LANES)
-                zeta[...] = value[:, lanes]
-                total = proto_ref[TAPS - 1 : TAPS, lanes] * zeta[pl.ds(0, out_frames), :]
+                slot = (member * 2 + part) * lane_tiles + tile
+                zeta[slot, 0:spectra, :] = value[:, lanes]
+                total = proto_ref[TAPS - 1 : TAPS, lanes] * zeta[slot, pl.ds(0, out_frames), :]
                 for tap in range(1, TAPS):
                     total = total + (
                         proto_ref[TAPS - 1 - tap : TAPS - tap, lanes]
-                        * zeta[pl.ds(tap, out_frames), :]
+                        * zeta[slot, pl.ds(tap, out_frames), :]
                     )
                 first = member * out_frames * words + 2 * tile + part
                 planes[pl.ds(first, out_frames, stride=words), :] = total
-    out_ref[...] = planes[...].astype(jnp.bfloat16)
+    out_ref[...] = planes[0 : out_ref.shape[0], :].astype(jnp.bfloat16)
 
 
 def synthesize(arranged, proto, table):
@@ -413,8 +425,8 @@
         out_specs=pl.BlockSpec((group * rows, LANES), lambda b: (b, 0)),
         out_shape=jax.ShapeDtypeStruct((beams * rows, LANES), jnp.bfloat16),
         scratch_shapes=[
-            pltpu.VMEM((spectra, LANES), jnp.float32),
-            pltpu.VMEM((group * rows, LANES), jnp.float32),
+            pltpu.VMEM((group * 2 * lane_tiles, spectra + 8, LANES), jnp.float32),
+            pltpu.VMEM((group * rows + 16 * lane_tiles, LANES), jnp.float32),
         ],
         compiler_params=pltpu.CompilerParams(vmem_limit_bytes=32 * 1024 * 1024),
         cost_estimate=pl.CostEstimate(

time: 302 us -> 300 us (level)
  no operation moved by 1% of the time
where the time goes in v6:
time: 300 us
  waiting for transfers between devices  138 us (46%)
  Pallas kernels  107 us (36%)
  starting transfers between devices  41.5 us (14%)
  other arithmetic  8.37 us (3%)
  local copies, waits for them, and re-layouts  4.2 us (1%)
    ppermute x15, waiting for transfers between devices, send(): return lax.ppermute(piece, 'chan', [(i, i ^ mask) for i in range(devices)])  133 us
    pallas_call x1, Pallas kernels, correlate(): pl.pallas_call(functools.partial(visibility_kernel, counts), grid=(local,...  41.9 us
    pallas_call x2, Pallas kernels, channelize(): pl.pallas_call(channelize_kernel, grid=(count // block,), in_specs=[pl.Bl...  33.3 us
    ppermute x15, starting transfers between devices, send(): return lax.ppermute(piece, 'chan', [(i, i ^ mask) for i in range(devices)])  29.7 us
    pallas_call x1, Pallas kernels, make_weights(): pl.pallas_call(weights_kernel, in_specs=[vmem] * 5, out_specs=vmem, out_s...  13.2 us
    all_to_all x2, starting transfers between devices, turn(): return lax.all_to_all(part, 'chan', split_axis=0, concat_axis=0, tiled=True)  11.8 us
    pallas_call x1, Pallas kernels, form_beams(): pl.pallas_call(functools.partial(beam_kernel, counts), in_specs=[pl.Block...  11.7 us
    sin x1, other arithmetic, make_weights(): jnp.sin(turns)  7.79 us
  transfers between devices with their start and end apart: 17, of which 10 were waited for; matrix products, arithmetic and copies ran while one was open for 4% of the time, Pallas kernels for 18%

profile of v6, /device:TPU:15, one launch (start us, length us, event | category | flops | bytes accessed | tf_op | source)
XLA Modules:
  0.0 299.9 jit_solution(17922007038037986029)
XLA Ops:
  0.6 9.5 %channelize.2 = (bf16[16,16,256]{2,1,0:T(8,128)(2,1)}, bf16[16,16,256]{2,1,0:T(8,128)(2,1)}, bf16[16,16,256]{2,1,0:T(8,128)(2,1)}, bf16[16,16,256]{2,1,0:T(8,128...) custom-call(s32[1]{0:T(128)} %bitcast.1.me_ref, ...), custom_call_target="tpu_custom_call" | custom-call | flops 2147483648 | bytes 4440064 | tf_op jit(solution)/shard_map/channelize/pallas_call | solution.py:124
  10.1 23.8 %channelize.3 = bf16[256,48,256]{2,1,0:T(8,128)(2,1)} custom-call(s32[1]{0:T(128)} %bitcast.1.me_ref, bf16[36608,128]{1,0:T(8,128)(2,1)} %bitcast.85, f32[16,256]{1,0:T(8,128)} %constant.95.clone.proto_ref, bf16[512,512]{1,0:T(8,128)(2,1)} %constant.96.clone.table_ref), custom_call_target="tpu_custom_call" | custom-call | flops 6442450944 | bytes 13320192 | tf_op jit(solution)/shard_map/channelize/pallas_call | solution.py:124
  33.9 0.0 copy-start.21
  34.0 0.0 copy-start.3
  34.0 6.7 %all-to-all-start = ((bf16[256,48,256]{2,1,0:T(8,128)(2,1)}), bf16[256,48,256]{2,1,0:T(8,128)(2,1)}, u32[]{:S(2)}, u32[]{:S(2)}) async-start(bf16[256,48,256]{2,1,0:T(8,128)(2,1)} %channelize.3), calls=%async_computation | async-start | bytes 12582912 | tf_op jit(solution)/shard_map/all_to_all | solution.py:447
  40.6 2.2 collective-permute-start.7
  42.8 0.8 collective-permute-start.8
  43.6 2.1 collective-permute-start.9
  45.7 1.3 collective-permute-start.10
  47.0 0.3 collective-permute-start
  47.3 0.3 copy.13
  47.7 0.1 slice.19
  47.7 0.3 copy-done.6
  48.0 0.1 reshape.96
  48.1 0.1 slice.17
  48.1 0.1 concatenate.24
  48.2 0.1 concatenate.25
  48.3 0.3 copy.15
  48.6 0.1 copy.14
  48.8 0.6 broadcast_multiply_fusion
  49.4 7.8 %fusion.3 = (f32[256,1024]{1,0:T(8,128)S(1)}, f32[256,1024]{1,0:T(8,128)S(1)}, f32[256,1024]{1,0:T(8,128)S(1)}, f32[256,1024]{1,0:T(8,128)S(1)}) fusion(s32[256,768]{1,0:T(8,128)S(1)} %copy.15, s32[256,256]{1,0:T(8,128)S(1)} %copy.14, s32[]{:T(128)S(6)} %mul.21), kind=kLoop, calls=%fused_computation.8 | loop fusion | flops 4456448 | bytes 5242884 | tf_op jit(solution)/shard_map/sin | solution.py:193
  57.2 0.0 copy-start.4
  57.3 13.2 %make_weights.1.refs_2_ = bf16[16,512,1024]{2,1,0:T(8,128)(2,1)} custom-call(f32[256,1024]{1,0:T(8,128)S(1)} %get-tuple-element.57.start_cos, f32[256,1024]{1,0:T(8,128)S(1)} %get-tuple-element.55.start_sin, f32[256,1024]{1,0:T(8,128)S(1)} %get-tuple-element.56.turn_cos, f32[256,1024]{1,0:T(8,128)S(1)} %get-tuple-element.54.turn_sin, ...), custom_call_target="tpu_custom_call" | custom-call | flops 41943040 | bytes 20971520 | tf_op jit(solution)/shard_map/make_weights/pallas_call | solution.py:180
  70.5 0.3 collective-permute-start.1
  70.9 9.9 %collective-permute-done.1 = bf16[16,16,256]{2,1,0:T(8,128)(2,1)S(1)} collective-permute-done((bf16[16,16,256]{2,1,0:T(8,128)(2,1)S(1)}, bf16[16,16,256]{2,1,0:T(8,128)(2,1)S(1)}, u32[]{:S(2)}, u32[]{:S(2)}) %collective-permute-start.1) | collective-permute-done | bytes 131104 | tf_op jit(solution)/shard_map/ppermute | solution.py:455
  80.8 5.6 %collective-permute-done.2 = bf16[16,16,256]{2,1,0:T(8,128)(2,1)S(1)} collective-permute-done((bf16[16,16,256]{2,1,0:T(8,128)(2,1)S(1)}, bf16[16,16,256]{2,1,0:T(8,128)(2,1)S(1)}, u32[]{:S(2)}, u32[]{:S(2)}) %collective-permute-start.2) | collective-permute-done | bytes 131104 | tf_op jit(solution)/shard_map/ppermute | solution.py:455
  86.4 1.1 collective-permute-start.3
  87.6 70.6 %collective-permute-done.3 = bf16[16,16,256]{2,1,0:T(8,128)(2,1)S(1)} collective-permute-done((bf16[16,16,256]{2,1,0:T(8,128)(2,1)S(1)}, bf16[16,16,256]{2,1,0:T(8,128)(2,1)S(1)}, u32[]{:S(2)}, u32[]{:S(2)}) %collective-permute-start.3) | collective-permute-done | bytes 131104 | tf_op jit(solution)/shard_map/ppermute | solution.py:455
  158.2 0.1 collective-permute-start.4
  158.3 16.1 %collective-permute-done.4 = bf16[16,16,256]{2,1,0:T(8,128)(2,1)S(1)} collective-permute-done((bf16[16,16,256]{2,1,0:T(8,128)(2,1)S(1)}, bf16[16,16,256]{2,1,0:T(8,128)(2,1)S(1)}, u32[]{:S(2)}, u32[]{:S(2)}) %collective-permute-start.4) | collective-permute-done | bytes 131104 | tf_op jit(solution)/shard_map/ppermute | solution.py:455
  174.4 2.2 collective-permute-start.5
  176.6 3.2 %collective-permute-done.5 = bf16[16,16,256]{2,1,0:T(8,128)(2,1)S(1)} collective-permute-done((bf16[16,16,256]{2,1,0:T(8,128)(2,1)S(1)}, bf16[16,16,256]{2,1,0:T(8,128)(2,1)S(1)}, u32[]{:S(2)}, u32[]{:S(2)}) %collective-permute-start.5) | collective-permute-done | bytes 131104 | tf_op jit(solution)/shard_map/ppermute | solution.py:455
  179.8 3.5 %collective-permute-start.6 = (bf16[16,16,256]{2,1,0:T(8,128)(2,1)S(1)}, bf16[16,16,256]{2,1,0:T(8,128)(2,1)S(1)}, u32[]{:S(2)}, u32[]{:S(2)}) collective-permute-start(bf16[16,16,256]{2,1,0:T(8,128)(2,1)S(1)} %copy-done.15), channel_id=1, source_target_pairs={{0,7},{1,6},{2,5},{3,4},{4,3},{5,2},{6,1},{7,0},{8,15},{9,14},{10,... | collective-permute-start | bytes 393224 | tf_op jit(solution)/shard_map/ppermute | solution.py:455
  183.3 6.8 %collective-permute-done.6 = bf16[16,16,256]{2,1,0:T(8,128)(2,1)S(1)} collective-permute-done((bf16[16,16,256]{2,1,0:T(8,128)(2,1)S(1)}, bf16[16,16,256]{2,1,0:T(8,128)(2,1)S(1)}, u32[]{:S(2)}, u32[]{:S(2)}) %collective-permute-start.6) | collective-permute-done | bytes 131104 | tf_op jit(solution)/shard_map/ppermute | solution.py:455
  190.1 10.5 %collective-permute-start.11 = (bf16[16,16,256]{2,1,0:T(8,128)(2,1)S(1)}, bf16[16,16,256]{2,1,0:T(8,128)(2,1)S(1)}, u32[]{:S(2)}, u32[]{:S(2)}) collective-permute-start(bf16[16,16,256]{2,1,0:T(8,128)(2,1)S(1)} %copy-done.10), channel_id=1, source_target_pairs={{0,12},{1,13},{2,14},{3,15},{4,8},{5,9},{6,10},{7,11},{8,4},{9,5},... | collective-permute-start | bytes 393224 | tf_op jit(solution)/shard_map/ppermute | solution.py:455
  200.6 0.7 collective-permute-start.12
  201.4 4.5 %collective-permute-start.13 = (bf16[16,16,256]{2,1,0:T(8,128)(2,1)S(1)}, bf16[16,16,256]{2,1,0:T(8,128)(2,1)S(1)}, u32[]{:S(2)}, u32[]{:S(2)}) collective-permute-start(bf16[16,16,256]{2,1,0:T(8,128)(2,1)S(1)} %copy-done.8), channel_id=1, source_target_pairs={{0,14},{1,15},{2,12},{3,13},{4,10},{5,11},{6,8},{7,9},{8,6},{9,7},... | collective-permute-start | bytes 393224 | tf_op jit(solution)/shard_map/ppermute | solution.py:455
  205.9 0.1 collective-permute-start.14
  206.1 13.6 %collective-permute-done.12 = bf16[16,16,256]{2,1,0:T(8,128)(2,1)S(1)} collective-permute-done((bf16[16,16,256]{2,1,0:T(8,128)(2,1)S(1)}, bf16[16,16,256]{2,1,0:T(8,128)(2,1)S(1)}, u32[]{:S(2)}, u32[]{:S(2)}) %collective-permute-start.12) | collective-permute-done | bytes 131104 | tf_op jit(solution)/shard_map/ppermute | solution.py:455
  219.7 4.7 %collective-permute-done.13 = bf16[16,16,256]{2,1,0:T(8,128)(2,1)S(1)} collective-permute-done((bf16[16,16,256]{2,1,0:T(8,128)(2,1)S(1)}, bf16[16,16,256]{2,1,0:T(8,128)(2,1)S(1)}, u32[]{:S(2)}, u32[]{:S(2)}) %collective-permute-start.13) | collective-permute-done | bytes 131104 | tf_op jit(solution)/shard_map/ppermute | solution.py:455
  224.4 2.8 collective-permute-done.14
  227.7 1.3 copy-done.2
  228.9 11.7 %form_beams.1 = bf16[256,16,256]{2,1,0:T(8,128)(2,1)} custom-call(bf16[16,16,16,256]{3,2,1,0:T(8,128)(2,1)} %bitcast.89, bf16[16,16,48,256]{3,2,1,0:T(8,128)(2,1)} %bitcast.40.refs_1_, bf16[16,512,1024]{2,1,0:T(8,128)(2,1)} %make_weights.1.refs_2_), custom_call_target="tpu_custom_call" | custom-call | flops 4294967296 | bytes 27262976 | tf_op jit(solution)/shard_map/form_beams/pallas_call | solution.py:262
  240.7 5.1 %all-to-all-start.1 = ((bf16[256,16,256]{2,1,0:T(8,128)(2,1)}), bf16[256,16,256]{2,1,0:T(8,128)(2,1)S(1)}, u32[]{:S(2)}, u32[]{:S(2)}) async-start(bf16[256,16,256]{2,1,0:T(8,128)(2,1)} %form_beams.1), calls=%async_computation.1 | async-start | bytes 4194304 | tf_op jit(solution)/shard_map/all_to_all | solution.py:447
  245.8 1.0 copy.12.order_ref
  246.8 41.9 %correlate.1 = bf16[16,36,2,128,128]{4,3,2,1,0:T(8,128)(2,1)} custom-call(s32[1024,1]{1,0:T(8,128)} %copy.12.order_ref, s32[1,1024]{1,0:T(1,128)} %constant.98.ids_ref, f32[1,1024]{1,0:T(1,128)} %get-tuple-element.53.flags_ref, bf16[16,16,16,256]{3,2,1,0:T(8,128)(2,1)} %bitcast.90, bf16[16,16,48,256]{3,2,1,0:T(8,128)(2,1)} %bitcast.40.refs_1_), custom_call_target="tpu_custom_call" | custom-call | flops 18253611008 | bytes 46137344 | tf_op jit(solution)/shard_map/correlate/pallas_call | solution.py:345
  288.7 4.5 %all-to-all-done.1 = bf16[256,16,256]{2,1,0:T(8,128)(2,1)S(1)} async-done(((bf16[256,16,256]{2,1,0:T(8,128)(2,1)}), bf16[256,16,256]{2,1,0:T(8,128)(2,1)S(1)}, u32[]{:S(2)}, u32[]{:S(2)}) %all-to-all-start.1) | async-done | bytes 2097184 | tf_op jit(solution)/shard_map/all_to_all | solution.py:447
  293.2 6.7 %synthesize.1 = bf16[7232,128]{1,0:T(8,128)(2,1)} custom-call(bf16[16,16,16,256]{3,2,1,0:T(8,128)(2,1)S(1)} %bitcast.83, f32[16,256]{1,0:T(8,128)S(1)} %copy-done.1, bf16[512,512]{1,0:T(8,128)(2,1)S(1)} %copy-done), custom_call_target="tpu_custom_call" | custom-call | flops 1073741824 | bytes 3948544 | tf_op jit(solution)/shard_map/synthesize/pallas_call | solution.py:417
  (80 shorter events, 0.6 us)
Async XLA Ops:
  33.9 6.7 %copy-start.14 = (bf16[16,16,256]{2,1,0:T(8,128)(2,1)S(1)}, bf16[16,16,256]{2,1,0:T(8,128)(2,1)}, u32[]{:S(2)}) copy-start(bf16[16,16,256]{2,1,0:T(8,128)(2,1)} %get-tuple-element.43) | copy-start | bytes 393220
  33.9 8.9 %copy-start.13 = (bf16[16,16,256]{2,1,0:T(8,128)(2,1)S(1)}, bf16[16,16,256]{2,1,0:T(8,128)(2,1)}, u32[]{:S(2)}) copy-start(bf16[16,16,256]{2,1,0:T(8,128)(2,1)} %get-tuple-element.44) | copy-start | bytes 393220
  33.9 9.7 %copy-start.12 = (bf16[16,16,256]{2,1,0:T(8,128)(2,1)S(1)}, bf16[16,16,256]{2,1,0:T(8,128)(2,1)}, u32[]{:S(2)}) copy-start(bf16[16,16,256]{2,1,0:T(8,128)(2,1)} %get-tuple-element.45) | copy-start | bytes 393220
  33.9 11.8 %copy-start.11 = (bf16[16,16,256]{2,1,0:T(8,128)(2,1)S(1)}, bf16[16,16,256]{2,1,0:T(8,128)(2,1)}, u32[]{:S(2)}) copy-start(bf16[16,16,256]{2,1,0:T(8,128)(2,1)} %get-tuple-element.46) | copy-start | bytes 393220
  33.9 13.0 %copy-start.21 = (bf16[16,16,256]{2,1,0:T(8,128)(2,1)S(1)}, bf16[16,16,256]{2,1,0:T(8,128)(2,1)}, u32[]{:S(2)}) copy-start(bf16[16,16,256]{2,1,0:T(8,128)(2,1)} %get-tuple-element.36) | copy-start | bytes 393220
  34.0 13.3 %copy-start.3 = (s32[256,1024]{1,0:T(8,128)S(1)}, s32[256,1024]{1,0:T(8,128)}, u32[]{:S(2)}) copy-start(s32[256,1024]{1,0:T(8,128)} %param.9) | copy-start | bytes 3145732
  34.0 193.7 %all-to-all-start = ((bf16[256,48,256]{2,1,0:T(8,128)(2,1)}), bf16[256,48,256]{2,1,0:T(8,128)(2,1)}, u32[]{:S(2)}, u32[]{:S(2)}) async-start(bf16[256,48,256]{2,1,0:T(8,128)(2,1)} %channelize.3), calls=%async_computation | async-start | bytes 12582912 | tf_op jit(solution)/shard_map/all_to_all | solution.py:447
  40.6 160.0 %collective-permute-start.7 = (bf16[16,16,256]{2,1,0:T(8,128)(2,1)S(1)}, bf16[16,16,256]{2,1,0:T(8,128)(2,1)S(1)}, u32[]{:S(2)}, u32[]{:S(2)}) collective-permute-start(bf16[16,16,256]{2,1,0:T(8,128)(2,1)S(1)} %copy-done.14), channel_id=1, source_target_pairs={{0,8},{1,9},{2,10},{3,11},{4,12},{5,13},{6,14},{7,15},{8,0},{9,1},... | collective-permute-start | bytes 393224 | tf_op jit(solution)/shard_map/ppermute | solution.py:455
  42.8 158.6 %collective-permute-start.8 = (bf16[16,16,256]{2,1,0:T(8,128)(2,1)S(1)}, bf16[16,16,256]{2,1,0:T(8,128)(2,1)S(1)}, u32[]{:S(2)}, u32[]{:S(2)}) collective-permute-start(bf16[16,16,256]{2,1,0:T(8,128)(2,1)S(1)} %copy-done.13), channel_id=1, source_target_pairs={{0,9},{1,8},{2,11},{3,10},{4,13},{5,12},{6,15},{7,14},{8,1},{9,0},... | collective-permute-start | bytes 393224 | tf_op jit(solution)/shard_map/ppermute | solution.py:455
  43.6 162.2 %collective-permute-start.9 = (bf16[16,16,256]{2,1,0:T(8,128)(2,1)S(1)}, bf16[16,16,256]{2,1,0:T(8,128)(2,1)S(1)}, u32[]{:S(2)}, u32[]{:S(2)}) collective-permute-start(bf16[16,16,256]{2,1,0:T(8,128)(2,1)S(1)} %copy-done.12), channel_id=1, source_target_pairs={{0,10},{1,11},{2,8},{3,9},{4,14},{5,15},{6,12},{7,13},{8,2},{9,3},... | collective-permute-start | bytes 393224 | tf_op jit(solution)/shard_map/ppermute | solution.py:455
  45.7 160.3 %collective-permute-start.10 = (bf16[16,16,256]{2,1,0:T(8,128)(2,1)S(1)}, bf16[16,16,256]{2,1,0:T(8,128)(2,1)S(1)}, u32[]{:S(2)}, u32[]{:S(2)}) collective-permute-start(bf16[16,16,256]{2,1,0:T(8,128)(2,1)S(1)} %copy-done.11), channel_id=1, source_target_pairs={{0,11},{1,10},{2,9},{3,8},{4,15},{5,14},{6,13},{7,12},{8,3},{9,2},... | collective-permute-start | bytes 393224 | tf_op jit(solution)/shard_map/ppermute | solution.py:455
  47.0 23.5 %collective-permute-start = (bf16[16,16,256]{2,1,0:T(8,128)(2,1)S(1)}, bf16[16,16,256]{2,1,0:T(8,128)(2,1)S(1)}, u32[]{:S(2)}, u32[]{:S(2)}) collective-permute-start(bf16[16,16,256]{2,1,0:T(8,128)(2,1)S(1)} %copy-done.21), channel_id=1, source_target_pairs={{0,1},{1,0},{2,3},{3,2},{4,5},{5,4},{6,7},{7,6},{8,9},{9,8},{10,11... | collective-permute-start | bytes 393224 | tf_op jit(solution)/shard_map/ppermute | solution.py:455
  47.3 0.7 copy-start.6
  57.2 13.3 %copy-start.4 = (bf16[16,16,256]{2,1,0:T(8,128)(2,1)S(1)}, bf16[16,16,256]{2,1,0:T(8,128)(2,1)}, u32[]{:S(2)}) copy-start(bf16[16,16,256]{2,1,0:T(8,128)(2,1)} %get-tuple-element.35) | copy-start | bytes 393220
  57.2 13.3 %copy-start.20 = (bf16[16,16,256]{2,1,0:T(8,128)(2,1)S(1)}, bf16[16,16,256]{2,1,0:T(8,128)(2,1)}, u32[]{:S(2)}) copy-start(bf16[16,16,256]{2,1,0:T(8,128)(2,1)} %get-tuple-element.37) | copy-start | bytes 393220
  57.2 23.6 %copy-start.19 = (bf16[16,16,256]{2,1,0:T(8,128)(2,1)S(1)}, bf16[16,16,256]{2,1,0:T(8,128)(2,1)}, u32[]{:S(2)}) copy-start(bf16[16,16,256]{2,1,0:T(8,128)(2,1)} %get-tuple-element.38) | copy-start | bytes 393220
  57.2 29.2 %copy-start.18 = (bf16[16,16,256]{2,1,0:T(8,128)(2,1)S(1)}, bf16[16,16,256]{2,1,0:T(8,128)(2,1)}, u32[]{:S(2)}) copy-start(bf16[16,16,256]{2,1,0:T(8,128)(2,1)} %get-tuple-element.39) | copy-start | bytes 393220
  57.2 100.9 %copy-start.17 = (bf16[16,16,256]{2,1,0:T(8,128)(2,1)S(1)}, bf16[16,16,256]{2,1,0:T(8,128)(2,1)}, u32[]{:S(2)}) copy-start(bf16[16,16,256]{2,1,0:T(8,128)(2,1)} %get-tuple-element.40) | copy-start | bytes 393220
  57.2 117.1 %copy-start.16 = (bf16[16,16,256]{2,1,0:T(8,128)(2,1)S(1)}, bf16[16,16,256]{2,1,0:T(8,128)(2,1)}, u32[]{:S(2)}) copy-start(bf16[16,16,256]{2,1,0:T(8,128)(2,1)} %get-tuple-element.41) | copy-start | bytes 393220
  57.2 122.6 %copy-start.15 = (bf16[16,16,256]{2,1,0:T(8,128)(2,1)S(1)}, bf16[16,16,256]{2,1,0:T(8,128)(2,1)}, u32[]{:S(2)}) copy-start(bf16[16,16,256]{2,1,0:T(8,128)(2,1)} %get-tuple-element.42) | copy-start | bytes 393220
  57.2 132.8 %copy-start.10 = (bf16[16,16,256]{2,1,0:T(8,128)(2,1)S(1)}, bf16[16,16,256]{2,1,0:T(8,128)(2,1)}, u32[]{:S(2)}) copy-start(bf16[16,16,256]{2,1,0:T(8,128)(2,1)} %get-tuple-element.47) | copy-start | bytes 393220
  70.5 130.1 %copy-start.9 = (bf16[16,16,256]{2,1,0:T(8,128)(2,1)S(1)}, bf16[16,16,256]{2,1,0:T(8,128)(2,1)}, u32[]{:S(2)}) copy-start(bf16[16,16,256]{2,1,0:T(8,128)(2,1)} %get-tuple-element.48) | copy-start | bytes 393220
  70.5 130.9 %copy-start.8 = (bf16[16,16,256]{2,1,0:T(8,128)(2,1)S(1)}, bf16[16,16,256]{2,1,0:T(8,128)(2,1)}, u32[]{:S(2)}) copy-start(bf16[16,16,256]{2,1,0:T(8,128)(2,1)} %get-tuple-element.49) | copy-start | bytes 393220
  70.5 135.4 %copy-start.7 = (bf16[16,16,256]{2,1,0:T(8,128)(2,1)S(1)}, bf16[16,16,256]{2,1,0:T(8,128)(2,1)}, u32[]{:S(2)}) copy-start(bf16[16,16,256]{2,1,0:T(8,128)(2,1)} %get-tuple-element.50) | copy-start | bytes 393220
  70.5 10.3 %collective-permute-start.1 = (bf16[16,16,256]{2,1,0:T(8,128)(2,1)S(1)}, bf16[16,16,256]{2,1,0:T(8,128)(2,1)S(1)}, u32[]{:S(2)}, u32[]{:S(2)}) collective-permute-start(bf16[16,16,256]{2,1,0:T(8,128)(2,1)S(1)} %copy-done.20), channel_id=1, source_target_pairs={{0,2},{1,3},{2,0},{3,1},{4,6},{5,7},{6,4},{7,5},{8,10},{9,11},{10,... | collective-permute-start | bytes 393224 | tf_op jit(solution)/shard_map/ppermute | solution.py:455
  80.8 5.6 %collective-permute-start.2 = (bf16[16,16,256]{2,1,0:T(8,128)(2,1)S(1)}, bf16[16,16,256]{2,1,0:T(8,128)(2,1)S(1)}, u32[]{:S(2)}, u32[]{:S(2)}) collective-permute-start(bf16[16,16,256]{2,1,0:T(8,128)(2,1)S(1)} %copy-done.19), channel_id=1, source_target_pairs={{0,3},{1,2},{2,1},{3,0},{4,7},{5,6},{6,5},{7,4},{8,11},{9,10},{10,... | collective-permute-start | bytes 393224 | tf_op jit(solution)/shard_map/ppermute | solution.py:455
  86.4 71.7 %collective-permute-start.3 = (bf16[16,16,256]{2,1,0:T(8,128)(2,1)S(1)}, bf16[16,16,256]{2,1,0:T(8,128)(2,1)S(1)}, u32[]{:S(2)}, u32[]{:S(2)}) collective-permute-start(bf16[16,16,256]{2,1,0:T(8,128)(2,1)S(1)} %copy-done.18), channel_id=1, source_target_pairs={{0,4},{1,5},{2,6},{3,7},{4,0},{5,1},{6,2},{7,3},{8,12},{9,13},{10,... | collective-permute-start | bytes 393224 | tf_op jit(solution)/shard_map/ppermute | solution.py:455
  158.2 16.2 %collective-permute-start.4 = (bf16[16,16,256]{2,1,0:T(8,128)(2,1)S(1)}, bf16[16,16,256]{2,1,0:T(8,128)(2,1)S(1)}, u32[]{:S(2)}, u32[]{:S(2)}) collective-permute-start(bf16[16,16,256]{2,1,0:T(8,128)(2,1)S(1)} %copy-done.17), channel_id=1, source_target_pairs={{0,5},{1,4},{2,7},{3,6},{4,1},{5,0},{6,3},{7,2},{8,13},{9,12},{10,... | collective-permute-start | bytes 393224 | tf_op jit(solution)/shard_map/ppermute | solution.py:455
  174.4 5.5 %collective-permute-start.5 = (bf16[16,16,256]{2,1,0:T(8,128)(2,1)S(1)}, bf16[16,16,256]{2,1,0:T(8,128)(2,1)S(1)}, u32[]{:S(2)}, u32[]{:S(2)}) collective-permute-start(bf16[16,16,256]{2,1,0:T(8,128)(2,1)S(1)} %copy-done.16), channel_id=1, source_target_pairs={{0,6},{1,7},{2,4},{3,5},{4,2},{5,3},{6,0},{7,1},{8,14},{9,15},{10,... | collective-permute-start | bytes 393224 | tf_op jit(solution)/shard_map/ppermute | solution.py:455
  179.8 10.3 %collective-permute-start.6 = (bf16[16,16,256]{2,1,0:T(8,128)(2,1)S(1)}, bf16[16,16,256]{2,1,0:T(8,128)(2,1)S(1)}, u32[]{:S(2)}, u32[]{:S(2)}) collective-permute-start(bf16[16,16,256]{2,1,0:T(8,128)(2,1)S(1)} %copy-done.15), channel_id=1, source_target_pairs={{0,7},{1,6},{2,5},{3,4},{4,3},{5,2},{6,1},{7,0},{8,15},{9,14},{10,... | collective-permute-start | bytes 393224 | tf_op jit(solution)/shard_map/ppermute | solution.py:455
  190.1 15.9 %collective-permute-start.11 = (bf16[16,16,256]{2,1,0:T(8,128)(2,1)S(1)}, bf16[16,16,256]{2,1,0:T(8,128)(2,1)S(1)}, u32[]{:S(2)}, u32[]{:S(2)}) collective-permute-start(bf16[16,16,256]{2,1,0:T(8,128)(2,1)S(1)} %copy-done.10), channel_id=1, source_target_pairs={{0,12},{1,13},{2,14},{3,15},{4,8},{5,9},{6,10},{7,11},{8,4},{9,5},... | collective-permute-start | bytes 393224 | tf_op jit(solution)/shard_map/ppermute | solution.py:455
  200.6 19.1 %collective-permute-start.12 = (bf16[16,16,256]{2,1,0:T(8,128)(2,1)S(1)}, bf16[16,16,256]{2,1,0:T(8,128)(2,1)S(1)}, u32[]{:S(2)}, u32[]{:S(2)}) collective-permute-start(bf16[16,16,256]{2,1,0:T(8,128)(2,1)S(1)} %copy-done.9), channel_id=1, source_target_pairs={{0,13},{1,12},{2,15},{3,14},{4,9},{5,8},{6,11},{7,10},{8,5},{9,4},... | collective-permute-start | bytes 393224 | tf_op jit(solution)/shard_map/ppermute | solution.py:455
  201.4 23.0 %collective-permute-start.13 = (bf16[16,16,256]{2,1,0:T(8,128)(2,1)S(1)}, bf16[16,16,256]{2,1,0:T(8,128)(2,1)S(1)}, u32[]{:S(2)}, u32[]{:S(2)}) collective-permute-start(bf16[16,16,256]{2,1,0:T(8,128)(2,1)S(1)} %copy-done.8), channel_id=1, source_target_pairs={{0,14},{1,15},{2,12},{3,13},{4,10},{5,11},{6,8},{7,9},{8,6},{9,7},... | collective-permute-start | bytes 393224 | tf_op jit(solution)/shard_map/ppermute | solution.py:455
  205.9 21.3 %collective-permute-start.14 = (bf16[16,16,256]{2,1,0:T(8,128)(2,1)S(1)}, bf16[16,16,256]{2,1,0:T(8,128)(2,1)S(1)}, u32[]{:S(2)}, u32[]{:S(2)}) collective-permute-start(bf16[16,16,256]{2,1,0:T(8,128)(2,1)S(1)} %copy-done.7), channel_id=1, source_target_pairs={{0,15},{1,14},{2,13},{3,12},{4,11},{5,10},{6,9},{7,8},{8,7},{9,6},... | collective-permute-start | bytes 393224 | tf_op jit(solution)/shard_map/ppermute | solution.py:455
  227.6 1.3 copy-start.2
  240.6 5.2 %copy-start.5 = (s32[1024]{0:T(1024)S(1)}, s32[1024]{0:T(1024)}, u32[]{:S(2)}) copy-start(s32[1024]{0:T(1024)} %param.10) | copy-start | bytes 12292
  240.7 52.6 %all-to-all-start.1 = ((bf16[256,16,256]{2,1,0:T(8,128)(2,1)}), bf16[256,16,256]{2,1,0:T(8,128)(2,1)S(1)}, u32[]{:S(2)}, u32[]{:S(2)}) async-start(bf16[256,16,256]{2,1,0:T(8,128)(2,1)} %form_beams.1), calls=%async_computation.1 | async-start | bytes 4194304 | tf_op jit(solution)/shard_map/all_to_all | solution.py:447
  246.8 46.4 %copy-start = (bf16[512,512]{1,0:T(8,128)(2,1)S(1)}, bf16[512,512]{1,0:T(8,128)(2,1)}, u32[]{:S(2)}) copy-start(bf16[512,512]{1,0:T(8,128)(2,1)} %constant.96.clone.table_ref) | copy-start | bytes 1572868
  246.8 46.4 %copy-start.1 = (f32[16,256]{1,0:T(8,128)S(1)}, f32[16,256]{1,0:T(8,128)}, u32[]{:S(2)}) copy-start(f32[16,256]{1,0:T(8,128)} %constant.95.clone.proto_ref) | copy-start | bytes 49156
